TPU v7x, 256 devices: a whole 4x4x8 slice. The times are simulated.
256 devices in a mesh: space: 32 (over x, y, core), tm: 8 (over z).
Axes of the slice: x: 4, y: 4, z: 8, core: 2. Of those that a mesh axis runs over, the one named last changes fastest.
Arguments:
- velocity: bfloat16 [256, 2, 512, 1024], P('tm', None, 'space'), may hold values from -8.4 to 8.4
Outputs:
- vorticity: bfloat16 [256, 512, 1024], P('tm', 'space')
- modes: float32 [32, 512, 1024], P('tm', 'space')
All inputs are finite; a program needn't handle non-finite values.
Results may differ from a plain program's by a relative error of at most 0.003.
Values may be sent and summed in bfloat16 or wider, within the bound.
A program may use at most 64 MiB of HBM per device.

v0:
```python
import jax
import jax.numpy as jnp
from jax import lax
from jax.sharding import PartitionSpec as P

RANK = 32


def extended(block, sides, width):
    for axis, dim in sides:
        count = lax.axis_size(axis)
        forward = [(i, i + 1) for i in range(count - 1)]
        forward.append((count - 1, 0))
        backward = [(target, source) for source, target in forward]
        low = lax.ppermute(
            lax.slice_in_dim(block, block.shape[dim] - width, None, axis=dim), axis, forward
        )
        high = lax.ppermute(lax.slice_in_dim(block, 0, width, axis=dim), axis, backward)
        block = jnp.concatenate([low, block, high], axis=dim)
    return block


def partner_2(value, axis, apart):
    mask = 2**apart
    pairs = [(source, source ^ mask) for source in range(lax.axis_size(axis))]
    return lax.ppermute(value, axis, pairs)


def merge_nodes(stacked):
    high = lax.Precision.HIGHEST
    gram = lax.psum(jnp.einsum("naxz,nbxz->nab", stacked, stacked, precision=high), "space")
    coeffs = gram[:, :, :RANK] + gram[:, :, RANK:]
    diagonal = jnp.diagonal(gram, axis1=1, axis2=2)
    scales = jnp.sqrt(diagonal[:, :RANK] + diagonal[:, RANK:])
    eye = jnp.broadcast_to(jnp.eye(RANK, dtype=jnp.float32), (stacked.shape[0], RANK, RANK))
    mixed = jnp.einsum("nab,naxz->nbxz", coeffs, stacked, precision=high)
    inner = lax.psum(jnp.einsum("naxz,nbxz->nab", mixed, mixed, precision=high), "space")
    lower = jnp.linalg.cholesky(inner)
    lower_inv = lax.linalg.triangular_solve(lower, eye, left_side=True, lower=True)
    factor = jnp.swapaxes(lower_inv, 1, 2) * scales[:, None, :]
    return jnp.einsum("nab,naxz->nbxz", factor, mixed, precision=high)


def spanwise(field):
    ahead = jnp.roll(field, -1, 2)
    behind = jnp.roll(field, 1, 2)
    ahead_two = jnp.roll(field, -2, 2)
    behind_two = jnp.roll(field, 2, 2)
    return (8.0 * (ahead - behind) - (ahead_two - behind_two)) / 12.0


def local(velocity):
    rows = velocity.shape[2]
    padded = extended(velocity, (("space", 2),), 2).astype(jnp.float32)
    stream_u = padded[:, 0, 2 : rows + 2]
    span_v = padded[:, 1]
    dv_dx = (
        8.0 * (span_v[:, 3 : rows + 3] - span_v[:, 1 : rows + 1])
        - (span_v[:, 4:] - span_v[:, :rows])
    ) / 12.0
    vorticity = (dv_dx - spanwise(stream_u)).astype(jnp.bfloat16)
    blocks = lax.axis_size("tm")
    levels = blocks.bit_length() - 1
    my_block = lax.axis_index("tm")
    share = RANK // blocks
    fields = vorticity.astype(jnp.float32)
    for level in range(levels):
        if level == 0:
            partner = partner_2(vorticity, "tm", 0).astype(jnp.float32)
        else:
            partner = partner_2(fields, "tm", level)
        upper = my_block // 2**level % 2 == 1
        first = jnp.where(upper, partner, fields)
        second = jnp.where(upper, fields, partner)
        fields = merge_nodes(jnp.concatenate([first, second], axis=0)[None])[0]
    modes = lax.dynamic_slice_in_dim(fields, my_block * share, share, 0)
    return (vorticity, modes)


def solution(mesh):
    in_specs = (P("tm", None, "space", None),)
    out_specs = (P("tm", "space", None), P("tm", "space", None))
    return jax.shard_map(local, mesh=mesh, in_specs=in_specs, out_specs=out_specs, check_vma=False)
```

profile of v0, /device:TPU:1, one launch (start us, length us, event | category | flops | bytes accessed | tf_op | source)
XLA Modules:
  0.0 1042.7 jit_solution(1491497612664828559)
XLA Ops:
  0.6 2.7 copy.17
  3.4 3.3 collective-permute-start.1
  6.7 3.5 collective-permute-done.1
  11.0 0.8 fusion.60
  11.9 0.8 fusion.58
  13.2 2.4 fusion.9
  15.6 1.7 collective-permute-start.2
  17.4 15.3 %collective-permute-done.2 = bf16[32,16,1024]{2,0,1:T(8,128)(2,1)S(1)} collective-permute-done((bf16[32,16,1024]{2,0,1:T(8,128)(2,1)S(1)}, bf16[32,16,1024]{2,0,1:T(8,128)(2,1)S(1)}, u32[]{:S(2)}, u32[]{:S(2)}) %collective-permute-start.2) | collective-permute-done | bytes 1048608 | tf_op jit(solution)/shard_map/ppermute | solution.py:26
  33.3 1.3 copy-done
  35.2 3.4 fusion.14
  38.6 132.6 %psum.42 = f32[1,64,64]{2,1,0:T(8,128)S(1)} all-reduce(f32[1,64,64]{2,1,0:T(8,128)S(1)} %fusion.14), channel_id=1, replica_groups=mesh['space'=32,'tm'=8] {'space'}, use_global_device_ids=true, to_apply=%region_0.1 | all-reduce | flops 4096 | bytes 32768 | tf_op jit(solution)/shard_map/psum | solution.py:31
  171.2 4.2 fusion.4
  175.4 1.8 convolution_bitcast_fusion.5
  177.2 123.8 %psum.43 = f32[1,32,32]{1,2,0:T(8,128)S(1)} all-reduce(f32[1,32,32]{1,2,0:T(8,128)S(1)} %convolution_bitcast_fusion.5), channel_id=1, replica_groups=mesh['space'=32,'tm'=8] {'space'}, use_global_device_ids=true, to_apply=%region_1.2 | all-reduce | flops 1024 | bytes 8192 | tf_op jit(solution)/shard_map/psum | solution.py:37
  301.1 2.9 custom-call.16
  305.3 2.4 custom-call.17
  307.8 0.8 gather_fusion
  308.9 3.3 fusion.62
  312.2 3.0 collective-permute-start.3
  315.2 89.8 %collective-permute-done.3 = f32[32,16,1024]{2,0,1:T(8,128)S(1)} collective-permute-done((f32[32,16,1024]{2,0,1:T(8,128)}, f32[32,16,1024]{2,0,1:T(8,128)S(1)}, u32[]{:S(2)}, u32[]{:S(2)}) %collective-permute-start.3) | collective-permute-done | bytes 2097184 | tf_op jit(solution)/shard_map/ppermute | solution.py:26
  405.0 2.1 broadcast_select_fusion.1
  407.1 1.3 copy-done.2
  408.4 0.7 copy-done.3
  409.1 3.4 fusion.15
  412.5 121.9 %psum.44 = f32[1,64,64]{2,1,0:T(8,128)S(1)} all-reduce(f32[1,64,64]{2,1,0:T(8,128)S(1)} %fusion.15), channel_id=1, replica_groups=mesh['space'=32,'tm'=8] {'space'}, use_global_device_ids=true, to_apply=%region_4.7 | all-reduce | flops 4096 | bytes 32768 | tf_op jit(solution)/shard_map/psum | solution.py:31
  534.3 4.2 fusion.2
  538.6 1.8 convolution_bitcast_fusion.3
  540.3 123.8 %psum.45 = f32[1,32,32]{1,2,0:T(8,128)S(1)} all-reduce(f32[1,32,32]{1,2,0:T(8,128)S(1)} %convolution_bitcast_fusion.3), channel_id=1, replica_groups=mesh['space'=32,'tm'=8] {'space'}, use_global_device_ids=true, to_apply=%region_5.8 | all-reduce | flops 1024 | bytes 8192 | tf_op jit(solution)/shard_map/psum | solution.py:37
  664.2 2.9 custom-call.18
  668.5 2.4 custom-call.19
  670.9 0.8 gather_fusion.1
  672.0 3.3 fusion.63
  675.3 6.5 collective-permute-start.4
  681.8 1.5 copy.29
  683.4 87.2 %collective-permute-done.4 = f32[32,16,1024]{2,0,1:T(8,128)S(1)} collective-permute-done((f32[32,16,1024]{2,0,1:T(8,128)}, f32[32,16,1024]{2,0,1:T(8,128)S(1)}, u32[]{:S(2)}, u32[]{:S(2)}) %collective-permute-start.4) | collective-permute-done | bytes 2097184 | tf_op jit(solution)/shard_map/ppermute | solution.py:26
  770.6 2.1 broadcast_select_fusion.3
  772.8 1.3 copy-done.4
  774.0 0.7 copy-done.5
  774.7 3.4 fusion.16
  778.1 123.8 %psum.46 = f32[1,64,64]{2,1,0:T(8,128)S(1)} all-reduce(f32[1,64,64]{2,1,0:T(8,128)S(1)} %fusion.16), channel_id=1, replica_groups=mesh['space'=32,'tm'=8] {'space'}, use_global_device_ids=true, to_apply=%region_6.9 | all-reduce | flops 4096 | bytes 32768 | tf_op jit(solution)/shard_map/psum | solution.py:31
  901.9 4.2 fusion
  906.2 1.8 convolution_bitcast_fusion.1
  907.9 123.8 %psum.47 = f32[1,32,32]{1,2,0:T(8,128)S(1)} all-reduce(f32[1,32,32]{1,2,0:T(8,128)S(1)} %convolution_bitcast_fusion.1), channel_id=1, replica_groups=mesh['space'=32,'tm'=8] {'space'}, use_global_device_ids=true, to_apply=%region_7.10 | all-reduce | flops 1024 | bytes 8192 | tf_op jit(solution)/shard_map/psum | solution.py:37
  1031.8 2.9 custom-call.20
  1036.0 2.4 custom-call.21
  1038.5 0.8 gather_fusion.2
  1039.6 1.9 fusion.64
  1041.6 0.9 copy.30
  (39 shorter events, 8.0 us)
Async XLA Ops:
  3.4 6.8 collective-permute-start.1
  6.7 3.9 collective-permute-start
  15.6 17.0 %collective-permute-start.2 = (bf16[32,16,1024]{2,0,1:T(8,128)(2,1)S(1)}, bf16[32,16,1024]{2,0,1:T(8,128)(2,1)S(1)}, u32[]{:S(2)}, u32[]{:S(2)}) collective-permute-start(bf16[32,16,1024]{2,0,1:T(8,128)(2,1)S(1)} %fusion.9), channel_id=1, source_target_pairs={{0,1},{1,0},{2,3},{3,2},{4,5},{5,4},{6,7},{7,6},{8,9},{9,8},{10,11... | collective-permute-start | bytes 3145736 | tf_op jit(solution)/shard_map/ppermute | solution.py:26
  33.2 1.3 copy-start
  33.2 2.0 copy-start.1
  312.2 92.8 %collective-permute-start.3 = (f32[32,16,1024]{2,0,1:T(8,128)}, f32[32,16,1024]{2,0,1:T(8,128)S(1)}, u32[]{:S(2)}, u32[]{:S(2)}) collective-permute-start(f32[32,16,1024]{2,0,1:T(8,128)} %fusion.62), channel_id=1, source_target_pairs={{0,2},{1,3},{2,0},{3,1},{4,6},{5,7},{6,4},{7,5},{8,10},{9,11},{10,... | collective-permute-start | bytes 6291464 | tf_op jit(solution)/shard_map/ppermute | solution.py:26
  407.1 1.3 copy-start.2
  407.1 2.0 copy-start.3
  675.3 95.3 %collective-permute-start.4 = (f32[32,16,1024]{2,0,1:T(8,128)}, f32[32,16,1024]{2,0,1:T(8,128)S(1)}, u32[]{:S(2)}, u32[]{:S(2)}) collective-permute-start(f32[32,16,1024]{2,0,1:T(8,128)} %fusion.63), channel_id=1, source_target_pairs={{0,4},{1,5},{2,6},{3,7},{4,0},{5,1},{6,2},{7,3},{8,12},{9,13},{10,... | collective-permute-start | bytes 6291464 | tf_op jit(solution)/shard_map/ppermute | solution.py:26
  772.7 1.3 copy-start.4
  772.7 2.0 copy-start.5
where the time goes:
time: 1050 us; the launch traced here: 1040 us
  blocking collectives  750 us (71%)
  waiting for transfers between devices  196 us (19%)
  matrix products  37.2 us (4%)
  other arithmetic  28.1 us (3%)
  local copies, waits for them, and re-layouts  15.8 us (2%)
  starting transfers between devices  14.6 us (1%)
    psum x3, blocking collectives, merge_nodes(): lax.psum(jnp.einsum('naxz,nbxz->nab', stacked, stacked, precision=high),...  378 us
    psum x3, blocking collectives, merge_nodes(): lax.psum(jnp.einsum('naxz,nbxz->nab', mixed, mixed, precision=high), 'spa...  371 us
    ppermute x3, waiting for transfers between devices, partner_2(): return lax.ppermute(value, axis, pairs)  192 us
  transfers between devices with their start and end apart: 5, of which 5 were waited for; matrix products, arithmetic and copies ran while one was open for 0% of the time, Pallas kernels for 0%

commit v1 on v0

v1 whole, which is shorter than its diff:
```python
import jax
import jax.numpy as jnp
from jax import lax
from jax.sharding import PartitionSpec as P

RANK = 32
HIGH = lax.Precision.HIGHEST


def halo_rows(block, width):
    count = lax.axis_size("space")
    forward = [(i, (i + 1) % count) for i in range(count)]
    backward = [(target, source) for source, target in forward]
    rows = block.shape[1]
    low = lax.ppermute(block[:, rows - width :], "space", forward)
    high = lax.ppermute(block[:, :width], "space", backward)
    return jnp.concatenate([low, block, high], axis=1)


def spanwise(field):
    ahead = jnp.roll(field, -1, 2)
    behind = jnp.roll(field, 1, 2)
    ahead_two = jnp.roll(field, -2, 2)
    behind_two = jnp.roll(field, 2, 2)
    return (8.0 * (ahead - behind) - (ahead_two - behind_two)) / 12.0


def merge_small(gram):
    coeffs = gram[:, :, :RANK] + gram[:, :, RANK:]
    diagonal = jnp.diagonal(gram, axis1=1, axis2=2)
    scales = jnp.sqrt(diagonal[:, :RANK] + diagonal[:, RANK:])
    half = jnp.einsum("nab,nbc->nac", gram, coeffs, precision=HIGH)
    inner = jnp.einsum("nab,nac->nbc", coeffs, half, precision=HIGH)
    lower = jnp.linalg.cholesky(inner)
    eye = jnp.broadcast_to(jnp.eye(RANK, dtype=jnp.float32), inner.shape)
    lower_inv = lax.linalg.triangular_solve(lower, eye, left_side=True, lower=True)
    factor = jnp.swapaxes(lower_inv, 1, 2) * scales[:, None, :]
    return jnp.einsum("nab,nbc->nac", coeffs, factor, precision=HIGH)


def tree_basis(gram, leaves):
    width = leaves * RANK
    basis = None
    span = 1
    while span < leaves:
        nodes = leaves // (2 * span)
        size = 2 * span * RANK
        sub = jnp.stack(
            [gram[k * size : (k + 1) * size, k * size : (k + 1) * size] for k in range(nodes)]
        )
        if basis is None:
            h = sub
        else:
            b = basis.reshape(nodes, 2, span * RANK, RANK)
            zero = jnp.zeros_like(b[:, 0])
            bd = jnp.concatenate(
                [
                    jnp.concatenate([b[:, 0], zero], axis=2),
                    jnp.concatenate([zero, b[:, 1]], axis=2),
                ],
                axis=1,
            )
            gb = jnp.einsum("nab,nbc->nac", sub, bd, precision=HIGH)
            h = jnp.einsum("nab,nac->nbc", bd, gb, precision=HIGH)
        c = merge_small(h)
        if basis is None:
            basis = c
        else:
            basis = jnp.einsum("nab,nbc->nac", bd, c, precision=HIGH)
        span *= 2
    return basis.reshape(width, RANK)


def local(velocity):
    rows = velocity.shape[2]
    span_v = halo_rows(velocity[:, 1], 2).astype(jnp.float32)
    stream_u = velocity[:, 0].astype(jnp.float32)
    dv_dx = (
        8.0 * (span_v[:, 3 : rows + 3] - span_v[:, 1 : rows + 1])
        - (span_v[:, 4:] - span_v[:, :rows])
    ) / 12.0
    vorticity = (dv_dx - spanwise(stream_u)).astype(jnp.bfloat16)
    blocks = lax.axis_size("tm")
    cells = lax.all_to_all(vorticity, "tm", 2, 0, tiled=True)
    flat = cells.reshape(cells.shape[0], -1)
    gram = jnp.einsum("ax,bx->ab", flat, flat, preferred_element_type=jnp.float32)
    gram = lax.psum(gram, ("space", "tm"))
    basis = tree_basis(gram, blocks)
    part = jnp.einsum(
        "ab,ax->bx", basis, flat.astype(jnp.float32), precision=HIGH
    ).reshape(RANK, rows, -1)
    modes = lax.all_to_all(part, "tm", 0, 2, tiled=True)
    return (vorticity, modes)


def solution(mesh):
    in_specs = (P("tm", None, "space", None),)
    out_specs = (P("tm", "space", None), P("tm", "space", None))
    return jax.shard_map(local, mesh=mesh, in_specs=in_specs, out_specs=out_specs, check_vma=False)
```

time: 1050 us -> 412 us (0.39)
  blocking collectives: 750 us -> 17.3 us
  waiting for transfers between devices: 196 us -> 274 us
  matrix products: 37.2 us -> 10.4 us
  local copies, waits for them, and re-layouts: 15.8 us -> 37.9 us
  other arithmetic: 28.1 us -> 44.8 us
  between operations: 1.13 us -> 14.4 us
    psum x6 -> x0, blocking collectives: 750 us -> none  [the longest x3 378 us: merge_nodes(): lax.psum(jnp.einsum('naxz,nbxz->nab', stacked, stacked, precision=high),...]
    psum x0 -> x1, waiting for transfers between devices: none -> 243 us  [local(): gram = lax.psum(gram, ('space', 'tm'))]
    ppermute x5 -> x2, waiting for transfers between devices: 196 us -> 1.94 us  [the longest x1 1.93 us: halo_rows(): high = lax.ppermute(block[:, :width], 'space', backward)]
    all_to_all x0 -> x1, waiting for transfers between devices: none -> 28.9 us  [local(): cells = lax.all_to_all(vorticity, 'tm', 2, 0, tiled=True)]
    dot_general x12 -> x17, matrix products: 36.5 us -> 8.34 us  [the longest x3 2.15 us: merge_small(): inner = jnp.einsum('nab,nac->nbc', coeffs, half, precision=HIGH)]
    another operation x15 -> x17, other arithmetic: 20 us -> 39.5 us  [the longest x9 21.5 us: merge_small(): lower = jnp.linalg.cholesky(inner)]
    all_to_all x0 -> x1, blocking collectives: none -> 17.3 us  [local(): modes = lax.all_to_all(part, 'tm', 0, 2, tiled=True)]
    ppermute x5 -> x2, starting transfers between devices: 14.6 us -> 3.41 us  [the longest x1 2.76 us: halo_rows(): low = lax.ppermute(block[:, rows - width:], 'space', forward)]
  transfers between devices with their start and end apart: 5 -> 4, of which waited for: 5 -> 3; matrix products, arithmetic and copies ran while one was open for 0% -> 1% of each run, Pallas kernels for 0% -> 0%
where the time goes in v1:
time: 412 us; the launch traced here: 411 us
  waiting for transfers between devices  274 us (67%)
  other arithmetic  44.8 us (11%)
  local copies, waits for them, and re-layouts  37.9 us (9%)
  blocking collectives  17.3 us (4%)
  between operations  14.4 us (3%)
  starting transfers between devices  12.1 us (3%)
  matrix products  10.4 us (3%)
    psum x1, waiting for transfers between devices, local(): gram = lax.psum(gram, ('space', 'tm'))  243 us
    all_to_all x1, waiting for transfers between devices, local(): cells = lax.all_to_all(vorticity, 'tm', 2, 0, tiled=True)  28.9 us
    another operation x9, other arithmetic, merge_small(): lower = jnp.linalg.cholesky(inner)  21.5 us
    another operation x7, other arithmetic, merge_small(): lax.linalg.triangular_solve(lower, eye, left_side=True, lower=True)  18 us
    all_to_all x1, blocking collectives, local(): modes = lax.all_to_all(part, 'tm', 0, 2, tiled=True)  17.3 us
    unnamed x8, local copies, waits for them, and re-layouts  13.2 us
    all_to_all x1, starting transfers between devices, local(): cells = lax.all_to_all(vorticity, 'tm', 2, 0, tiled=True)  8.48 us
  transfers between devices with their start and end apart: 4, of which 3 were waited for; matrix products, arithmetic and copies ran while one was open for 1% of the time, Pallas kernels for 0%

profile of v1, /device:TPU:1, one launch (start us, length us, event | category | flops | bytes accessed | tf_op | source)
XLA Modules:
  0.0 410.9 jit_solution(9131504356403751906)
XLA Ops:
  7.2 1.9 bitcast_convert_fusion
  9.0 0.6 copy.179
  9.6 2.8 collective-permute-start
  12.4 0.6 collective-permute-start.1
  13.0 0.7 fusion.72
  13.8 0.7 fusion.74
  14.9 1.9 collective-permute-done.1
  17.0 0.8 copy_convert_fusion
  17.8 2.2 fusion.3
  20.0 5.1 %copy.130 = bf16[32,16,1024]{0,1,2:T(8,128)(2,1)} copy(bf16[32,16,1024]{2,1,0:T(8,128)(2,1)S(1)} %fusion.3) | data formatting | bytes 2097152 | tf_op jit(solution)/shard_map/convert_element_type | solution.py:82
  25.1 7.8 %reshape.157 = bf16[8,2,32768]{2,1,0:T(2,128)(2,1)} reshape(bf16[1024,16,32]{2,1,0:T(8,128)(2,1)} %bitcast.133) | data formatting | bytes 2097152
  32.9 8.5 %all-to-all-start = ((bf16[8,2,32768]{2,1,0:T(2,128)(2,1)}), bf16[8,2,32768]{2,1,0:T(2,128)(2,1)S(1)}, u32[]{:S(2)}, u32[]{:S(2)}) async-start(bf16[8,2,32768]{2,1,0:T(2,128)(2,1)} %reshape.157), calls=%async_computation | async-start | bytes 2097152 | tf_op jit(solution)/shard_map/all_to_all | solution.py:84
  41.7 28.9 %all-to-all-done = bf16[8,2,32768]{2,1,0:T(2,128)(2,1)S(1)} async-done(((bf16[8,2,32768]{2,1,0:T(2,128)(2,1)}), bf16[8,2,32768]{2,1,0:T(2,128)(2,1)S(1)}, u32[]{:S(2)}, u32[]{:S(2)}) %all-to-all-start) | async-done | bytes 1048608 | tf_op jit(solution)/shard_map/all_to_all | solution.py:84
  70.6 4.5 %reshape.158 = bf16[1024,16,32]{2,1,0:T(8,128)(2,1)} reshape(bf16[8,2,32768]{2,1,0:T(2,128)(2,1)S(1)} %all-to-all-done) | data formatting | bytes 2097152
  75.1 5.4 %copy.131 = bf16[32,16,8,128]{3,1,0,2:T(8,128)(2,1)S(1)} copy(bf16[32,16,8,128]{0,1,3,2:T(8,128)(2,1)} %bitcast.132) | data formatting | bytes 2097152 | tf_op jit(solution)/shard_map/all_to_all | solution.py:84
  80.5 1.2 fusion.10
  81.7 0.7 copy.133
  82.7 0.5 copy.152
  83.2 243.0 %all-reduce.6.cloned.1.call-done = f32[256,256]{0,1:T(8,128)} async-done(((f32[256,256]{0,1:T(8,128)}), f32[256,256]{0,1:T(8,128)}) %all-reduce.6.cloned.1.call-update) | async-done | bytes 262160 | tf_op jit(solution)/shard_map/psum | solution.py:87
  326.3 0.9 slice_bitcast_fusion.7
  327.2 1.9 copy.137
  329.1 0.9 fusion.70
  330.0 1.5 gather_fusion
  331.5 0.8 copy.138
  332.4 1.1 fusion.69
  333.6 11.7 %custom-call.21 = f32[4,32,32]{2,1,0:T(8,128)S(1)} custom-call(f32[4,32,32]{2,1,0:T(8,128)S(1)} %fusion.19), custom_call_target="Cholesky" | custom-call | tf_op jit(solution)/shard_map/jit(cholesky)/cholesky | solution.py:34
  345.5 9.8 %custom-call.22 = f32[4,1,32,32]{2,3,1,0:T(8,128)S(1)} custom-call(f32[4,1,32,32]{3,2,1,0:T(8,128)S(1)} %select_bitcast_fusion), custom_call_target="InvertDiagBlocksLowerTriangular" | custom-call | tf_op jit(solution)/shard_map/triangular_solve | solution.py:36
  355.4 0.9 convolution_multiply_fusion
  356.3 0.3 fusion.68
  356.7 0.3 fusion.13
  356.9 0.3 fusion.39
  357.3 1.9 copy.147
  359.2 0.8 fusion.67
  360.0 1.5 gather_fusion.1
  361.4 0.8 copy.148
  362.3 0.9 fusion.66
  363.4 5.9 %custom-call.23 = f32[2,32,32]{2,1,0:T(8,128)S(1)} custom-call(f32[2,32,32]{2,1,0:T(8,128)S(1)} %fusion.32), custom_call_target="Cholesky" | custom-call | tf_op jit(solution)/shard_map/jit(cholesky)/cholesky | solution.py:34
  369.5 4.9 %custom-call.24 = f32[2,1,32,32]{2,3,1,0:T(8,128)S(1)} custom-call(f32[2,1,32,32]{3,2,1,0:T(8,128)S(1)} %select_bitcast_fusion.1), custom_call_target="InvertDiagBlocksLowerTriangular" | custom-call | tf_op jit(solution)/shard_map/triangular_solve | solution.py:36
  374.4 0.9 convolution_multiply_fusion.1
  375.8 0.3 fusion.23
  376.3 0.8 gather_fusion.2
  377.5 2.9 custom-call.25
  380.5 0.6 compare_reduce_fusion
  381.1 0.7 fusion.34
  381.8 2.4 custom-call.26
  384.8 1.0 fusion.76
  386.0 17.3 %all_to_all.33 = f32[32,16,128]{2,1,0:T(8,128)S(1)} all-to-all(f32[32,16,128]{2,1,0:T(8,128)S(1)} %copy.153), channel_id=1, replica_groups=mesh['space'=32,'tm'=8] {'tm'}, dimensions={0} | all-to-all | bytes 524288 | tf_op jit(solution)/shard_map/all_to_all | solution.py:92
  403.3 0.7 copy.180
  (45 shorter events, 3.7 us)
Async XLA Ops:
  9.6 5.2 %collective-permute-start = (bf16[32,2,1024]{2,0,1:T(8,128)(2,1)S(1)}, bf16[32,2,1024]{2,0,1:T(8,128)(2,1)S(1)}, u32[]{:S(2)}, u32[]{:S(2)}) collective-permute-start(bf16[32,2,1024]{2,0,1:T(8,128)(2,1)S(1)} %get-tuple-element.18), channel_id=1, source_target_pairs={{0,8},{8,16},{16,24},{24,32},{32,40},{40,48},{48,56},{56,64},{64,7... | collective-permute-start | bytes 393224 | tf_op jit(solution)/shard_map/ppermute | solution.py:15
  12.4 4.4 %collective-permute-start.1 = (bf16[32,2,1024]{2,0,1:T(8,128)(2,1)S(1)}, bf16[32,2,1024]{2,0,1:T(8,128)(2,1)S(1)}, u32[]{:S(2)}, u32[]{:S(2)}) collective-permute-start(bf16[32,2,1024]{2,0,1:T(8,128)(2,1)S(1)} %get-tuple-element.19), channel_id=1, source_target_pairs={{8,0},{16,8},{24,16},{32,24},{40,32},{48,40},{56,48},{64,56},{72,6... | collective-permute-start | bytes 393224 | tf_op jit(solution)/shard_map/ppermute | solution.py:16
  20.0 5.1 %copy-start = (bf16[32,16,1024]{2,1,0:T(8,128)(2,1)}, bf16[32,16,1024]{2,1,0:T(8,128)(2,1)S(1)}, u32[]{:S(2)}) copy-start(bf16[32,16,1024]{2,1,0:T(8,128)(2,1)S(1)} %fusion.3) | copy-start | bytes 3145732
  32.9 37.7 %all-to-all-start = ((bf16[8,2,32768]{2,1,0:T(2,128)(2,1)}), bf16[8,2,32768]{2,1,0:T(2,128)(2,1)S(1)}, u32[]{:S(2)}, u32[]{:S(2)}) async-start(bf16[8,2,32768]{2,1,0:T(2,128)(2,1)} %reshape.157), calls=%async_computation | async-start | bytes 2097152 | tf_op jit(solution)/shard_map/all_to_all | solution.py:84
  41.4 284.9 %all-reduce.6.cloned.1.call-start = ((), (), s32[]{:S(2)}) async-start(), calls=%async_computation.2 | async-start | bytes 524288 | tf_op jit(solution)/shard_map/psum | solution.py:87
  327.2 29.5 %copy-start.1 = (f32[256,256]{0,1:T(8,128)S(1)}, f32[256,256]{0,1:T(8,128)}, u32[]{:S(2)}) copy-start(f32[256,256]{0,1:T(8,128)} %all-reduce.6.cloned.1.call-done) | copy-start | bytes 786436
Sparse Core Ops, SparseCore 0:
  81.8 244.3 all-reduce.5

commit v2 on v1

--- a/solution.py
+++ b/solution.py
@@ -1,6 +1,10 @@
+import functools
+
 import jax
 import jax.numpy as jnp
 from jax import lax
+from jax.experimental import pallas as pl
+from jax.experimental.pallas import tpu as pltpu
 from jax.sharding import PartitionSpec as P
 
 RANK = 32
@@ -71,6 +75,130 @@
     return basis.reshape(width, RANK)
 
 
+MESH = pl.DeviceIdType.MESH
+
+
+def allreduce_kernel(n_space, n_tm, g_ref, out_ref, buf1, buf2, buf3, send1, recv1, send2, recv2, send3, recv3):
+    s = lax.axis_index("space")
+    t = lax.axis_index("tm")
+
+    barrier = pltpu.get_barrier_semaphore()
+
+    def greet_space(k, carry):
+        b = lax.rem(s + k, n_space)
+        pl.semaphore_signal(barrier, inc=1, device_id=(b, t), device_id_type=MESH)
+        return carry
+
+    def greet_tm(k, carry):
+        a = lax.rem(t + k, n_tm)
+        pl.semaphore_signal(barrier, inc=1, device_id=(s, a), device_id_type=MESH)
+        return carry
+
+    lax.fori_loop(1, n_space, greet_space, 0)
+    lax.fori_loop(1, n_tm, greet_tm, 0)
+    pl.semaphore_wait(barrier, (n_space - 1) + (n_tm - 1))
+
+    def space_copy(src, dst_buf, send, recv, k):
+        b = lax.rem(s + k, n_space)
+        return pltpu.make_async_remote_copy(
+            src_ref=src(b), dst_ref=dst_buf.at[s], send_sem=send.at[k], recv_sem=recv.at[s],
+            device_id=(b, t), device_id_type=MESH,
+        )
+
+    def space_wait(dst_buf, send, recv, k):
+        j = lax.rem(s + k, n_space)
+        pltpu.make_async_remote_copy(
+            src_ref=dst_buf.at[j], dst_ref=dst_buf.at[j], send_sem=send.at[k], recv_sem=recv.at[j],
+            device_id=(j, t), device_id_type=MESH,
+        ).wait_recv()
+
+    def send_p1(k, carry):
+        space_copy(lambda b: g_ref.at[b], buf1, send1, recv1, k).start()
+        return carry
+
+    lax.fori_loop(1, n_space, send_p1, 0)
+    buf1[s] = g_ref[s]
+
+    def wait_p1(k, carry):
+        space_wait(buf1, send1, recv1, k)
+        return carry
+
+    lax.fori_loop(1, n_space, wait_p1, 0)
+    acc = buf1[0]
+    for j in range(1, n_space):
+        acc = acc + buf1[j]
+    buf2[t] = acc
+
+    copies = []
+    for k in range(1, n_tm):
+        a = lax.rem(t + k, n_tm)
+        c = pltpu.make_async_remote_copy(
+            src_ref=buf2.at[t], dst_ref=buf2.at[t], send_sem=send2.at[k], recv_sem=recv2.at[t],
+            device_id=(s, a), device_id_type=MESH,
+        )
+        c.start()
+        copies.append(c)
+    for k in range(1, n_tm):
+        j = lax.rem(t + k, n_tm)
+        pltpu.make_async_remote_copy(
+            src_ref=buf2.at[j], dst_ref=buf2.at[j], send_sem=send2.at[k], recv_sem=recv2.at[j],
+            device_id=(s, j), device_id_type=MESH,
+        ).wait_recv()
+    for c in copies:
+        c.wait_send()
+    acc = buf2[0]
+    for j in range(1, n_tm):
+        acc = acc + buf2[j]
+    buf3[s] = acc
+
+    def send_p3(k, carry):
+        space_copy(lambda b: buf3.at[s], buf3, send3, recv3, k).start()
+        return carry
+
+    lax.fori_loop(1, n_space, send_p3, 0)
+
+    def wait_p3(k, carry):
+        space_wait(buf3, send3, recv3, k)
+        return carry
+
+    lax.fori_loop(1, n_space, wait_p3, 0)
+
+    def drain(k, carry):
+        space_copy(lambda b: g_ref.at[b], buf1, send1, recv1, k).wait_send()
+        space_copy(lambda b: buf3.at[s], buf3, send3, recv3, k).wait_send()
+        return carry
+
+    lax.fori_loop(1, n_space, drain, 0)
+    out_ref[...] = buf3[...]
+
+
+def allreduce(gram):
+    n_space = lax.axis_size("space")
+    n_tm = lax.axis_size("tm")
+    size = gram.shape[0]
+    chunks = gram.reshape(n_space, size // n_space, size)
+    shape = chunks.shape
+    out = pl.pallas_call(
+        functools.partial(allreduce_kernel, n_space, n_tm),
+        out_shape=jax.ShapeDtypeStruct(shape, jnp.float32),
+        in_specs=[pl.BlockSpec(memory_space=pltpu.VMEM)],
+        out_specs=pl.BlockSpec(memory_space=pltpu.VMEM),
+        scratch_shapes=[
+            pltpu.VMEM(shape, jnp.float32),
+            pltpu.VMEM((n_tm,) + shape[1:], jnp.float32),
+            pltpu.VMEM(shape, jnp.float32),
+            pltpu.SemaphoreType.DMA((n_space,)),
+            pltpu.SemaphoreType.DMA((n_space,)),
+            pltpu.SemaphoreType.DMA((n_tm,)),
+            pltpu.SemaphoreType.DMA((n_tm,)),
+            pltpu.SemaphoreType.DMA((n_space,)),
+            pltpu.SemaphoreType.DMA((n_space,)),
+        ],
+        compiler_params=pltpu.CompilerParams(collective_id=0, has_side_effects=True),
+    )(chunks)
+    return out.reshape(size, size)
+
+
 def local(velocity):
     rows = velocity.shape[2]
     span_v = halo_rows(velocity[:, 1], 2).astype(jnp.float32)
@@ -84,7 +212,7 @@
     cells = lax.all_to_all(vorticity, "tm", 2, 0, tiled=True)
     flat = cells.reshape(cells.shape[0], -1)
     gram = jnp.einsum("ax,bx->ab", flat, flat, preferred_element_type=jnp.float32)
-    gram = lax.psum(gram, ("space", "tm"))
+    gram = allreduce(gram)
     basis = tree_basis(gram, blocks)
     part = jnp.einsum(
         "ab,ax->bx", basis, flat.astype(jnp.float32), precision=HIGH

time: 412 us -> 180 us (0.44)
  waiting for transfers between devices: 274 us -> 30.4 us
  Pallas kernels: 0 us -> 24.4 us
  between operations: 14.4 us -> 0.99 us
    psum x1 -> x0, waiting for transfers between devices: 243 us -> none  [local(): gram = lax.psum(gram, ('space', 'tm'))]
    pallas_call x0 -> x1, Pallas kernels: none -> 24.4 us  [allreduce(): pl.pallas_call(functools.partial(allreduce_kernel, n_space, n_tm), out_sh...]
    unnamed x8 -> x10, local copies, waits for them, and re-layouts: 13.2 us -> 13.4 us
  transfers between devices with their start and end apart: 4 -> 3, of which waited for: 3 -> 2; matrix products, arithmetic and copies ran while one was open for 1% -> 1% of each run, Pallas kernels for 0% -> 0%
where the time goes in v2:
time: 180 us; the launch traced here: 179 us
  other arithmetic  44.9 us (25%)
  local copies, waits for them, and re-layouts  39.9 us (22%)
  waiting for transfers between devices  30.4 us (17%)
  Pallas kernels  24.4 us (14%)
  blocking collectives  15.4 us (9%)
  starting transfers between devices  11.9 us (7%)
  matrix products  11.4 us (6%)
    all_to_all x1, waiting for transfers between devices, local(): cells = lax.all_to_all(vorticity, 'tm', 2, 0, tiled=True)  28.5 us
    pallas_call x1, Pallas kernels, allreduce(): pl.pallas_call(functools.partial(allreduce_kernel, n_space, n_tm), out_sh...  24.4 us
    another operation x9, other arithmetic, merge_small(): lower = jnp.linalg.cholesky(inner)  21.5 us
    another operation x7, other arithmetic, merge_small(): lax.linalg.triangular_solve(lower, eye, left_side=True, lower=True)  18 us
    all_to_all x1, blocking collectives, local(): modes = lax.all_to_all(part, 'tm', 0, 2, tiled=True)  15.4 us
    unnamed x10, local copies, waits for them, and re-layouts  13.4 us
    all_to_all x1, starting transfers between devices, local(): cells = lax.all_to_all(vorticity, 'tm', 2, 0, tiled=True)  8.48 us
    gather x5, local copies, waits for them, and re-layouts, merge_small(): diagonal = jnp.diagonal(gram, axis1=1, axis2=2)  5.4 us
  transfers between devices with their start and end apart: 3, of which 2 were waited for; matrix products, arithmetic and copies ran while one was open for 1% of the time, Pallas kernels for 0%

profile of v2, /device:TPU:1, one launch (start us, length us, event | category | flops | bytes accessed | tf_op | source)
XLA Modules:
  0.0 179.3 jit_solution(5613114596836068142)
XLA Ops:
  0.6 1.9 %bitcast_convert_fusion = (f32[32,16,1024]{2,1,0:T(8,128)S(1)}, bf16[32,1,16,1024]{3,2,1,0:T(8,128)(2,1)S(1)}) fusion(bf16[32,2,16,1024]{3,2,1,0:T(8,128)(2,1)} %param.1), kind=kLoop, calls=%fused_computation.25 | loop fusion | flops 524288 | bytes 5242880 | tf_op jit(solution)/shard_map/convert_element_type | solution.py:205
  2.5 0.6 copy.208
  3.1 2.8 %collective-permute-start = (bf16[32,2,1024]{2,0,1:T(8,128)(2,1)S(1)}, bf16[32,2,1024]{2,0,1:T(8,128)(2,1)S(1)}, u32[]{:S(2)}, u32[]{:S(2)}) collective-permute-start(bf16[32,2,1024]{2,0,1:T(8,128)(2,1)S(1)} %get-tuple-element.18), channel_id=1, source_target_pairs={{0,8},{8,16},{16,24},{24,32},{32,40},{40,48},{48,56},{56,64},{64,7... | collective-permute-start | bytes 393224 | tf_op jit(solution)/shard_map/ppermute | solution.py:19
  5.9 0.6 collective-permute-start.1
  6.5 0.7 fusion.70
  7.3 0.7 fusion.72
  8.3 1.9 %collective-permute-done.1 = bf16[32,2,1024]{2,0,1:T(8,128)(2,1)S(1)} collective-permute-done((bf16[32,2,1024]{2,0,1:T(8,128)(2,1)S(1)}, bf16[32,2,1024]{2,0,1:T(8,128)(2,1)S(1)}, u32[]{:S(2)}, u32[]{:S(2)}) %collective-permute-start.1) | collective-permute-done | bytes 131104 | tf_op jit(solution)/shard_map/ppermute | solution.py:20
  10.4 0.8 copy_convert_fusion
  11.2 2.2 %fusion.3 = bf16[32,16,1024]{2,1,0:T(8,128)(2,1)S(1)} fusion(f32[32,20,1024]{2,1,0:T(8,128)S(1)} %copy_convert_fusion, f32[32,16,1]{2,1,0:T(8,128)S(1)} %get-tuple-element.13, f32[32,16,1023]{2,1,0:T(8,128)S(1)} %get-tuple-element.15, f32[32,16,1023]{2,1,0:T(8,128)S(1)} %get-tuple-element.14, f32[32,16,1]{2,1,0:T(8,128)S(1)} %get-tuple-element.12, ...), kind=kLoop, calls=%fused_computation.7 | loop fusion | flops 8388608 | bytes 17825792 | tf_op jit(solution)/shard_map/convert_element_type | solution.py:210
  13.5 5.1 %copy.160 = bf16[32,16,1024]{0,1,2:T(8,128)(2,1)} copy(bf16[32,16,1024]{2,1,0:T(8,128)(2,1)S(1)} %fusion.3) | data formatting | bytes 2097152 | tf_op jit(solution)/shard_map/convert_element_type | solution.py:210
  18.6 7.8 %reshape.166 = bf16[8,2,32768]{2,1,0:T(2,128)(2,1)} reshape(bf16[1024,16,32]{2,1,0:T(8,128)(2,1)} %bitcast.137) | data formatting | bytes 2097152
  26.4 8.5 %all-to-all-start = ((bf16[8,2,32768]{2,1,0:T(2,128)(2,1)}), bf16[8,2,32768]{2,1,0:T(2,128)(2,1)S(1)}, u32[]{:S(2)}, u32[]{:S(2)}) async-start(bf16[8,2,32768]{2,1,0:T(2,128)(2,1)} %reshape.166), calls=%async_computation | async-start | bytes 2097152 | tf_op jit(solution)/shard_map/all_to_all | solution.py:212
  34.9 0.7 copy.166
  35.6 28.5 %all-to-all-done = bf16[8,2,32768]{2,1,0:T(2,128)(2,1)S(1)} async-done(((bf16[8,2,32768]{2,1,0:T(2,128)(2,1)}), bf16[8,2,32768]{2,1,0:T(2,128)(2,1)S(1)}, u32[]{:S(2)}, u32[]{:S(2)}) %all-to-all-start) | async-done | bytes 1048608 | tf_op jit(solution)/shard_map/all_to_all | solution.py:212
  64.1 4.5 %reshape.167 = bf16[1024,16,32]{2,1,0:T(8,128)(2,1)} reshape(bf16[8,2,32768]{2,1,0:T(2,128)(2,1)S(1)} %all-to-all-done) | data formatting | bytes 2097152
  68.6 5.4 %copy.161 = bf16[32,16,8,128]{3,1,0,2:T(8,128)(2,1)S(1)} copy(bf16[32,16,8,128]{0,1,3,2:T(8,128)(2,1)} %bitcast.136) | data formatting | bytes 2097152 | tf_op jit(solution)/shard_map/all_to_all | solution.py:212
  74.0 0.5 dot_general.61
  74.5 0.5 reshape.163
  75.0 1.2 fusion.75.g_ref
  76.2 24.4 %shard_map.30 = f32[32,8,256]{2,1,0:T(8,128)} custom-call(f32[32,8,256]{2,1,0:T(8,128)} %fusion.75.g_ref), custom_call_target="tpu_custom_call" | custom-call | tf_op jit(solution)/shard_map/pallas_call | solution.py:181
  100.6 0.9 fusion.74
  101.9 1.9 %copy.170 = f32[4,64,64]{0,2,1:T(8,128)S(1)} copy(f32[4,64,64]{1,2,0:T(8,128)S(1)} %pad_maximum_fusion.1) | data formatting | bytes 131072 | tf_op jit(solution)/shard_map/stack | solution.py:52
  103.8 0.9 fusion.68
  104.6 0.6 slice_bitcast_fusion.1
  105.3 1.5 gather_fusion
  106.8 0.8 copy.171
  107.7 1.1 fusion.67
  108.9 11.7 %custom-call.21 = f32[4,32,32]{2,1,0:T(8,128)S(1)} custom-call(f32[4,32,32]{2,1,0:T(8,128)S(1)} %fusion.16), custom_call_target="Cholesky" | custom-call | tf_op jit(solution)/shard_map/jit(cholesky)/cholesky | solution.py:38
  120.8 9.8 %custom-call.22 = f32[4,1,32,32]{2,3,1,0:T(8,128)S(1)} custom-call(f32[4,1,32,32]{3,2,1,0:T(8,128)S(1)} %select_bitcast_fusion), custom_call_target="InvertDiagBlocksLowerTriangular" | custom-call | tf_op jit(solution)/shard_map/triangular_solve | solution.py:40
  130.7 0.9 convolution_multiply_fusion
  131.9 1.2 fusion.10
  133.5 1.9 %copy.179 = f32[2,64,64]{0,2,1:T(8,128)S(1)} copy(f32[2,64,64]{1,2,0:T(8,128)S(1)} %fusion.36) | data formatting | bytes 65536 | tf_op jit(solution)/shard_map/nab,nac->nbc/dot_general | solution.py:68
  135.4 0.8 fusion.65
  136.2 1.5 gather_fusion.1
  137.7 0.8 copy.180
  138.6 0.9 fusion.64
  139.6 5.9 %custom-call.23 = f32[2,32,32]{2,1,0:T(8,128)S(1)} custom-call(f32[2,32,32]{2,1,0:T(8,128)S(1)} %fusion.29), custom_call_target="Cholesky" | custom-call | tf_op jit(solution)/shard_map/jit(cholesky)/cholesky | solution.py:38
  145.7 4.9 %custom-call.24 = f32[2,1,32,32]{2,3,1,0:T(8,128)S(1)} custom-call(f32[2,1,32,32]{3,2,1,0:T(8,128)S(1)} %select_bitcast_fusion.1), custom_call_target="InvertDiagBlocksLowerTriangular" | custom-call | tf_op jit(solution)/shard_map/triangular_solve | solution.py:40
  150.6 0.9 convolution_multiply_fusion.1
  152.6 0.8 gather_fusion.2
  153.8 2.9 %custom-call.25 = f32[1,32,32]{2,1,0:T(8,128)S(1)} custom-call(f32[1,32,32]{2,1,0:T(8,128)S(1)} %fusion.33), custom_call_target="Cholesky" | custom-call | tf_op jit(solution)/shard_map/jit(cholesky)/cholesky | solution.py:38
  156.8 0.6 compare_reduce_fusion
  157.4 0.7 fusion.31
  158.1 2.4 %custom-call.26 = f32[1,1,32,32]{2,3,1,0:T(8,128)S(1)} custom-call(f32[1,1,32,32]{3,2,1,0:T(8,128)S(1)} %fusion.31), custom_call_target="InvertDiagBlocksLowerTriangular" | custom-call | tf_op jit(solution)/shard_map/triangular_solve | solution.py:40
  161.4 0.5 copy.194
  162.0 1.0 fusion.76
  163.1 15.4 %all_to_all.33 = f32[32,16,128]{2,1,0:T(8,128)S(1)} all-to-all(f32[32,16,128]{2,1,0:T(8,128)S(1)} %copy.185), channel_id=1, replica_groups=mesh['space'=32,'tm'=8] {'tm'}, dimensions={0} | all-to-all | bytes 524288 | tf_op jit(solution)/shard_map/all_to_all | solution.py:220
  178.6 0.7 copy.209
  (49 shorter events, 4.8 us)
Async XLA Ops:
  3.1 5.2 %collective-permute-start = (bf16[32,2,1024]{2,0,1:T(8,128)(2,1)S(1)}, bf16[32,2,1024]{2,0,1:T(8,128)(2,1)S(1)}, u32[]{:S(2)}, u32[]{:S(2)}) collective-permute-start(bf16[32,2,1024]{2,0,1:T(8,128)(2,1)S(1)} %get-tuple-element.18), channel_id=1, source_target_pairs={{0,8},{8,16},{16,24},{24,32},{32,40},{40,48},{48,56},{56,64},{64,7... | collective-permute-start | bytes 393224 | tf_op jit(solution)/shard_map/ppermute | solution.py:19
  5.9 4.4 %collective-permute-start.1 = (bf16[32,2,1024]{2,0,1:T(8,128)(2,1)S(1)}, bf16[32,2,1024]{2,0,1:T(8,128)(2,1)S(1)}, u32[]{:S(2)}, u32[]{:S(2)}) collective-permute-start(bf16[32,2,1024]{2,0,1:T(8,128)(2,1)S(1)} %get-tuple-element.19), channel_id=1, source_target_pairs={{8,0},{16,8},{24,16},{32,24},{40,32},{48,40},{56,48},{64,56},{72,6... | collective-permute-start | bytes 393224 | tf_op jit(solution)/shard_map/ppermute | solution.py:20
  13.5 5.1 %copy-start = (bf16[32,16,1024]{2,1,0:T(8,128)(2,1)}, bf16[32,16,1024]{2,1,0:T(8,128)(2,1)S(1)}, u32[]{:S(2)}) copy-start(bf16[32,16,1024]{2,1,0:T(8,128)(2,1)S(1)} %fusion.3) | copy-start | bytes 3145732
  26.4 37.7 %all-to-all-start = ((bf16[8,2,32768]{2,1,0:T(2,128)(2,1)}), bf16[8,2,32768]{2,1,0:T(2,128)(2,1)S(1)}, u32[]{:S(2)}, u32[]{:S(2)}) async-start(bf16[8,2,32768]{2,1,0:T(2,128)(2,1)} %reshape.166), calls=%async_computation | async-start | bytes 2097152 | tf_op jit(solution)/shard_map/all_to_all | solution.py:212
  100.6 4.1 %copy-start.1 = (f32[32,8,256]{2,1,0:T(8,128)S(1)}, f32[32,8,256]{2,1,0:T(8,128)}, u32[]{:S(2)}) copy-start(f32[32,8,256]{2,1,0:T(8,128)} %shard_map.30) | copy-start | bytes 786436

commit v3 on v2

--- a/solution.py
+++ b/solution.py
@@ -199,6 +199,58 @@
     return out.reshape(size, size)
 
 
+def a2a_kernel(n_tm, src_at, dst_at, x_ref, out_ref, buf, send, recv, own):
+    s = lax.axis_index("space")
+    t = lax.axis_index("tm")
+    barrier = pltpu.get_barrier_semaphore()
+    for k in range(1, n_tm):
+        a = lax.rem(t + k, n_tm)
+        pl.semaphore_signal(barrier, inc=1, device_id=(s, a), device_id_type=MESH)
+    pl.semaphore_wait(barrier, n_tm - 1)
+    copies = []
+    for k in range(1, n_tm):
+        a = lax.rem(t + k, n_tm)
+        c = pltpu.make_async_remote_copy(
+            src_ref=src_at(x_ref, a), dst_ref=dst_at(buf, t), send_sem=send.at[k], recv_sem=recv.at[t],
+            device_id=(s, a), device_id_type=MESH,
+        )
+        c.start()
+        copies.append(c)
+    mine = pltpu.make_async_copy(src_at(x_ref, t), dst_at(buf, t), own.at[0])
+    mine.start()
+    mine.wait()
+    for k in range(1, n_tm):
+        j = lax.rem(t + k, n_tm)
+        pltpu.make_async_remote_copy(
+            src_ref=src_at(x_ref, j), dst_ref=dst_at(buf, j), send_sem=send.at[k], recv_sem=recv.at[j],
+            device_id=(s, j), device_id_type=MESH,
+        ).wait_recv()
+    for c in copies:
+        c.wait_send()
+    out_ref[...] = buf[...]
+
+
+def all_to_all(x, out_shape, src_at, dst_at, cid):
+    n_tm = lax.axis_size("tm")
+    return pl.pallas_call(
+        functools.partial(a2a_kernel, n_tm, src_at, dst_at),
+        out_shape=jax.ShapeDtypeStruct(out_shape, x.dtype),
+        in_specs=[pl.BlockSpec(memory_space=pltpu.VMEM)],
+        out_specs=pl.BlockSpec(memory_space=pltpu.VMEM),
+        scratch_shapes=[
+            pltpu.VMEM(out_shape, x.dtype),
+            pltpu.SemaphoreType.DMA((n_tm,)),
+            pltpu.SemaphoreType.DMA((n_tm,)),
+            pltpu.SemaphoreType.DMA((1,)),
+        ],
+        compiler_params=pltpu.CompilerParams(collective_id=cid, has_side_effects=True),
+    )(x)
+
+
+def lanes(a, width):
+    return pl.ds(pl.multiple_of(a * width, width), width)
+
+
 def local(velocity):
     rows = velocity.shape[2]
     span_v = halo_rows(velocity[:, 1], 2).astype(jnp.float32)
@@ -209,15 +261,27 @@
     ) / 12.0
     vorticity = (dv_dx - spanwise(stream_u)).astype(jnp.bfloat16)
     blocks = lax.axis_size("tm")
-    cells = lax.all_to_all(vorticity, "tm", 2, 0, tiled=True)
-    flat = cells.reshape(cells.shape[0], -1)
-    gram = jnp.einsum("ax,bx->ab", flat, flat, preferred_element_type=jnp.float32)
+    cols = vorticity.shape[2]
+    width = cols // blocks
+    cells = all_to_all(
+        vorticity,
+        (blocks,) + vorticity.shape[:2] + (width,),
+        lambda ref, a: ref.at[:, :, lanes(a, width)],
+        lambda ref, j: ref.at[j],
+        1,
+    ).reshape(blocks * RANK, rows, width)
+    gram = jnp.einsum("axz,bxz->ab", cells, cells, preferred_element_type=jnp.float32)
     gram = allreduce(gram)
     basis = tree_basis(gram, blocks)
-    part = jnp.einsum(
-        "ab,ax->bx", basis, flat.astype(jnp.float32), precision=HIGH
-    ).reshape(RANK, rows, -1)
-    modes = lax.all_to_all(part, "tm", 0, 2, tiled=True)
+    part = jnp.einsum("ab,axz->bxz", basis, cells.astype(jnp.float32), precision=HIGH)
+    share = RANK // blocks
+    modes = all_to_all(
+        part,
+        (share, rows, cols),
+        lambda ref, a: ref.at[pl.ds(a * share, share)],
+        lambda ref, j: ref.at[:, :, lanes(j, width)],
+        2,
+    )
     return (vorticity, modes)
 
 

time: 180 us -> 154 us (0.86)
  Pallas kernels: 24.4 us -> 71.7 us
  waiting for transfers between devices: 30.4 us -> 0.01 us
  local copies, waits for them, and re-layouts: 39.9 us -> 20 us
  blocking collectives: 15.4 us -> 0 us
  starting transfers between devices: 11.9 us -> 3.24 us
  other arithmetic: 44.9 us -> 47.5 us
  matrix products: 11.4 us -> 9.58 us
    pallas_call x0 -> x2, Pallas kernels: none -> 43.7 us  [all_to_all(): pl.pallas_call(functools.partial(a2a_kernel, n_tm, src_at, dst_at), out_s...]
    all_to_all x1 -> x0, waiting for transfers between devices: 28.5 us -> none  [local(): cells = lax.all_to_all(vorticity, 'tm', 2, 0, tiled=True)]
    all_to_all x1 -> x0, blocking collectives: 15.4 us -> none  [local(): modes = lax.all_to_all(part, 'tm', 0, 2, tiled=True)]
    unnamed x10 -> x15, local copies, waits for them, and re-layouts: 13.4 us -> 2.35 us
    all_to_all x1 -> x0, starting transfers between devices: 8.48 us -> none  [local(): cells = lax.all_to_all(vorticity, 'tm', 2, 0, tiled=True)]
    all_to_all x2 -> x0, local copies, waits for them, and re-layouts: 6.08 us -> none  [the longest x1 5.36 us: local(): cells = lax.all_to_all(vorticity, 'tm', 2, 0, tiled=True)]
    convert_element_type x1 -> x0, local copies, waits for them, and re-layouts: 5.11 us -> none  [local(): vorticity = (dv_dx - spanwise(stream_u)).astype(jnp.bfloat16)]
    pallas_call x1, Pallas kernels: 24.4 us -> 27.9 us  [allreduce(): pl.pallas_call(functools.partial(allreduce_kernel, n_space, n_tm), out_sh...]
  transfers between devices with their start and end apart: 3 -> 2, of which waited for: 2 -> 0; matrix products, arithmetic and copies ran while one was open for 1% -> 4% of each run, Pallas kernels for 0% -> 0%
where the time goes in v3:
time: 154 us; the launch traced here: 153 us
  Pallas kernels  71.7 us (47%)
  other arithmetic  47.5 us (31%)
  local copies, waits for them, and re-layouts  20 us (13%)
  matrix products  9.58 us (6%)
  starting transfers between devices  3.24 us (2%)
    pallas_call x2, Pallas kernels, all_to_all(): pl.pallas_call(functools.partial(a2a_kernel, n_tm, src_at, dst_at), out_s...  43.7 us
    pallas_call x1, Pallas kernels, allreduce(): pl.pallas_call(functools.partial(allreduce_kernel, n_space, n_tm), out_sh...  27.9 us
    another operation x9, other arithmetic, merge_small(): lower = jnp.linalg.cholesky(inner)  21.5 us
    another operation x7, other arithmetic, merge_small(): lax.linalg.triangular_solve(lower, eye, left_side=True, lower=True)  18 us
    gather x5, local copies, waits for them, and re-layouts, merge_small(): diagonal = jnp.diagonal(gram, axis1=1, axis2=2)  4.08 us
    convert_element_type x1, other arithmetic, local(): vorticity = (dv_dx - spanwise(stream_u)).astype(jnp.bfloat16)  4.07 us
    slice x2, local copies, waits for them, and re-layouts, spanwise(): behind = jnp.roll(field, 1, 2)  3.6 us
  transfers between devices with their start and end apart: 2, of which 0 were waited for; matrix products, arithmetic and copies ran while one was open for 4% of the time, Pallas kernels for 0%

profile of v3, /device:TPU:1, one launch (start us, length us, event | category | flops | bytes accessed | tf_op | source)
XLA Modules:
  0.0 153.0 jit_solution(5338283252814737627)
XLA Ops:
  0.6 1.9 %bitcast_convert_fusion = (f32[32,16,1024]{2,1,0:T(8,128)S(1)}, bf16[32,16,1024]{2,1,0:T(8,128)(2,1)S(1)}) fusion(bf16[32,2,16,1024]{3,2,1,0:T(8,128)(2,1)} %param.1), kind=kLoop, calls=%fused_computation.24 | loop fusion | flops 524288 | bytes 5242880 | tf_op jit(solution)/shard_map/convert_element_type | solution.py:257
  2.5 0.9 fusion.78
  3.4 2.7 %collective-permute-start = (bf16[32,2,1024]{2,1,0:T(2,128)(2,1)}, bf16[32,2,1024]{2,1,0:T(2,128)(2,1)}, u32[]{:S(2)}, u32[]{:S(2)}) collective-permute-start(bf16[32,2,1024]{2,1,0:T(2,128)(2,1)} %get-tuple-element.12), channel_id=1, source_target_pairs={{0,8},{8,16},{16,24},{24,32},{32,40},{40,48},{48,56},{56,64},{64,7... | collective-permute-start | bytes 393224 | tf_op jit(solution)/shard_map/ppermute | solution.py:19
  6.1 0.6 collective-permute-start.1
  6.7 2.2 %fusion.75 = (f32[32,16,1022]{2,1,0:T(8,128)S(1)}, f32[32,16,1022]{2,1,0:T(8,128)}) fusion(f32[32,16,1024]{2,1,0:T(8,128)S(1)} %get-tuple-element.10), kind=kLoop, calls=%fused_computation.123 | loop fusion | bytes 8372224 | tf_op jit(solution)/shard_map/jit(_roll_static)/slice | solution.py:28
  8.9 2.7 %fusion.77 = (f32[32,16,1023]{2,1,0:T(8,128)}, f32[32,16,1023]{2,1,0:T(8,128)}) fusion(f32[32,16,1024]{2,1,0:T(8,128)S(1)} %get-tuple-element.10), kind=kLoop, calls=%fused_computation.125 | loop fusion | bytes 8380416 | tf_op jit(solution)/shard_map/jit(_roll_static)/slice | solution.py:26
  11.6 0.8 fusion.74
  12.4 0.9 fusion.76
  13.4 1.8 %maximum_convert_fusion = f32[32,20,1024]{2,1,0:T(8,128)S(1)} fusion(bf16[32,2,1024]{2,1,0:T(2,128)(2,1)} %collective-permute-done.1, bf16[32,16,1024]{2,1,0:T(8,128)(2,1)S(1)} %get-tuple-element.11, bf16[32,2,1024]{2,1,0:T(2,128)(2,1)} %collective-permute-done), kind=kLoop, calls=%fused_computation.15 | loop fusion | flops 3932160 | bytes 3932160 | tf_op jit(solution)/shard_map/convert_element_type | solution.py:256
  15.2 0.5 copy-done.1
  15.7 4.1 %fusion.3.x_ref = bf16[32,16,1024]{2,1,0:T(8,128)(2,1)} fusion(f32[32,20,1024]{2,1,0:T(8,128)S(1)} %maximum_convert_fusion, f32[32,16,1]{2,1,0:T(8,128)} %get-tuple-element.7, f32[32,16,1023]{2,1,0:T(8,128)} %get-tuple-element.9, f32[32,16,1023]{2,1,0:T(8,128)S(1)} %copy-done.1, f32[32,16,1]{2,1,0:T(8,128)} %get-tuple-element.6, ...), kind=kLoop, calls=%fused_computation.7 | loop fusion | flops 8388608 | bytes 17825792 | tf_op jit(solution)/shard_map/convert_element_type | solution.py:262
  19.8 32.0 %shard_map.30 = bf16[8,32,16,128]{3,2,1,0:T(8,128)(2,1)} custom-call(bf16[32,16,1024]{2,1,0:T(8,128)(2,1)} %fusion.3.x_ref), custom_call_target="tpu_custom_call" | custom-call | tf_op jit(solution)/shard_map/pallas_call | solution.py:235
  51.7 2.7 %convolution_bitcast_fusion.g_ref = f32[32,8,256]{2,1,0:T(8,128)} fusion(bf16[32,8,16,128]{3,2,1,0:T(8,128)(2,1)} %bitcast.121, bf16[256,16,128]{2,1,0:T(8,128)(2,1)} %bitcast.122), kind=kOutput, calls=%fused_computation.16 | convolution fusion | flops 268435456 | bytes 2359296 | tf_op jit(solution)/shard_map/axz,bxz->ab/dot_general | solution.py:273
  54.5 27.9 %shard_map.31 = f32[32,8,256]{2,1,0:T(8,128)} custom-call(f32[32,8,256]{2,1,0:T(8,128)} %convolution_bitcast_fusion.g_ref), custom_call_target="tpu_custom_call" | custom-call | tf_op jit(solution)/shard_map/pallas_call | solution.py:181
  82.4 0.9 fusion.79
  83.7 1.9 %copy.107 = f32[4,64,64]{0,2,1:T(8,128)S(1)} copy(f32[4,64,64]{1,2,0:T(8,128)S(1)} %pad_maximum_fusion) | data formatting | bytes 131072 | tf_op jit(solution)/shard_map/stack | solution.py:52
  85.6 0.2 fusion.73
  85.9 0.9 gather_fusion
  86.9 0.2 fusion.72
  87.3 11.7 %custom-call.21 = f32[4,32,32]{2,1,0:T(8,128)S(1)} custom-call(f32[4,32,32]{2,1,0:T(8,128)S(1)} %fusion.21), custom_call_target="Cholesky" | custom-call | tf_op jit(solution)/shard_map/jit(cholesky)/cholesky | solution.py:38
  99.3 9.8 %custom-call.22 = f32[4,1,32,32]{2,3,1,0:T(8,128)S(1)} custom-call(f32[4,1,32,32]{3,2,1,0:T(8,128)S(1)} %select_bitcast_fusion), custom_call_target="InvertDiagBlocksLowerTriangular" | custom-call | tf_op jit(solution)/shard_map/triangular_solve | solution.py:40
  109.1 0.2 convolution_multiply_fusion
  109.3 0.3 fusion.71
  109.6 0.3 fusion.15
  110.0 0.3 fusion.41
  110.3 1.9 %copy.116 = f32[2,64,64]{0,2,1:T(8,128)S(1)} copy(f32[2,64,64]{1,2,0:T(8,128)S(1)} %fusion.41) | data formatting | bytes 65536 | tf_op jit(solution)/shard_map/nab,nac->nbc/dot_general | solution.py:68
  112.2 0.8 fusion.70
  113.0 1.5 gather_fusion.1
  114.5 0.8 copy.117
  115.4 0.9 fusion.69
  116.5 5.9 %custom-call.23 = f32[2,32,32]{2,1,0:T(8,128)S(1)} custom-call(f32[2,32,32]{2,1,0:T(8,128)S(1)} %fusion.34), custom_call_target="Cholesky" | custom-call | tf_op jit(solution)/shard_map/jit(cholesky)/cholesky | solution.py:38
  122.6 4.9 %custom-call.24 = f32[2,1,32,32]{2,3,1,0:T(8,128)S(1)} custom-call(f32[2,1,32,32]{3,2,1,0:T(8,128)S(1)} %select_bitcast_fusion.1), custom_call_target="InvertDiagBlocksLowerTriangular" | custom-call | tf_op jit(solution)/shard_map/triangular_solve | solution.py:40
  127.5 0.9 convolution_multiply_fusion.1
  128.4 0.2 fusion.68
  128.6 0.2 convolution_bitcast_fusion.2
  128.9 0.4 fusion.25
  129.3 0.2 fusion.23
  129.5 0.8 gather_fusion.2
  130.7 2.9 %custom-call.25 = f32[1,32,32]{2,1,0:T(8,128)S(1)} custom-call(f32[1,32,32]{2,1,0:T(8,128)S(1)} %fusion.38), custom_call_target="Cholesky" | custom-call | tf_op jit(solution)/shard_map/jit(cholesky)/cholesky | solution.py:38
  133.6 0.6 compare_reduce_fusion
  134.3 0.7 fusion.36
  134.9 2.4 %custom-call.26 = f32[1,1,32,32]{2,3,1,0:T(8,128)S(1)} custom-call(f32[1,1,32,32]{3,2,1,0:T(8,128)S(1)} %fusion.36), custom_call_target="InvertDiagBlocksLowerTriangular" | custom-call | tf_op jit(solution)/shard_map/triangular_solve | solution.py:40
  137.5 0.2 fusion.9
  137.8 0.2 convolution_bitcast_fusion.1
  138.0 0.7 fusion.12
  138.7 0.9 copy.122.x_ref
  139.6 11.8 %shard_map.32 = f32[4,16,1024]{2,1,0:T(8,128)} custom-call(f32[32,16,128]{2,1,0:T(8,128)} %copy.122.x_ref), custom_call_target="tpu_custom_call" | custom-call | tf_op jit(solution)/shard_map/pallas_call | solution.py:235
  151.3 1.7 %copy.146 = f32[4,16,1024]{2,1,0:T(8,128)} copy(f32[4,16,1024]{2,1,0:T(8,128)} %shard_map.32) | data formatting | bytes 524288
  (46 shorter events, 2.0 us)
Async XLA Ops:
  3.4 10.0 %collective-permute-start = (bf16[32,2,1024]{2,1,0:T(2,128)(2,1)}, bf16[32,2,1024]{2,1,0:T(2,128)(2,1)}, u32[]{:S(2)}, u32[]{:S(2)}) collective-permute-start(bf16[32,2,1024]{2,1,0:T(2,128)(2,1)} %get-tuple-element.12), channel_id=1, source_target_pairs={{0,8},{8,16},{16,24},{24,32},{32,40},{40,48},{48,56},{56,64},{64,7... | collective-permute-start | bytes 393224 | tf_op jit(solution)/shard_map/ppermute | solution.py:19
  6.1 7.3 %collective-permute-start.1 = (bf16[32,2,1024]{2,1,0:T(2,128)(2,1)}, bf16[32,2,1024]{2,1,0:T(2,128)(2,1)}, u32[]{:S(2)}, u32[]{:S(2)}) collective-permute-start(bf16[32,2,1024]{2,1,0:T(2,128)(2,1)} %get-tuple-element.13), channel_id=1, source_target_pairs={{8,0},{16,8},{24,16},{32,24},{40,32},{48,40},{56,48},{64,56},{72,6... | collective-permute-start | bytes 393224 | tf_op jit(solution)/shard_map/ppermute | solution.py:20
  13.3 95.8 %copy-start.5 = (f32[32,32]{0,1:T(8,128)}, f32[32,32]{0,1:T(8,128)S(1)}, u32[]{:S(2)}) copy-start(f32[32,32]{0,1:T(8,128)S(1)} %copy.103) | copy-start | bytes 12292
  13.3 1.8 %copy-start = (f32[32,16,1022]{2,1,0:T(8,128)S(1)}, f32[32,16,1022]{2,1,0:T(8,128)}, u32[]{:S(2)}) copy-start(f32[32,16,1022]{2,1,0:T(8,128)} %get-tuple-element.5) | copy-start | bytes 6279172
  13.4 2.3 %copy-start.1 = (f32[32,16,1023]{2,1,0:T(8,128)S(1)}, f32[32,16,1023]{2,1,0:T(8,128)}, u32[]{:S(2)}) copy-start(f32[32,16,1023]{2,1,0:T(8,128)} %get-tuple-element.8) | copy-start | bytes 6285316
  13.4 2.3 %copy-start.4 = (f32[32,16,2]{2,1,0:T(8,128)S(1)}, f32[32,16,2]{2,1,0:T(8,128)}, u32[]{:S(2)}) copy-start(f32[32,16,2]{2,1,0:T(8,128)} %get-tuple-element.3) | copy-start | bytes 12292
  82.4 3.5 %copy-start.3 = (f32[32,8,256]{2,1,0:T(8,128)S(1)}, f32[32,8,256]{2,1,0:T(8,128)}, u32[]{:S(2)}) copy-start(f32[32,8,256]{2,1,0:T(8,128)} %shard_map.31) | copy-start | bytes 786436
  110.3 27.7 %copy-start.2 = (bf16[8,32,16,128]{3,2,1,0:T(8,128)(2,1)S(1)}, bf16[8,32,16,128]{3,2,1,0:T(8,128)(2,1)}, u32[]{:S(2)}) copy-start(bf16[8,32,16,128]{3,2,1,0:T(8,128)(2,1)} %shard_map.30) | copy-start | bytes 3145732

commit v4 on v3

--- a/solution.py
+++ b/solution.py
@@ -251,6 +251,80 @@
     return pl.ds(pl.multiple_of(a * width, width), width)
 
 
+def bdot(x, y):
+    return jnp.einsum("nab,nbc->nac", x, y, precision=HIGH, preferred_element_type=jnp.float32)
+
+
+def bdot_t(x, y):
+    return jnp.einsum("nac,nbc->nab", x, y, precision=HIGH, preferred_element_type=jnp.float32)
+
+
+def iotas(shape):
+    return lax.broadcasted_iota(jnp.int32, shape, 1), lax.broadcasted_iota(jnp.int32, shape, 2)
+
+
+def merge_coeffs(h):
+    n = h.shape[0]
+    kt = h[:, :RANK, :] + h[:, RANK:, :]
+    row, col = iotas(h.shape)
+    dcol = jnp.sum(jnp.where(row == col, h, 0.0), axis=2, keepdims=True)
+    scales = jnp.sqrt(dcol[:, :RANK] + dcol[:, RANK:])
+    inner = bdot_t(bdot(kt, h), kt)
+    row, col = iotas(inner.shape)
+    eye = jnp.where(row == col, 1.0, 0.0)
+
+    def step(j, carry):
+        a, r = carry
+        at_row = row == j
+        at_col = col == j
+        a_row = jnp.sum(jnp.where(at_row, a, 0.0), axis=1, keepdims=True)
+        r_row = jnp.sum(jnp.where(at_row, r, 0.0), axis=1, keepdims=True)
+        a_col = jnp.sum(jnp.where(at_col, a, 0.0), axis=2, keepdims=True)
+        pivot = jnp.sum(jnp.where(at_col[:, :1], a_row, 0.0), axis=2, keepdims=True)
+        factor = jnp.where(row[:, :, :1] > j, a_col / pivot, 0.0)
+        return a - factor * a_row, r - factor * r_row
+
+    a, r = lax.fori_loop(0, RANK, step, (inner, eye * jnp.ones((n, 1, 1), jnp.float32)))
+    diag_u = jnp.sum(jnp.where(row == col, a, 0.0), axis=2, keepdims=True)
+    return bdot(r * (scales / jnp.sqrt(diag_u)), kt)
+
+
+def place(x, offset, width):
+    n, _, w = x.shape
+    row, col = iotas((n, w, width))
+    return bdot(x, jnp.where(col == row + offset, 1.0, 0.0))
+
+
+def tree_kernel(h0_ref, g1_ref, g2_ref, out_ref):
+    ct = merge_coeffs(h0_ref[...])
+    basis = ct
+    for g_ref in (g1_ref, g2_ref):
+        n = g_ref.shape[0]
+        w = basis.shape[2]
+        pairs = basis.reshape(n, 2, RANK, w)
+        bt = jnp.concatenate(
+            [place(pairs[:, 0], 0, 2 * w), place(pairs[:, 1], w, 2 * w)], axis=1
+        )
+        h = bdot_t(bdot(bt, g_ref[...]), bt)
+        basis = bdot(merge_coeffs(h), bt)
+    out_ref[...] = basis
+
+
+def tree_pallas(gram, leaves):
+    size = 2 * RANK
+    h0 = jnp.stack([gram[k * size : (k + 1) * size, k * size : (k + 1) * size] for k in range(leaves // 2)])
+    big = 2 * size
+    g1 = jnp.stack([gram[k * big : (k + 1) * big, k * big : (k + 1) * big] for k in range(leaves // 4)])
+    g2 = gram[None]
+    out = pl.pallas_call(
+        tree_kernel,
+        out_shape=jax.ShapeDtypeStruct((1, RANK, leaves * RANK), jnp.float32),
+        in_specs=[pl.BlockSpec(memory_space=pltpu.VMEM)] * 3,
+        out_specs=pl.BlockSpec(memory_space=pltpu.VMEM),
+    )(h0, g1, g2)
+    return out[0]
+
+
 def local(velocity):
     rows = velocity.shape[2]
     span_v = halo_rows(velocity[:, 1], 2).astype(jnp.float32)
@@ -272,8 +346,8 @@
     ).reshape(blocks * RANK, rows, width)
     gram = jnp.einsum("axz,bxz->ab", cells, cells, preferred_element_type=jnp.float32)
     gram = allreduce(gram)
-    basis = tree_basis(gram, blocks)
-    part = jnp.einsum("ab,axz->bxz", basis, cells.astype(jnp.float32), precision=HIGH)
+    basis_t = tree_pallas(gram, blocks)
+    part = jnp.einsum("ba,axz->bxz", basis_t, cells.astype(jnp.float32), precision=HIGH)
     share = RANK // blocks
     modes = all_to_all(
         part,

time: 154 us -> 111 us (0.72)
  other arithmetic: 47.5 us -> 6.86 us
  Pallas kernels: 71.7 us -> 86.8 us
  local copies, waits for them, and re-layouts: 20 us -> 6.29 us
  matrix products: 9.58 us -> 4.22 us
  waiting for transfers between devices: 0.01 us -> 1.94 us
    another operation x17 -> x2, other arithmetic: 39.5 us -> 1.31 us  [the longest x1 0.67 us: tree_pallas(): jnp.stack([gram[k * size:(k + 1) * size, k * size:(k + 1) * size] for k i...]
    pallas_call x0 -> x1, Pallas kernels: none -> 15.5 us  [tree_pallas(): pl.pallas_call(tree_kernel, out_shape=jax.ShapeDtypeStruct((1, RANK, leav...]
    dot_general x16 -> x1, matrix products: 5.52 us -> 1.41 us  [local(): jnp.einsum('ba,axz->bxz', basis_t, cells.astype(jnp.float32), precision=H...]
    gather x5 -> x0, local copies, waits for them, and re-layouts: 4.08 us -> none  [merge_small(): diagonal = jnp.diagonal(gram, axis1=1, axis2=2)]
    slice x2, local copies, waits for them, and re-layouts: 3.6 us -> 0.88 us  [spanwise(): behind = jnp.roll(field, 1, 2)]
    dot_general x5 -> x1, local copies, waits for them, and re-layouts: 2.99 us -> 0.86 us  [local(): jnp.einsum('ba,axz->bxz', basis_t, cells.astype(jnp.float32), precision=H...]
    slice x2, local copies, waits for them, and re-layouts: 2.96 us -> 0.89 us  [spanwise(): behind_two = jnp.roll(field, 2, 2)]
    ppermute x1, waiting for transfers between devices: 0.01 us -> 1.93 us  [halo_rows(): high = lax.ppermute(block[:, :width], 'space', backward)]
  transfers between devices with their start and end apart: 2 -> 2, of which waited for: 0 -> 1; matrix products, arithmetic and copies ran while one was open for 4% -> 2% of each run, Pallas kernels for 0% -> 0%
where the time goes in v4:
time: 111 us; the launch traced here: 110 us
  Pallas kernels  86.8 us (78%)
  other arithmetic  6.86 us (6%)
  local copies, waits for them, and re-layouts  6.29 us (6%)
  matrix products  4.22 us (4%)
  starting transfers between devices  3.41 us (3%)
  waiting for transfers between devices  1.94 us (2%)
    pallas_call x2, Pallas kernels, all_to_all(): pl.pallas_call(functools.partial(a2a_kernel, n_tm, src_at, dst_at), out_s...  44.7 us
    pallas_call x1, Pallas kernels, allreduce(): pl.pallas_call(functools.partial(allreduce_kernel, n_space, n_tm), out_sh...  26.7 us
    pallas_call x1, Pallas kernels, tree_pallas(): pl.pallas_call(tree_kernel, out_shape=jax.ShapeDtypeStruct((1, RANK, leav...  15.5 us
    convert_element_type x1, other arithmetic, local(): vorticity = (dv_dx - spanwise(stream_u)).astype(jnp.bfloat16)  3.02 us
    dot_general x1, matrix products, local(): jnp.einsum('axz,bxz->ab', cells, cells, preferred_element_type=jnp.float32)  2.81 us
    ppermute x1, starting transfers between devices, halo_rows(): low = lax.ppermute(block[:, rows - width:], 'space', forward)  2.76 us
  transfers between devices with their start and end apart: 2, of which 1 were waited for; matrix products, arithmetic and copies ran while one was open for 2% of the time, Pallas kernels for 0%

profile of v4, /device:TPU:1, one launch (start us, length us, event | category | flops | bytes accessed | tf_op | source)
XLA Modules:
  0.0 110.3 jit_solution(11854744419524939110)
XLA Ops:
  0.6 1.9 %bitcast_convert_fusion = (f32[32,16,1024]{2,1,0:T(8,128)S(1)}, bf16[32,16,1024]{2,1,0:T(8,128)(2,1)S(1)}) fusion(bf16[32,2,16,1024]{3,2,1,0:T(8,128)(2,1)} %param.1), kind=kLoop, calls=%fused_computation.14 | loop fusion | flops 524288 | bytes 5242880 | tf_op jit(solution)/shard_map/convert_element_type | solution.py:331
  2.5 0.2 fusion.18
  2.7 2.8 %collective-permute-start = (bf16[32,2,1024]{2,1,0:T(2,128)(2,1)S(1)}, bf16[32,2,1024]{2,1,0:T(2,128)(2,1)S(1)}, u32[]{:S(2)}, u32[]{:S(2)}) collective-permute-start(bf16[32,2,1024]{2,1,0:T(2,128)(2,1)S(1)} %get-tuple-element.12), channel_id=1, source_target_pairs={{0,8},{8,16},{16,24},{24,32},{32,40},{40,48},{48,56},{56,64},{64,7... | collective-permute-start | bytes 393224 | tf_op jit(solution)/shard_map/ppermute | solution.py:19
  5.5 0.6 collective-permute-start.1
  6.1 0.1 fusion.16
  6.3 0.7 fusion.17
  7.0 0.7 fusion.15
  7.8 0.1 fusion.14
  7.9 0.0 collective-permute-done
  7.9 1.9 %collective-permute-done.1 = bf16[32,2,1024]{2,1,0:T(2,128)(2,1)S(1)} collective-permute-done((bf16[32,2,1024]{2,1,0:T(2,128)(2,1)S(1)}, bf16[32,2,1024]{2,1,0:T(2,128)(2,1)S(1)}, u32[]{:S(2)}, u32[]{:S(2)}) %collective-permute-start.1) | collective-permute-done | bytes 131104 | tf_op jit(solution)/shard_map/ppermute | solution.py:20
  9.9 0.7 maximum_convert_fusion
  10.5 3.0 %fusion.3.x_ref = bf16[32,16,1024]{2,1,0:T(8,128)(2,1)} fusion(f32[32,20,1024]{2,1,0:T(8,128)S(1)} %maximum_convert_fusion, f32[32,16,1]{2,1,0:T(8,128)S(1)} %get-tuple-element.7, f32[32,16,1023]{2,1,0:T(8,128)S(1)} %get-tuple-element.9, f32[32,16,1023]{2,1,0:T(8,128)S(1)} %get-tuple-element.8, f32[32,16,1]{2,1,0:T(8,128)S(1)} %get-tuple-element.6, ...), kind=kLoop, calls=%fused_computation.4 | loop fusion | flops 8388608 | bytes 17825792 | tf_op jit(solution)/shard_map/convert_element_type | solution.py:336
  13.6 33.0 %shard_map.30 = bf16[8,32,16,128]{3,2,1,0:T(8,128)(2,1)} custom-call(bf16[32,16,1024]{2,1,0:T(8,128)(2,1)} %fusion.3.x_ref), custom_call_target="tpu_custom_call" | custom-call | tf_op jit(solution)/shard_map/pallas_call | solution.py:235
  46.5 0.0 copy-start
  46.5 2.8 %convolution_bitcast_fusion.g_ref = f32[32,8,256]{2,1,0:T(8,128)} fusion(bf16[32,8,16,128]{3,2,1,0:T(8,128)(2,1)} %bitcast.36, bf16[256,16,128]{2,1,0:T(8,128)(2,1)} %bitcast.35), kind=kOutput, calls=%fused_computation.13 | convolution fusion | flops 268435456 | bytes 2359296 | tf_op jit(solution)/shard_map/axz,bxz->ab/dot_general | solution.py:347
  49.4 26.7 %shard_map.31 = f32[32,8,256]{2,1,0:T(8,128)} custom-call(f32[32,8,256]{2,1,0:T(8,128)} %convolution_bitcast_fusion.g_ref), custom_call_target="tpu_custom_call" | custom-call | tf_op jit(solution)/shard_map/pallas_call | solution.py:181
  76.0 0.9 slice_bitcast_fusion.6
  76.9 0.9 slice_bitcast_fusion.2
  77.8 0.6 pad_maximum_fusion.1.g1_ref
  78.5 0.7 pad_maximum_fusion.h0_ref
  79.1 15.5 %shard_map.32 = f32[1,32,256]{2,1,0:T(8,128)} custom-call(f32[4,64,64]{2,1,0:T(8,128)} %pad_maximum_fusion.h0_ref, f32[2,128,128]{2,1,0:T(8,128)} %pad_maximum_fusion.1.g1_ref, f32[1,256,256]{2,1,0:T(8,128)} %bitcast.40), custom_call_target="tpu_custom_call" | custom-call | tf_op jit(solution)/shard_map/pallas_call | solution.py:319
  94.6 0.0 copy-done
  94.6 1.4 %fusion.10 = f32[32,16,128]{2,0,1:T(8,128)S(1)} fusion(bf16[256,16,128]{2,1,0:T(8,128)(2,1)S(1)} %bitcast.37, f32[1,32,256]{2,1,0:T(8,128)} %shard_map.32), kind=kOutput, calls=%fused_computation.18 | convolution fusion | flops 201326592 | bytes 1343488 | tf_op jit(solution)/shard_map/ba,axz->bxz/dot_general | solution.py:350
  96.0 0.9 copy.8.x_ref
  96.9 11.7 %shard_map.33 = f32[4,16,1024]{2,1,0:T(8,128)} custom-call(f32[32,16,128]{2,1,0:T(8,128)} %copy.8.x_ref), custom_call_target="tpu_custom_call" | custom-call | tf_op jit(solution)/shard_map/pallas_call | solution.py:235
  108.6 1.7 %copy.21 = f32[4,16,1024]{2,1,0:T(8,128)} copy(f32[4,16,1024]{2,1,0:T(8,128)} %shard_map.33) | data formatting | bytes 524288
Async XLA Ops:
  2.7 5.2 %collective-permute-start = (bf16[32,2,1024]{2,1,0:T(2,128)(2,1)S(1)}, bf16[32,2,1024]{2,1,0:T(2,128)(2,1)S(1)}, u32[]{:S(2)}, u32[]{:S(2)}) collective-permute-start(bf16[32,2,1024]{2,1,0:T(2,128)(2,1)S(1)} %get-tuple-element.12), channel_id=1, source_target_pairs={{0,8},{8,16},{16,24},{24,32},{32,40},{40,48},{48,56},{56,64},{64,7... | collective-permute-start | bytes 393224 | tf_op jit(solution)/shard_map/ppermute | solution.py:19
  5.5 4.4 %collective-permute-start.1 = (bf16[32,2,1024]{2,1,0:T(2,128)(2,1)S(1)}, bf16[32,2,1024]{2,1,0:T(2,128)(2,1)S(1)}, u32[]{:S(2)}, u32[]{:S(2)}) collective-permute-start(bf16[32,2,1024]{2,1,0:T(2,128)(2,1)S(1)} %get-tuple-element.13), channel_id=1, source_target_pairs={{8,0},{16,8},{24,16},{32,24},{40,32},{48,40},{56,48},{64,56},{72,6... | collective-permute-start | bytes 393224 | tf_op jit(solution)/shard_map/ppermute | solution.py:20
  46.5 48.0 %copy-start = (bf16[8,32,16,128]{3,2,1,0:T(8,128)(2,1)S(1)}, bf16[8,32,16,128]{3,2,1,0:T(8,128)(2,1)}, u32[]{:S(2)}) copy-start(bf16[8,32,16,128]{3,2,1,0:T(8,128)(2,1)} %shard_map.30) | copy-start | bytes 3145732

commit v5 on v4

--- a/solution.py
+++ b/solution.py
@@ -27,52 +27,6 @@
     ahead_two = jnp.roll(field, -2, 2)
     behind_two = jnp.roll(field, 2, 2)
     return (8.0 * (ahead - behind) - (ahead_two - behind_two)) / 12.0
-
-
-def merge_small(gram):
-    coeffs = gram[:, :, :RANK] + gram[:, :, RANK:]
-    diagonal = jnp.diagonal(gram, axis1=1, axis2=2)
-    scales = jnp.sqrt(diagonal[:, :RANK] + diagonal[:, RANK:])
-    half = jnp.einsum("nab,nbc->nac", gram, coeffs, precision=HIGH)
-    inner = jnp.einsum("nab,nac->nbc", coeffs, half, precision=HIGH)
-    lower = jnp.linalg.cholesky(inner)
-    eye = jnp.broadcast_to(jnp.eye(RANK, dtype=jnp.float32), inner.shape)
-    lower_inv = lax.linalg.triangular_solve(lower, eye, left_side=True, lower=True)
-    factor = jnp.swapaxes(lower_inv, 1, 2) * scales[:, None, :]
-    return jnp.einsum("nab,nbc->nac", coeffs, factor, precision=HIGH)
-
-
-def tree_basis(gram, leaves):
-    width = leaves * RANK
-    basis = None
-    span = 1
-    while span < leaves:
-        nodes = leaves // (2 * span)
-        size = 2 * span * RANK
-        sub = jnp.stack(
-            [gram[k * size : (k + 1) * size, k * size : (k + 1) * size] for k in range(nodes)]
-        )
-        if basis is None:
-            h = sub
-        else:
-            b = basis.reshape(nodes, 2, span * RANK, RANK)
-            zero = jnp.zeros_like(b[:, 0])
-            bd = jnp.concatenate(
-                [
-                    jnp.concatenate([b[:, 0], zero], axis=2),
-                    jnp.concatenate([zero, b[:, 1]], axis=2),
-                ],
-                axis=1,
-            )
-            gb = jnp.einsum("nab,nbc->nac", sub, bd, precision=HIGH)
-            h = jnp.einsum("nab,nac->nbc", bd, gb, precision=HIGH)
-        c = merge_small(h)
-        if basis is None:
-            basis = c
-        else:
-            basis = jnp.einsum("nab,nbc->nac", bd, c, precision=HIGH)
-        span *= 2
-    return basis.reshape(width, RANK)
 
 
 MESH = pl.DeviceIdType.MESH
@@ -295,34 +249,90 @@
     return bdot(x, jnp.where(col == row + offset, 1.0, 0.0))
 
 
-def tree_kernel(h0_ref, g1_ref, g2_ref, out_ref):
-    ct = merge_coeffs(h0_ref[...])
-    basis = ct
-    for g_ref in (g1_ref, g2_ref):
-        n = g_ref.shape[0]
+def tree_levels(g_ref):
+    size = 2 * RANK
+    leaves = g_ref.shape[0] // RANK
+    picks = []
+    for k in range(leaves // 2):
+        lane0 = (k * size) // 128 * 128
+        block = g_ref[k * size : (k + 1) * size, lane0 : lane0 + 128][None]
+        picks.append(place(block, -(k * size - lane0), size))
+    basis = merge_coeffs(jnp.concatenate(picks, axis=0))
+    while basis.shape[0] > 1:
+        n = basis.shape[0] // 2
         w = basis.shape[2]
         pairs = basis.reshape(n, 2, RANK, w)
         bt = jnp.concatenate(
             [place(pairs[:, 0], 0, 2 * w), place(pairs[:, 1], w, 2 * w)], axis=1
         )
-        h = bdot_t(bdot(bt, g_ref[...]), bt)
+        gs = jnp.concatenate(
+            [g_ref[k * 2 * w : (k + 1) * 2 * w, k * 2 * w : (k + 1) * 2 * w][None] for k in range(n)],
+            axis=0,
+        )
+        h = bdot_t(bdot(bt, gs), bt)
         basis = bdot(merge_coeffs(h), bt)
-    out_ref[...] = basis
-
-
-def tree_pallas(gram, leaves):
-    size = 2 * RANK
-    h0 = jnp.stack([gram[k * size : (k + 1) * size, k * size : (k + 1) * size] for k in range(leaves // 2)])
-    big = 2 * size
-    g1 = jnp.stack([gram[k * big : (k + 1) * big, k * big : (k + 1) * big] for k in range(leaves // 4)])
-    g2 = gram[None]
-    out = pl.pallas_call(
-        tree_kernel,
-        out_shape=jax.ShapeDtypeStruct((1, RANK, leaves * RANK), jnp.float32),
-        in_specs=[pl.BlockSpec(memory_space=pltpu.VMEM)] * 3,
+    return basis[0]
+
+
+def finish_kernel(n_tm, g_ref, w_ref, out_ref, part_ref, buf, send, recv, own):
+    s = lax.axis_index("space")
+    t = lax.axis_index("tm")
+    barrier = pltpu.get_barrier_semaphore()
+    for k in range(1, n_tm):
+        a = lax.rem(t + k, n_tm)
+        pl.semaphore_signal(barrier, inc=1, device_id=(s, a), device_id_type=MESH)
+    basis_t = tree_levels(g_ref)
+    for x in range(w_ref.shape[0]):
+        part_ref[x] = jnp.dot(
+            basis_t, w_ref[x].astype(jnp.float32), precision=HIGH, preferred_element_type=jnp.float32
+        )
+    share = part_ref.shape[1] // n_tm
+    width = w_ref.shape[2]
+    src_at = lambda a: part_ref.at[:, pl.ds(a * share, share), :]
+    dst_at = lambda j: buf.at[:, :, lanes(j, width)]
+    pl.semaphore_wait(barrier, n_tm - 1)
+    copies = []
+    for k in range(1, n_tm):
+        a = lax.rem(t + k, n_tm)
+        c = pltpu.make_async_remote_copy(
+            src_ref=src_at(a), dst_ref=dst_at(t), send_sem=send.at[k], recv_sem=recv.at[t],
+            device_id=(s, a), device_id_type=MESH,
+        )
+        c.start()
+        copies.append(c)
+    mine = pltpu.make_async_copy(src_at(t), dst_at(t), own.at[0])
+    mine.start()
+    mine.wait()
+    for k in range(1, n_tm):
+        j = lax.rem(t + k, n_tm)
+        pltpu.make_async_remote_copy(
+            src_ref=src_at(j), dst_ref=dst_at(j), send_sem=send.at[k], recv_sem=recv.at[j],
+            device_id=(s, j), device_id_type=MESH,
+        ).wait_recv()
+    for c in copies:
+        c.wait_send()
+    out_ref[...] = buf[...]
+
+
+def finish(gram, cells_x):
+    n_tm = lax.axis_size("tm")
+    rows, _, width = cells_x.shape
+    share = RANK // n_tm
+    out_shape = (rows, share, width * n_tm)
+    return pl.pallas_call(
+        functools.partial(finish_kernel, n_tm),
+        out_shape=jax.ShapeDtypeStruct(out_shape, jnp.float32),
+        in_specs=[pl.BlockSpec(memory_space=pltpu.VMEM)] * 2,
         out_specs=pl.BlockSpec(memory_space=pltpu.VMEM),
-    )(h0, g1, g2)
-    return out[0]
+        scratch_shapes=[
+            pltpu.VMEM((rows, RANK, width), jnp.float32),
+            pltpu.VMEM(out_shape, jnp.float32),
+            pltpu.SemaphoreType.DMA((n_tm,)),
+            pltpu.SemaphoreType.DMA((n_tm,)),
+            pltpu.SemaphoreType.DMA((1,)),
+        ],
+        compiler_params=pltpu.CompilerParams(collective_id=2, has_side_effects=True),
+    )(gram, cells_x)
 
 
 def local(velocity):
@@ -337,25 +347,17 @@
     blocks = lax.axis_size("tm")
     cols = vorticity.shape[2]
     width = cols // blocks
-    cells = all_to_all(
-        vorticity,
-        (blocks,) + vorticity.shape[:2] + (width,),
+    vort_x = jnp.swapaxes(vorticity, 0, 1)
+    cells_x = all_to_all(
+        vort_x,
+        (rows, blocks * RANK, width),
         lambda ref, a: ref.at[:, :, lanes(a, width)],
-        lambda ref, j: ref.at[j],
+        lambda ref, j: ref.at[:, pl.ds(j * RANK, RANK), :],
         1,
-    ).reshape(blocks * RANK, rows, width)
-    gram = jnp.einsum("axz,bxz->ab", cells, cells, preferred_element_type=jnp.float32)
+    )
+    gram = jnp.einsum("xaz,xbz->ab", cells_x, cells_x, preferred_element_type=jnp.float32)
     gram = allreduce(gram)
-    basis_t = tree_pallas(gram, blocks)
-    part = jnp.einsum("ba,axz->bxz", basis_t, cells.astype(jnp.float32), precision=HIGH)
-    share = RANK // blocks
-    modes = all_to_all(
-        part,
-        (share, rows, cols),
-        lambda ref, a: ref.at[pl.ds(a * share, share)],
-        lambda ref, j: ref.at[:, :, lanes(j, width)],
-        2,
-    )
+    modes = jnp.swapaxes(finish(gram, cells_x), 0, 1)
     return (vorticity, modes)
 
 

time: 111 us -> 104 us (0.937)
  other arithmetic: 6.86 us -> 3.77 us
  Pallas kernels: 86.8 us -> 84.7 us
  matrix products: 4.22 us -> 2.71 us
    pallas_call x2 -> x1, Pallas kernels: 44.7 us -> 33 us  [all_to_all(): pl.pallas_call(functools.partial(a2a_kernel, n_tm, src_at, dst_at), out_s...]
    pallas_call x1, Pallas kernels: 15.5 us -> 25.1 us  [finish(): pl.pallas_call(functools.partial(finish_kernel, n_tm), out_shape=jax.Shap...]
    another operation x2 -> x0, local copies, waits for them, and re-layouts: 1.77 us -> none  [the longest x1 0.89 us: tree_pallas(): jnp.stack([gram[k * size:(k + 1) * size, k * size:(k + 1) * size] for k i...]
    slice x0 -> x1, local copies, waits for them, and re-layouts: none -> 1.72 us  [local(): stream_u = velocity[:, 0].astype(jnp.float32)]
    unnamed x3 -> x4, local copies, waits for them, and re-layouts: 1.68 us -> 3.36 us
    dot_general x2 -> x1, matrix products: 4.22 us -> 2.71 us  [local(): jnp.einsum('xaz,xbz->ab', cells_x, cells_x, preferred_element_type=jnp.fl...]
    another operation x2 -> x0, other arithmetic: 1.31 us -> none  [the longest x1 0.67 us: tree_pallas(): jnp.stack([gram[k * size:(k + 1) * size, k * size:(k + 1) * size] for k i...]
where the time goes in v5:
time: 104 us
  Pallas kernels  84.7 us (81%)
  local copies, waits for them, and re-layouts  6.9 us (7%)
  other arithmetic  3.77 us (4%)
  starting transfers between devices  3.41 us (3%)
  matrix products  2.71 us (3%)
  waiting for transfers between devices  1.92 us (2%)
    pallas_call x1, Pallas kernels, all_to_all(): pl.pallas_call(functools.partial(a2a_kernel, n_tm, src_at, dst_at), out_s...  33 us
    pallas_call x1, Pallas kernels, allreduce(): pl.pallas_call(functools.partial(allreduce_kernel, n_space, n_tm), out_sh...  26.7 us
    pallas_call x1, Pallas kernels, finish(): pl.pallas_call(functools.partial(finish_kernel, n_tm), out_shape=jax.Shap...  25.1 us
    unnamed x4, local copies, waits for them, and re-layouts  3.36 us
    ppermute x1, starting transfers between devices, halo_rows(): low = lax.ppermute(block[:, rows - width:], 'space', forward)  2.76 us
    dot_general x1, matrix products, local(): jnp.einsum('xaz,xbz->ab', cells_x, cells_x, preferred_element_type=jnp.fl...  2.71 us
    convert_element_type x1, other arithmetic, local(): vorticity = (dv_dx - spanwise(stream_u)).astype(jnp.bfloat16)  2.38 us
  transfers between devices with their start and end apart: 2, of which 1 were waited for; matrix products, arithmetic and copies ran while one was open for 2% of the time, Pallas kernels for 0%

profile of v5, /device:TPU:1, one launch (start us, length us, event | category | flops | bytes accessed | tf_op | source)
XLA Modules:
  0.0 104.2 jit_solution(13204831675902535068)
XLA Ops:
  0.6 1.7 %fusion.13 = (bf16[32,1,16,1024]{3,2,1,0:T(8,128)(2,1)S(1)}, bf16[32,1,16,1024]{3,2,1,0:T(8,128)(2,1)S(1)}) fusion(bf16[32,2,16,1024]{3,2,1,0:T(8,128)(2,1)} %param.1), kind=kLoop, calls=%fused_computation.21 | loop fusion | bytes 4194304 | tf_op jit(solution)/shard_map/slice | solution.py:341
  2.4 1.2 %fusion.8 = (f32[32,16,1024]{2,0,1:T(8,128)S(1)}, bf16[32,16,1024]{2,0,1:T(8,128)(2,1)S(1)}) fusion(bf16[32,1,16,1024]{3,2,1,0:T(8,128)(2,1)S(1)} %get-tuple-element.12, bf16[32,1,16,1024]{3,2,1,0:T(8,128)(2,1)S(1)} %get-tuple-element.13), kind=kLoop, calls=%fused_computation.15 | loop fusion | flops 524288 | bytes 5242880 | tf_op jit(solution)/shard_map/convert_element_type | solution.py:341
  3.6 2.8 %collective-permute-start = (bf16[32,2,1024]{2,0,1:T(8,128)(2,1)S(1)}, bf16[32,2,1024]{2,0,1:T(8,128)(2,1)S(1)}, u32[]{:S(2)}, u32[]{:S(2)}) collective-permute-start(bf16[32,2,1024]{2,0,1:T(8,128)(2,1)S(1)} %get-tuple-element.14), channel_id=1, source_target_pairs={{0,8},{8,16},{16,24},{24,32},{32,40},{40,48},{48,56},{56,64},{64,7... | collective-permute-start | bytes 393224 | tf_op jit(solution)/shard_map/ppermute | solution.py:19
  6.3 0.6 collective-permute-start.1
  7.0 0.1 fusion.11
  7.1 0.8 fusion.12
  7.9 0.8 fusion.10
  8.7 0.1 fusion.9
  8.8 0.0 collective-permute-done
  8.8 1.9 %collective-permute-done.1 = bf16[32,2,1024]{2,0,1:T(8,128)(2,1)S(1)} collective-permute-done((bf16[32,2,1024]{2,0,1:T(8,128)(2,1)S(1)}, bf16[32,2,1024]{2,0,1:T(8,128)(2,1)S(1)}, u32[]{:S(2)}, u32[]{:S(2)}) %collective-permute-start.1) | collective-permute-done | bytes 131104 | tf_op jit(solution)/shard_map/ppermute | solution.py:20
  10.7 0.2 maximum_convert_fusion
  10.9 2.4 %fusion.3 = bf16[32,16,1024]{2,0,1:T(8,128)(2,1)S(1)} fusion(f32[32,20,1024]{2,0,1:T(8,128)S(1)} %maximum_convert_fusion, f32[32,16,1]{2,0,1:T(8,128)S(1)} %get-tuple-element.9, f32[32,16,1023]{2,0,1:T(8,128)S(1)} %get-tuple-element.11, f32[32,16,1023]{2,0,1:T(8,128)S(1)} %get-tuple-element.10, f32[32,16,1]{2,0,1:T(8,128)S(1)} %get-tuple-element.8, ...), kind=kLoop, calls=%fused_computation.4 | loop fusion | flops 8388608 | bytes 17825792 | tf_op jit(solution)/shard_map/convert_element_type | solution.py:346
  13.3 0.0 copy-start
  13.3 1.5 %copy.5 = bf16[32,16,1024]{2,1,0:T(8,128)(2,1)} copy(bf16[32,16,1024]{2,0,1:T(8,128)(2,1)S(1)} %fusion.3) | data formatting | bytes 2097152
  14.9 0.0 copy-done
  14.9 33.0 %shard_map.30.w_ref = bf16[16,256,128]{2,1,0:T(8,128)(2,1)} custom-call(bf16[16,32,1024]{2,1,0:T(8,128)(2,1)} %bitcast.16), custom_call_target="tpu_custom_call" | custom-call | tf_op jit(solution)/shard_map/pallas_call | solution.py:189
  47.9 2.7 %convolution_bitcast_fusion.g_ref = f32[32,8,256]{2,1,0:T(8,128)} fusion(bf16[16,256,128]{2,1,0:T(8,128)(2,1)} %shard_map.30.w_ref), kind=kOutput, calls=%fused_computation.13 | convolution fusion | flops 268435456 | bytes 1310720 | tf_op jit(solution)/shard_map/xaz,xbz->ab/dot_general | solution.py:358
  50.6 26.7 %shard_map.31 = f32[32,8,256]{2,1,0:T(8,128)} custom-call(f32[32,8,256]{2,1,0:T(8,128)} %convolution_bitcast_fusion.g_ref), custom_call_target="tpu_custom_call" | custom-call | tf_op jit(solution)/shard_map/pallas_call | solution.py:135
  77.2 25.1 %shard_map.32 = f32[16,4,1024]{2,1,0:T(4,128)} custom-call(f32[256,256]{1,0:T(8,128)} %bitcast.17, bf16[16,256,128]{2,1,0:T(8,128)(2,1)} %shard_map.30.w_ref), custom_call_target="tpu_custom_call" | custom-call | tf_op jit(solution)/shard_map/pallas_call | solution.py:322
  102.3 1.8 %copy.6 = f32[4,16,1024]{2,1,0:T(8,128)} copy(f32[4,16,1024]{2,0,1:T(4,128)} %bitcast.18) | data formatting | bytes 524288
  (1 shorter events, 0.0 us)
Async XLA Ops:
  3.6 5.2 %collective-permute-start = (bf16[32,2,1024]{2,0,1:T(8,128)(2,1)S(1)}, bf16[32,2,1024]{2,0,1:T(8,128)(2,1)S(1)}, u32[]{:S(2)}, u32[]{:S(2)}) collective-permute-start(bf16[32,2,1024]{2,0,1:T(8,128)(2,1)S(1)} %get-tuple-element.14), channel_id=1, source_target_pairs={{0,8},{8,16},{16,24},{24,32},{32,40},{40,48},{48,56},{56,64},{64,7... | collective-permute-start | bytes 393224 | tf_op jit(solution)/shard_map/ppermute | solution.py:19
  6.3 4.4 %collective-permute-start.1 = (bf16[32,2,1024]{2,0,1:T(8,128)(2,1)S(1)}, bf16[32,2,1024]{2,0,1:T(8,128)(2,1)S(1)}, u32[]{:S(2)}, u32[]{:S(2)}) collective-permute-start(bf16[32,2,1024]{2,0,1:T(8,128)(2,1)S(1)} %get-tuple-element.15), channel_id=1, source_target_pairs={{8,0},{16,8},{24,16},{32,24},{40,32},{48,40},{56,48},{64,56},{72,6... | collective-permute-start | bytes 393224 | tf_op jit(solution)/shard_map/ppermute | solution.py:20
  13.3 1.6 %copy-start = (bf16[32,16,1024]{2,0,1:T(8,128)(2,1)}, bf16[32,16,1024]{2,0,1:T(8,128)(2,1)S(1)}, u32[]{:S(2)}) copy-start(bf16[32,16,1024]{2,0,1:T(8,128)(2,1)S(1)} %fusion.3) | copy-start | bytes 3145732

commit v6 on v5

--- a/solution.py
+++ b/solution.py
@@ -238,7 +238,7 @@
         factor = jnp.where(row[:, :, :1] > j, a_col / pivot, 0.0)
         return a - factor * a_row, r - factor * r_row
 
-    a, r = lax.fori_loop(0, RANK, step, (inner, eye * jnp.ones((n, 1, 1), jnp.float32)))
+    a, r = lax.fori_loop(0, RANK, step, (inner, eye * jnp.ones((n, 1, 1), jnp.float32)), unroll=True)
     diag_u = jnp.sum(jnp.where(row == col, a, 0.0), axis=2, keepdims=True)
     return bdot(r * (scales / jnp.sqrt(diag_u)), kt)
 

time: 104 us -> 103 us (level)
  no operation moved by 1% of the time
where the time goes in v6:
time: 103 us
  Pallas kernels  83.7 us (81%)
  local copies, waits for them, and re-layouts  6.9 us (7%)
  other arithmetic  3.77 us (4%)
  starting transfers between devices  3.59 us (3%)
  matrix products  2.72 us (3%)
  waiting for transfers between devices  1.74 us (2%)
    pallas_call x1, Pallas kernels, all_to_all(): pl.pallas_call(functools.partial(a2a_kernel, n_tm, src_at, dst_at), out_s...  33 us
    pallas_call x1, Pallas kernels, allreduce(): pl.pallas_call(functools.partial(allreduce_kernel, n_space, n_tm), out_sh...  26.7 us
    pallas_call x1, Pallas kernels, finish(): pl.pallas_call(functools.partial(finish_kernel, n_tm), out_shape=jax.Shap...  24.1 us
    unnamed x4, local copies, waits for them, and re-layouts  3.36 us
    ppermute x1, starting transfers between devices, halo_rows(): low = lax.ppermute(block[:, rows - width:], 'space', forward)  2.76 us
    dot_general x1, matrix products, local(): jnp.einsum('xaz,xbz->ab', cells_x, cells_x, preferred_element_type=jnp.fl...  2.72 us
    convert_element_type x1, other arithmetic, local(): vorticity = (dv_dx - spanwise(stream_u)).astype(jnp.bfloat16)  2.38 us
  transfers between devices with their start and end apart: 2, of which 1 were waited for; matrix products, arithmetic and copies ran while one was open for 2% of the time, Pallas kernels for 0%

profile of v6, /device:TPU:1, one launch (start us, length us, event | category | flops | bytes accessed | tf_op | source)
XLA Modules:
  0.0 103.2 jit_solution(8529864564396557351)
XLA Ops:
  0.6 1.7 %fusion.13 = (bf16[32,1,16,1024]{3,2,1,0:T(8,128)(2,1)S(1)}, bf16[32,1,16,1024]{3,2,1,0:T(8,128)(2,1)S(1)}) fusion(bf16[32,2,16,1024]{3,2,1,0:T(8,128)(2,1)} %param.1), kind=kLoop, calls=%fused_computation.21 | loop fusion | bytes 4194304 | tf_op jit(solution)/shard_map/slice | solution.py:341
  2.4 1.2 %fusion.8 = (f32[32,16,1024]{2,0,1:T(8,128)S(1)}, bf16[32,16,1024]{2,0,1:T(8,128)(2,1)S(1)}) fusion(bf16[32,1,16,1024]{3,2,1,0:T(8,128)(2,1)S(1)} %get-tuple-element.12, bf16[32,1,16,1024]{3,2,1,0:T(8,128)(2,1)S(1)} %get-tuple-element.13), kind=kLoop, calls=%fused_computation.15 | loop fusion | flops 524288 | bytes 5242880 | tf_op jit(solution)/shard_map/convert_element_type | solution.py:341
  3.6 2.8 %collective-permute-start = (bf16[32,2,1024]{2,0,1:T(8,128)(2,1)S(1)}, bf16[32,2,1024]{2,0,1:T(8,128)(2,1)S(1)}, u32[]{:S(2)}, u32[]{:S(2)}) collective-permute-start(bf16[32,2,1024]{2,0,1:T(8,128)(2,1)S(1)} %get-tuple-element.14), channel_id=1, source_target_pairs={{0,8},{8,16},{16,24},{24,32},{32,40},{40,48},{48,56},{56,64},{64,7... | collective-permute-start | bytes 393224 | tf_op jit(solution)/shard_map/ppermute | solution.py:19
  6.3 0.8 collective-permute-start.1
  7.2 0.1 fusion.11
  7.3 0.8 fusion.12
  8.1 0.8 fusion.10
  8.8 0.1 fusion.9
  9.0 0.0 collective-permute-done
  9.0 1.7 %collective-permute-done.1 = bf16[32,2,1024]{2,0,1:T(8,128)(2,1)S(1)} collective-permute-done((bf16[32,2,1024]{2,0,1:T(8,128)(2,1)S(1)}, bf16[32,2,1024]{2,0,1:T(8,128)(2,1)S(1)}, u32[]{:S(2)}, u32[]{:S(2)}) %collective-permute-start.1) | collective-permute-done | bytes 131104 | tf_op jit(solution)/shard_map/ppermute | solution.py:20
  10.7 0.2 maximum_convert_fusion
  10.9 2.4 %fusion.3 = bf16[32,16,1024]{2,0,1:T(8,128)(2,1)S(1)} fusion(f32[32,20,1024]{2,0,1:T(8,128)S(1)} %maximum_convert_fusion, f32[32,16,1]{2,0,1:T(8,128)S(1)} %get-tuple-element.9, f32[32,16,1023]{2,0,1:T(8,128)S(1)} %get-tuple-element.11, f32[32,16,1023]{2,0,1:T(8,128)S(1)} %get-tuple-element.10, f32[32,16,1]{2,0,1:T(8,128)S(1)} %get-tuple-element.8, ...), kind=kLoop, calls=%fused_computation.4 | loop fusion | flops 8388608 | bytes 17825792 | tf_op jit(solution)/shard_map/convert_element_type | solution.py:346
  13.3 0.0 copy-start
  13.3 1.5 %copy.5 = bf16[32,16,1024]{2,1,0:T(8,128)(2,1)} copy(bf16[32,16,1024]{2,0,1:T(8,128)(2,1)S(1)} %fusion.3) | data formatting | bytes 2097152
  14.9 0.0 copy-done
  14.9 33.0 %shard_map.30.w_ref = bf16[16,256,128]{2,1,0:T(8,128)(2,1)} custom-call(bf16[16,32,1024]{2,1,0:T(8,128)(2,1)} %bitcast.16), custom_call_target="tpu_custom_call" | custom-call | tf_op jit(solution)/shard_map/pallas_call | solution.py:189
  47.9 2.7 %convolution_bitcast_fusion.g_ref = f32[32,8,256]{2,1,0:T(8,128)} fusion(bf16[16,256,128]{2,1,0:T(8,128)(2,1)} %shard_map.30.w_ref), kind=kOutput, calls=%fused_computation.13 | convolution fusion | flops 268435456 | bytes 1310720 | tf_op jit(solution)/shard_map/xaz,xbz->ab/dot_general | solution.py:358
  50.6 26.7 %shard_map.31 = f32[32,8,256]{2,1,0:T(8,128)} custom-call(f32[32,8,256]{2,1,0:T(8,128)} %convolution_bitcast_fusion.g_ref), custom_call_target="tpu_custom_call" | custom-call | tf_op jit(solution)/shard_map/pallas_call | solution.py:135
  77.2 24.1 %shard_map.32 = f32[16,4,1024]{2,1,0:T(4,128)} custom-call(f32[256,256]{1,0:T(8,128)} %bitcast.17, bf16[16,256,128]{2,1,0:T(8,128)(2,1)} %shard_map.30.w_ref), custom_call_target="tpu_custom_call" | custom-call | tf_op jit(solution)/shard_map/pallas_call | solution.py:322
  101.3 1.8 %copy.6 = f32[4,16,1024]{2,1,0:T(8,128)} copy(f32[4,16,1024]{2,0,1:T(4,128)} %bitcast.18) | data formatting | bytes 524288
  (1 shorter events, 0.0 us)
Async XLA Ops:
  3.6 5.4 %collective-permute-start = (bf16[32,2,1024]{2,0,1:T(8,128)(2,1)S(1)}, bf16[32,2,1024]{2,0,1:T(8,128)(2,1)S(1)}, u32[]{:S(2)}, u32[]{:S(2)}) collective-permute-start(bf16[32,2,1024]{2,0,1:T(8,128)(2,1)S(1)} %get-tuple-element.14), channel_id=1, source_target_pairs={{0,8},{8,16},{16,24},{24,32},{32,40},{40,48},{48,56},{56,64},{64,7... | collective-permute-start | bytes 393224 | tf_op jit(solution)/shard_map/ppermute | solution.py:19
  6.3 4.4 %collective-permute-start.1 = (bf16[32,2,1024]{2,0,1:T(8,128)(2,1)S(1)}, bf16[32,2,1024]{2,0,1:T(8,128)(2,1)S(1)}, u32[]{:S(2)}, u32[]{:S(2)}) collective-permute-start(bf16[32,2,1024]{2,0,1:T(8,128)(2,1)S(1)} %get-tuple-element.15), channel_id=1, source_target_pairs={{8,0},{16,8},{24,16},{32,24},{40,32},{48,40},{56,48},{64,56},{72,6... | collective-permute-start | bytes 393224 | tf_op jit(solution)/shard_map/ppermute | solution.py:20
  13.3 1.6 %copy-start = (bf16[32,16,1024]{2,0,1:T(8,128)(2,1)}, bf16[32,16,1024]{2,0,1:T(8,128)(2,1)S(1)}, u32[]{:S(2)}) copy-start(bf16[32,16,1024]{2,0,1:T(8,128)(2,1)S(1)} %fusion.3) | copy-start | bytes 3145732

commit v7 on v6

--- a/solution.py
+++ b/solution.py
@@ -32,10 +32,9 @@
 MESH = pl.DeviceIdType.MESH
 
 
-def allreduce_kernel(n_space, n_tm, g_ref, out_ref, buf1, buf2, buf3, send1, recv1, send2, recv2, send3, recv3):
+def greet_all(n_space, n_tm):
     s = lax.axis_index("space")
     t = lax.axis_index("tm")
-
     barrier = pltpu.get_barrier_semaphore()
 
     def greet_space(k, carry):
@@ -51,6 +50,11 @@
     lax.fori_loop(1, n_space, greet_space, 0)
     lax.fori_loop(1, n_tm, greet_tm, 0)
     pl.semaphore_wait(barrier, (n_space - 1) + (n_tm - 1))
+
+
+def allreduce_body(n_space, n_tm, g_ref, out_ref, buf1, buf2, buf3, send1, recv1, send2, recv2, send3, recv3):
+    s = lax.axis_index("space")
+    t = lax.axis_index("tm")
 
     def space_copy(src, dst_buf, send, recv, k):
         b = lax.rem(s + k, n_space)
@@ -126,41 +130,9 @@
     out_ref[...] = buf3[...]
 
 
-def allreduce(gram):
-    n_space = lax.axis_size("space")
-    n_tm = lax.axis_size("tm")
-    size = gram.shape[0]
-    chunks = gram.reshape(n_space, size // n_space, size)
-    shape = chunks.shape
-    out = pl.pallas_call(
-        functools.partial(allreduce_kernel, n_space, n_tm),
-        out_shape=jax.ShapeDtypeStruct(shape, jnp.float32),
-        in_specs=[pl.BlockSpec(memory_space=pltpu.VMEM)],
-        out_specs=pl.BlockSpec(memory_space=pltpu.VMEM),
-        scratch_shapes=[
-            pltpu.VMEM(shape, jnp.float32),
-            pltpu.VMEM((n_tm,) + shape[1:], jnp.float32),
-            pltpu.VMEM(shape, jnp.float32),
-            pltpu.SemaphoreType.DMA((n_space,)),
-            pltpu.SemaphoreType.DMA((n_space,)),
-            pltpu.SemaphoreType.DMA((n_tm,)),
-            pltpu.SemaphoreType.DMA((n_tm,)),
-            pltpu.SemaphoreType.DMA((n_space,)),
-            pltpu.SemaphoreType.DMA((n_space,)),
-        ],
-        compiler_params=pltpu.CompilerParams(collective_id=0, has_side_effects=True),
-    )(chunks)
-    return out.reshape(size, size)
-
-
-def a2a_kernel(n_tm, src_at, dst_at, x_ref, out_ref, buf, send, recv, own):
+def a2a_body(n_tm, src_at, dst_at, x_ref, buf, send, recv, own):
     s = lax.axis_index("space")
     t = lax.axis_index("tm")
-    barrier = pltpu.get_barrier_semaphore()
-    for k in range(1, n_tm):
-        a = lax.rem(t + k, n_tm)
-        pl.semaphore_signal(barrier, inc=1, device_id=(s, a), device_id_type=MESH)
-    pl.semaphore_wait(barrier, n_tm - 1)
     copies = []
     for k in range(1, n_tm):
         a = lax.rem(t + k, n_tm)
@@ -181,24 +153,65 @@
         ).wait_recv()
     for c in copies:
         c.wait_send()
-    out_ref[...] = buf[...]
-
-
-def all_to_all(x, out_shape, src_at, dst_at, cid):
+
+
+def front_kernel(n_space, n_tm, x_ref, cells_ref, g_out_ref, cells, gpart, buf1, buf2, buf3, *sems):
+    send, recv, own = sems[:3]
+    greet_all(n_space, n_tm)
+    rows, _, cols = x_ref.shape
+    width = cols // n_tm
+    a2a_body(
+        n_tm,
+        lambda ref, a: ref.at[:, :, lanes(a, width)],
+        lambda ref, j: ref.at[:, pl.ds(j * RANK, RANK), :],
+        x_ref, cells, send, recv, own,
+    )
+    size = cells.shape[1]
+    gram = jnp.zeros((size, size), jnp.float32)
+    for x in range(rows):
+        w = cells[x]
+        gram = gram + lax.dot_general(
+            w, w, (((1,), (1,)), ((), ())), preferred_element_type=jnp.float32
+        )
+    gpart[...] = gram.reshape(gpart.shape)
+    allreduce_body(n_space, n_tm, gpart, g_out_ref, buf1, buf2, buf3, *sems[3:])
+    cells_ref[...] = cells[...]
+
+
+def front(vort_x):
+    n_space = lax.axis_size("space")
     n_tm = lax.axis_size("tm")
-    return pl.pallas_call(
-        functools.partial(a2a_kernel, n_tm, src_at, dst_at),
-        out_shape=jax.ShapeDtypeStruct(out_shape, x.dtype),
+    rows, _, cols = vort_x.shape
+    size = n_tm * RANK
+    cells_shape = (rows, size, cols // n_tm)
+    chunks = (n_space, size // n_space, size)
+    cells_x, gram = pl.pallas_call(
+        functools.partial(front_kernel, n_space, n_tm),
+        out_shape=(
+            jax.ShapeDtypeStruct(cells_shape, vort_x.dtype),
+            jax.ShapeDtypeStruct(chunks, jnp.float32),
+        ),
         in_specs=[pl.BlockSpec(memory_space=pltpu.VMEM)],
-        out_specs=pl.BlockSpec(memory_space=pltpu.VMEM),
+        out_specs=(pl.BlockSpec(memory_space=pltpu.VMEM), pl.BlockSpec(memory_space=pltpu.VMEM)),
         scratch_shapes=[
-            pltpu.VMEM(out_shape, x.dtype),
+            pltpu.VMEM(cells_shape, vort_x.dtype),
+            pltpu.VMEM(chunks, jnp.float32),
+            pltpu.VMEM(chunks, jnp.float32),
+            pltpu.VMEM((n_tm,) + chunks[1:], jnp.float32),
+            pltpu.VMEM(chunks, jnp.float32),
             pltpu.SemaphoreType.DMA((n_tm,)),
             pltpu.SemaphoreType.DMA((n_tm,)),
             pltpu.SemaphoreType.DMA((1,)),
+            pltpu.SemaphoreType.DMA((n_space,)),
+            pltpu.SemaphoreType.DMA((n_space,)),
+            pltpu.SemaphoreType.DMA((n_tm,)),
+            pltpu.SemaphoreType.DMA((n_tm,)),
+            pltpu.SemaphoreType.DMA((n_space,)),
+            pltpu.SemaphoreType.DMA((n_space,)),
         ],
-        compiler_params=pltpu.CompilerParams(collective_id=cid, has_side_effects=True),
-    )(x)
+        compiler_params=pltpu.CompilerParams(collective_id=0, has_side_effects=True),
+    )(vort_x)
+    return cells_x, gram.reshape(size, size)
 
 
 def lanes(a, width):
@@ -348,15 +361,7 @@
     cols = vorticity.shape[2]
     width = cols // blocks
     vort_x = jnp.swapaxes(vorticity, 0, 1)
-    cells_x = all_to_all(
-        vort_x,
-        (rows, blocks * RANK, width),
-        lambda ref, a: ref.at[:, :, lanes(a, width)],
-        lambda ref, j: ref.at[:, pl.ds(j * RANK, RANK), :],
-        1,
-    )
-    gram = jnp.einsum("xaz,xbz->ab", cells_x, cells_x, preferred_element_type=jnp.float32)
-    gram = allreduce(gram)
+    cells_x, gram = front(vort_x)
     modes = jnp.swapaxes(finish(gram, cells_x), 0, 1)
     return (vorticity, modes)
 

time: 103 us -> 101 us (0.981)
  matrix products: 2.72 us -> 0 us
    dot_general x1 -> x0, matrix products: 2.72 us -> none  [local(): jnp.einsum('xaz,xbz->ab', cells_x, cells_x, preferred_element_type=jnp.fl...]
    pallas_call x2 -> x1, Pallas kernels: 59.6 us -> 57.4 us  [front(): pl.pallas_call(functools.partial(front_kernel, n_space, n_tm), out_shape=...]
    pallas_call x1, Pallas kernels: 24.1 us -> 26.3 us  [finish(): pl.pallas_call(functools.partial(finish_kernel, n_tm), out_shape=jax.Shap...]
where the time goes in v7:
time: 101 us; the launch traced here: 100 us
  Pallas kernels  83.7 us (83%)
  local copies, waits for them, and re-layouts  6.9 us (7%)
  other arithmetic  3.77 us (4%)
  starting transfers between devices  3.59 us (4%)
  waiting for transfers between devices  1.74 us (2%)
    pallas_call x1, Pallas kernels, front(): pl.pallas_call(functools.partial(front_kernel, n_space, n_tm), out_shape=...  57.4 us
    pallas_call x1, Pallas kernels, finish(): pl.pallas_call(functools.partial(finish_kernel, n_tm), out_shape=jax.Shap...  26.3 us
    unnamed x4, local copies, waits for them, and re-layouts  3.36 us
    ppermute x1, starting transfers between devices, halo_rows(): low = lax.ppermute(block[:, rows - width:], 'space', forward)  2.76 us
    convert_element_type x1, other arithmetic, local(): vorticity = (dv_dx - spanwise(stream_u)).astype(jnp.bfloat16)  2.38 us
  transfers between devices with their start and end apart: 2, of which 1 were waited for; matrix products, arithmetic and copies ran while one was open for 2% of the time, Pallas kernels for 0%

profile of v7, /device:TPU:1, one launch (start us, length us, event | category | flops | bytes accessed | tf_op | source)
XLA Modules:
  0.0 100.4 jit_solution(17330496810727364786)
XLA Ops:
  0.6 1.7 %fusion.13 = (bf16[32,1,16,1024]{3,2,1,0:T(8,128)(2,1)S(1)}, bf16[32,1,16,1024]{3,2,1,0:T(8,128)(2,1)S(1)}) fusion(bf16[32,2,16,1024]{3,2,1,0:T(8,128)(2,1)} %param.1), kind=kLoop, calls=%fused_computation.20 | loop fusion | bytes 4194304 | tf_op jit(solution)/shard_map/slice | solution.py:354
  2.4 1.2 %fusion.8 = (f32[32,16,1024]{2,0,1:T(8,128)S(1)}, bf16[32,16,1024]{2,0,1:T(8,128)(2,1)S(1)}) fusion(bf16[32,1,16,1024]{3,2,1,0:T(8,128)(2,1)S(1)} %get-tuple-element.16, bf16[32,1,16,1024]{3,2,1,0:T(8,128)(2,1)S(1)} %get-tuple-element.17), kind=kLoop, calls=%fused_computation.14 | loop fusion | flops 524288 | bytes 5242880 | tf_op jit(solution)/shard_map/convert_element_type | solution.py:354
  3.6 2.8 %collective-permute-start = (bf16[32,2,1024]{2,0,1:T(8,128)(2,1)S(1)}, bf16[32,2,1024]{2,0,1:T(8,128)(2,1)S(1)}, u32[]{:S(2)}, u32[]{:S(2)}) collective-permute-start(bf16[32,2,1024]{2,0,1:T(8,128)(2,1)S(1)} %get-tuple-element.18), channel_id=1, source_target_pairs={{0,8},{8,16},{16,24},{24,32},{32,40},{40,48},{48,56},{56,64},{64,7... | collective-permute-start | bytes 393224 | tf_op jit(solution)/shard_map/ppermute | solution.py:19
  6.3 0.8 collective-permute-start.1
  7.2 0.1 fusion.11
  7.3 0.8 fusion.12
  8.1 0.8 fusion.10
  8.8 0.1 fusion.9
  9.0 0.0 collective-permute-done
  9.0 1.7 %collective-permute-done.1 = bf16[32,2,1024]{2,0,1:T(8,128)(2,1)S(1)} collective-permute-done((bf16[32,2,1024]{2,0,1:T(8,128)(2,1)S(1)}, bf16[32,2,1024]{2,0,1:T(8,128)(2,1)S(1)}, u32[]{:S(2)}, u32[]{:S(2)}) %collective-permute-start.1) | collective-permute-done | bytes 131104 | tf_op jit(solution)/shard_map/ppermute | solution.py:20
  10.7 0.2 maximum_convert_fusion
  10.9 2.4 %fusion.3 = bf16[32,16,1024]{2,0,1:T(8,128)(2,1)S(1)} fusion(f32[32,20,1024]{2,0,1:T(8,128)S(1)} %maximum_convert_fusion, f32[32,16,1]{2,0,1:T(8,128)S(1)} %get-tuple-element.13, f32[32,16,1023]{2,0,1:T(8,128)S(1)} %get-tuple-element.15, f32[32,16,1023]{2,0,1:T(8,128)S(1)} %get-tuple-element.14, f32[32,16,1]{2,0,1:T(8,128)S(1)} %get-tuple-element.12, ...), kind=kLoop, calls=%fused_computation.4 | loop fusion | flops 8388608 | bytes 17825792 | tf_op jit(solution)/shard_map/convert_element_type | solution.py:359
  13.3 0.0 copy-start
  13.3 1.5 %copy.5 = bf16[32,16,1024]{2,1,0:T(8,128)(2,1)} copy(bf16[32,16,1024]{2,0,1:T(8,128)(2,1)S(1)} %fusion.3) | data formatting | bytes 2097152
  14.9 0.0 copy-done
  14.9 57.4 %shard_map.30 = (bf16[16,256,128]{2,1,0:T(8,128)(2,1)}, f32[32,8,256]{2,1,0:T(8,128)}) custom-call(bf16[16,32,1024]{2,1,0:T(8,128)(2,1)} %bitcast.10), custom_call_target="tpu_custom_call" | custom-call | tf_op jit(solution)/shard_map/pallas_call | solution.py:188
  72.3 26.3 %shard_map.31 = f32[16,4,1024]{2,1,0:T(4,128)} custom-call(f32[256,256]{1,0:T(8,128)} %bitcast.12, bf16[16,256,128]{2,1,0:T(8,128)(2,1)} %get-tuple-element.5.w_ref), custom_call_target="tpu_custom_call" | custom-call | tf_op jit(solution)/shard_map/pallas_call | solution.py:335
  98.6 1.8 %copy.6 = f32[4,16,1024]{2,1,0:T(8,128)} copy(f32[4,16,1024]{2,0,1:T(4,128)} %bitcast.11) | data formatting | bytes 524288
  (1 shorter events, 0.0 us)
Async XLA Ops:
  3.6 5.4 %collective-permute-start = (bf16[32,2,1024]{2,0,1:T(8,128)(2,1)S(1)}, bf16[32,2,1024]{2,0,1:T(8,128)(2,1)S(1)}, u32[]{:S(2)}, u32[]{:S(2)}) collective-permute-start(bf16[32,2,1024]{2,0,1:T(8,128)(2,1)S(1)} %get-tuple-element.18), channel_id=1, source_target_pairs={{0,8},{8,16},{16,24},{24,32},{32,40},{40,48},{48,56},{56,64},{64,7... | collective-permute-start | bytes 393224 | tf_op jit(solution)/shard_map/ppermute | solution.py:19
  6.3 4.4 %collective-permute-start.1 = (bf16[32,2,1024]{2,0,1:T(8,128)(2,1)S(1)}, bf16[32,2,1024]{2,0,1:T(8,128)(2,1)S(1)}, u32[]{:S(2)}, u32[]{:S(2)}) collective-permute-start(bf16[32,2,1024]{2,0,1:T(8,128)(2,1)S(1)} %get-tuple-element.19), channel_id=1, source_target_pairs={{8,0},{16,8},{24,16},{32,24},{40,32},{48,40},{56,48},{64,56},{72,6... | collective-permute-start | bytes 393224 | tf_op jit(solution)/shard_map/ppermute | solution.py:20
  13.3 1.6 %copy-start = (bf16[32,16,1024]{2,0,1:T(8,128)(2,1)}, bf16[32,16,1024]{2,0,1:T(8,128)(2,1)S(1)}, u32[]{:S(2)}) copy-start(bf16[32,16,1024]{2,0,1:T(8,128)(2,1)S(1)} %fusion.3) | copy-start | bytes 3145732

commit v8 on v7

--- a/solution.py
+++ b/solution.py
@@ -240,18 +240,15 @@
     row, col = iotas(inner.shape)
     eye = jnp.where(row == col, 1.0, 0.0)
 
-    def step(j, carry):
-        a, r = carry
-        at_row = row == j
-        at_col = col == j
-        a_row = jnp.sum(jnp.where(at_row, a, 0.0), axis=1, keepdims=True)
-        r_row = jnp.sum(jnp.where(at_row, r, 0.0), axis=1, keepdims=True)
-        a_col = jnp.sum(jnp.where(at_col, a, 0.0), axis=2, keepdims=True)
-        pivot = jnp.sum(jnp.where(at_col[:, :1], a_row, 0.0), axis=2, keepdims=True)
-        factor = jnp.where(row[:, :, :1] > j, a_col / pivot, 0.0)
-        return a - factor * a_row, r - factor * r_row
-
-    a, r = lax.fori_loop(0, RANK, step, (inner, eye * jnp.ones((n, 1, 1), jnp.float32)), unroll=True)
+    a = inner
+    r = eye * jnp.ones((n, 1, 1), jnp.float32)
+    below = row[:, :, :1]
+    for j in range(RANK):
+        a_row = a[:, j : j + 1, :]
+        r_row = r[:, j : j + 1, :]
+        factor = jnp.where(below > j, a[:, :, j : j + 1] / a_row[:, :, j : j + 1], 0.0)
+        a = a - factor * a_row
+        r = r - factor * r_row
     diag_u = jnp.sum(jnp.where(row == col, a, 0.0), axis=2, keepdims=True)
     return bdot(r * (scales / jnp.sqrt(diag_u)), kt)
 

time: 101 us -> 99.1 us (0.981)
  Pallas kernels: 83.7 us -> 82.2 us
    pallas_call x1, Pallas kernels: 26.3 us -> 24.8 us  [finish(): pl.pallas_call(functools.partial(finish_kernel, n_tm), out_shape=jax.Shap...]
where the time goes in v8:
time: 99.1 us; the launch traced here: 98.9 us
  Pallas kernels  82.2 us (83%)
  local copies, waits for them, and re-layouts  6.9 us (7%)
  other arithmetic  3.77 us (4%)
  starting transfers between devices  3.59 us (4%)
  waiting for transfers between devices  1.74 us (2%)
    pallas_call x1, Pallas kernels, front(): pl.pallas_call(functools.partial(front_kernel, n_space, n_tm), out_shape=...  57.4 us
    pallas_call x1, Pallas kernels, finish(): pl.pallas_call(functools.partial(finish_kernel, n_tm), out_shape=jax.Shap...  24.8 us
    unnamed x4, local copies, waits for them, and re-layouts  3.36 us
    ppermute x1, starting transfers between devices, halo_rows(): low = lax.ppermute(block[:, rows - width:], 'space', forward)  2.76 us
    convert_element_type x1, other arithmetic, local(): vorticity = (dv_dx - spanwise(stream_u)).astype(jnp.bfloat16)  2.38 us
  transfers between devices with their start and end apart: 2, of which 1 were waited for; matrix products, arithmetic and copies ran while one was open for 2% of the time, Pallas kernels for 0%

profile of v8, /device:TPU:1, one launch (start us, length us, event | category | flops | bytes accessed | tf_op | source)
XLA Modules:
  0.0 98.9 jit_solution(14025691535807591880)
XLA Ops:
  0.6 1.7 %fusion.13 = (bf16[32,1,16,1024]{3,2,1,0:T(8,128)(2,1)S(1)}, bf16[32,1,16,1024]{3,2,1,0:T(8,128)(2,1)S(1)}) fusion(bf16[32,2,16,1024]{3,2,1,0:T(8,128)(2,1)} %param.1), kind=kLoop, calls=%fused_computation.20 | loop fusion | bytes 4194304 | tf_op jit(solution)/shard_map/slice | solution.py:351
  2.4 1.2 %fusion.8 = (f32[32,16,1024]{2,0,1:T(8,128)S(1)}, bf16[32,16,1024]{2,0,1:T(8,128)(2,1)S(1)}) fusion(bf16[32,1,16,1024]{3,2,1,0:T(8,128)(2,1)S(1)} %get-tuple-element.16, bf16[32,1,16,1024]{3,2,1,0:T(8,128)(2,1)S(1)} %get-tuple-element.17), kind=kLoop, calls=%fused_computation.14 | loop fusion | flops 524288 | bytes 5242880 | tf_op jit(solution)/shard_map/convert_element_type | solution.py:351
  3.6 2.8 %collective-permute-start = (bf16[32,2,1024]{2,0,1:T(8,128)(2,1)S(1)}, bf16[32,2,1024]{2,0,1:T(8,128)(2,1)S(1)}, u32[]{:S(2)}, u32[]{:S(2)}) collective-permute-start(bf16[32,2,1024]{2,0,1:T(8,128)(2,1)S(1)} %get-tuple-element.18), channel_id=1, source_target_pairs={{0,8},{8,16},{16,24},{24,32},{32,40},{40,48},{48,56},{56,64},{64,7... | collective-permute-start | bytes 393224 | tf_op jit(solution)/shard_map/ppermute | solution.py:19
  6.3 0.8 collective-permute-start.1
  7.2 0.1 fusion.11
  7.3 0.8 fusion.12
  8.1 0.8 fusion.10
  8.8 0.1 fusion.9
  9.0 0.0 collective-permute-done
  9.0 1.7 %collective-permute-done.1 = bf16[32,2,1024]{2,0,1:T(8,128)(2,1)S(1)} collective-permute-done((bf16[32,2,1024]{2,0,1:T(8,128)(2,1)S(1)}, bf16[32,2,1024]{2,0,1:T(8,128)(2,1)S(1)}, u32[]{:S(2)}, u32[]{:S(2)}) %collective-permute-start.1) | collective-permute-done | bytes 131104 | tf_op jit(solution)/shard_map/ppermute | solution.py:20
  10.7 0.2 maximum_convert_fusion
  10.9 2.4 %fusion.3 = bf16[32,16,1024]{2,0,1:T(8,128)(2,1)S(1)} fusion(f32[32,20,1024]{2,0,1:T(8,128)S(1)} %maximum_convert_fusion, f32[32,16,1]{2,0,1:T(8,128)S(1)} %get-tuple-element.13, f32[32,16,1023]{2,0,1:T(8,128)S(1)} %get-tuple-element.15, f32[32,16,1023]{2,0,1:T(8,128)S(1)} %get-tuple-element.14, f32[32,16,1]{2,0,1:T(8,128)S(1)} %get-tuple-element.12, ...), kind=kLoop, calls=%fused_computation.4 | loop fusion | flops 8388608 | bytes 17825792 | tf_op jit(solution)/shard_map/convert_element_type | solution.py:356
  13.3 0.0 copy-start
  13.3 1.5 %copy.5 = bf16[32,16,1024]{2,1,0:T(8,128)(2,1)} copy(bf16[32,16,1024]{2,0,1:T(8,128)(2,1)S(1)} %fusion.3) | data formatting | bytes 2097152
  14.9 0.0 copy-done
  14.9 57.4 %shard_map.30 = (bf16[16,256,128]{2,1,0:T(8,128)(2,1)}, f32[32,8,256]{2,1,0:T(8,128)}) custom-call(bf16[16,32,1024]{2,1,0:T(8,128)(2,1)} %bitcast.10), custom_call_target="tpu_custom_call" | custom-call | tf_op jit(solution)/shard_map/pallas_call | solution.py:188
  72.3 24.8 %shard_map.31 = f32[16,4,1024]{2,1,0:T(4,128)} custom-call(f32[256,256]{1,0:T(8,128)} %bitcast.12, bf16[16,256,128]{2,1,0:T(8,128)(2,1)} %get-tuple-element.5.w_ref), custom_call_target="tpu_custom_call" | custom-call | tf_op jit(solution)/shard_map/pallas_call | solution.py:332
  97.1 1.8 %copy.6 = f32[4,16,1024]{2,1,0:T(8,128)} copy(f32[4,16,1024]{2,0,1:T(4,128)} %bitcast.11) | data formatting | bytes 524288
  (1 shorter events, 0.0 us)
Async XLA Ops:
  3.6 5.4 %collective-permute-start = (bf16[32,2,1024]{2,0,1:T(8,128)(2,1)S(1)}, bf16[32,2,1024]{2,0,1:T(8,128)(2,1)S(1)}, u32[]{:S(2)}, u32[]{:S(2)}) collective-permute-start(bf16[32,2,1024]{2,0,1:T(8,128)(2,1)S(1)} %get-tuple-element.18), channel_id=1, source_target_pairs={{0,8},{8,16},{16,24},{24,32},{32,40},{40,48},{48,56},{56,64},{64,7... | collective-permute-start | bytes 393224 | tf_op jit(solution)/shard_map/ppermute | solution.py:19
  6.3 4.4 %collective-permute-start.1 = (bf16[32,2,1024]{2,0,1:T(8,128)(2,1)S(1)}, bf16[32,2,1024]{2,0,1:T(8,128)(2,1)S(1)}, u32[]{:S(2)}, u32[]{:S(2)}) collective-permute-start(bf16[32,2,1024]{2,0,1:T(8,128)(2,1)S(1)} %get-tuple-element.19), channel_id=1, source_target_pairs={{8,0},{16,8},{24,16},{32,24},{40,32},{48,40},{56,48},{64,56},{72,6... | collective-permute-start | bytes 393224 | tf_op jit(solution)/shard_map/ppermute | solution.py:20
  13.3 1.6 %copy-start = (bf16[32,16,1024]{2,0,1:T(8,128)(2,1)}, bf16[32,16,1024]{2,0,1:T(8,128)(2,1)S(1)}, u32[]{:S(2)}) copy-start(bf16[32,16,1024]{2,0,1:T(8,128)(2,1)S(1)} %fusion.3) | copy-start | bytes 3145732

commit v9 on v8

--- a/solution.py
+++ b/solution.py
@@ -238,10 +238,9 @@
     scales = jnp.sqrt(dcol[:, :RANK] + dcol[:, RANK:])
     inner = bdot_t(bdot(kt, h), kt)
     row, col = iotas(inner.shape)
-    eye = jnp.where(row == col, 1.0, 0.0)
 
     a = inner
-    r = eye * jnp.ones((n, 1, 1), jnp.float32)
+    r = kt
     below = row[:, :, :1]
     for j in range(RANK):
         a_row = a[:, j : j + 1, :]
@@ -250,7 +249,7 @@
         a = a - factor * a_row
         r = r - factor * r_row
     diag_u = jnp.sum(jnp.where(row == col, a, 0.0), axis=2, keepdims=True)
-    return bdot(r * (scales / jnp.sqrt(diag_u)), kt)
+    return r * (scales / jnp.sqrt(diag_u))
 
 
 def place(x, offset, width):

time: 99.1 us -> 98.7 us (level)
  no operation moved by 1% of the time
where the time goes in v9:
time: 98.7 us; the launch traced here: 98.5 us
  Pallas kernels  81.8 us (83%)
  local copies, waits for them, and re-layouts  6.9 us (7%)
  other arithmetic  3.77 us (4%)
  starting transfers between devices  3.59 us (4%)
  waiting for transfers between devices  1.74 us (2%)
    pallas_call x1, Pallas kernels, front(): pl.pallas_call(functools.partial(front_kernel, n_space, n_tm), out_shape=...  57.4 us
    pallas_call x1, Pallas kernels, finish(): pl.pallas_call(functools.partial(finish_kernel, n_tm), out_shape=jax.Shap...  24.4 us
    unnamed x4, local copies, waits for them, and re-layouts  3.36 us
    ppermute x1, starting transfers between devices, halo_rows(): low = lax.ppermute(block[:, rows - width:], 'space', forward)  2.76 us
    convert_element_type x1, other arithmetic, local(): vorticity = (dv_dx - spanwise(stream_u)).astype(jnp.bfloat16)  2.38 us
  transfers between devices with their start and end apart: 2, of which 1 were waited for; matrix products, arithmetic and copies ran while one was open for 2% of the time, Pallas kernels for 0%

profile of v9, /device:TPU:1, one launch (start us, length us, event | category | flops | bytes accessed | tf_op | source)
XLA Modules:
  0.0 98.5 jit_solution(12935164877116374931)
XLA Ops:
  0.6 1.7 %fusion.13 = (bf16[32,1,16,1024]{3,2,1,0:T(8,128)(2,1)S(1)}, bf16[32,1,16,1024]{3,2,1,0:T(8,128)(2,1)S(1)}) fusion(bf16[32,2,16,1024]{3,2,1,0:T(8,128)(2,1)} %param.1), kind=kLoop, calls=%fused_computation.20 | loop fusion | bytes 4194304 | tf_op jit(solution)/shard_map/slice | solution.py:350
  2.4 1.2 %fusion.8 = (f32[32,16,1024]{2,0,1:T(8,128)S(1)}, bf16[32,16,1024]{2,0,1:T(8,128)(2,1)S(1)}) fusion(bf16[32,1,16,1024]{3,2,1,0:T(8,128)(2,1)S(1)} %get-tuple-element.16, bf16[32,1,16,1024]{3,2,1,0:T(8,128)(2,1)S(1)} %get-tuple-element.17), kind=kLoop, calls=%fused_computation.14 | loop fusion | flops 524288 | bytes 5242880 | tf_op jit(solution)/shard_map/convert_element_type | solution.py:350
  3.6 2.8 %collective-permute-start = (bf16[32,2,1024]{2,0,1:T(8,128)(2,1)S(1)}, bf16[32,2,1024]{2,0,1:T(8,128)(2,1)S(1)}, u32[]{:S(2)}, u32[]{:S(2)}) collective-permute-start(bf16[32,2,1024]{2,0,1:T(8,128)(2,1)S(1)} %get-tuple-element.18), channel_id=1, source_target_pairs={{0,8},{8,16},{16,24},{24,32},{32,40},{40,48},{48,56},{56,64},{64,7... | collective-permute-start | bytes 393224 | tf_op jit(solution)/shard_map/ppermute | solution.py:19
  6.3 0.8 collective-permute-start.1
  7.2 0.1 fusion.11
  7.3 0.8 fusion.12
  8.1 0.8 fusion.10
  8.8 0.1 fusion.9
  9.0 0.0 collective-permute-done
  9.0 1.7 %collective-permute-done.1 = bf16[32,2,1024]{2,0,1:T(8,128)(2,1)S(1)} collective-permute-done((bf16[32,2,1024]{2,0,1:T(8,128)(2,1)S(1)}, bf16[32,2,1024]{2,0,1:T(8,128)(2,1)S(1)}, u32[]{:S(2)}, u32[]{:S(2)}) %collective-permute-start.1) | collective-permute-done | bytes 131104 | tf_op jit(solution)/shard_map/ppermute | solution.py:20
  10.7 0.2 maximum_convert_fusion
  10.9 2.4 %fusion.3 = bf16[32,16,1024]{2,0,1:T(8,128)(2,1)S(1)} fusion(f32[32,20,1024]{2,0,1:T(8,128)S(1)} %maximum_convert_fusion, f32[32,16,1]{2,0,1:T(8,128)S(1)} %get-tuple-element.13, f32[32,16,1023]{2,0,1:T(8,128)S(1)} %get-tuple-element.15, f32[32,16,1023]{2,0,1:T(8,128)S(1)} %get-tuple-element.14, f32[32,16,1]{2,0,1:T(8,128)S(1)} %get-tuple-element.12, ...), kind=kLoop, calls=%fused_computation.4 | loop fusion | flops 8388608 | bytes 17825792 | tf_op jit(solution)/shard_map/convert_element_type | solution.py:355
  13.3 0.0 copy-start
  13.3 1.5 %copy.5 = bf16[32,16,1024]{2,1,0:T(8,128)(2,1)} copy(bf16[32,16,1024]{2,0,1:T(8,128)(2,1)S(1)} %fusion.3) | data formatting | bytes 2097152
  14.9 0.0 copy-done
  14.9 57.4 %shard_map.30 = (bf16[16,256,128]{2,1,0:T(8,128)(2,1)}, f32[32,8,256]{2,1,0:T(8,128)}) custom-call(bf16[16,32,1024]{2,1,0:T(8,128)(2,1)} %bitcast.10), custom_call_target="tpu_custom_call" | custom-call | tf_op jit(solution)/shard_map/pallas_call | solution.py:188
  72.3 24.4 %shard_map.31 = f32[16,4,1024]{2,1,0:T(4,128)} custom-call(f32[256,256]{1,0:T(8,128)} %bitcast.12, bf16[16,256,128]{2,1,0:T(8,128)(2,1)} %get-tuple-element.5.w_ref), custom_call_target="tpu_custom_call" | custom-call | tf_op jit(solution)/shard_map/pallas_call | solution.py:331
  96.7 1.8 %copy.6 = f32[4,16,1024]{2,1,0:T(8,128)} copy(f32[4,16,1024]{2,0,1:T(4,128)} %bitcast.11) | data formatting | bytes 524288
  (1 shorter events, 0.0 us)
Async XLA Ops:
  3.6 5.4 %collective-permute-start = (bf16[32,2,1024]{2,0,1:T(8,128)(2,1)S(1)}, bf16[32,2,1024]{2,0,1:T(8,128)(2,1)S(1)}, u32[]{:S(2)}, u32[]{:S(2)}) collective-permute-start(bf16[32,2,1024]{2,0,1:T(8,128)(2,1)S(1)} %get-tuple-element.18), channel_id=1, source_target_pairs={{0,8},{8,16},{16,24},{24,32},{32,40},{40,48},{48,56},{56,64},{64,7... | collective-permute-start | bytes 393224 | tf_op jit(solution)/shard_map/ppermute | solution.py:19
  6.3 4.4 %collective-permute-start.1 = (bf16[32,2,1024]{2,0,1:T(8,128)(2,1)S(1)}, bf16[32,2,1024]{2,0,1:T(8,128)(2,1)S(1)}, u32[]{:S(2)}, u32[]{:S(2)}) collective-permute-start(bf16[32,2,1024]{2,0,1:T(8,128)(2,1)S(1)} %get-tuple-element.19), channel_id=1, source_target_pairs={{8,0},{16,8},{24,16},{32,24},{40,32},{48,40},{56,48},{64,56},{72,6... | collective-permute-start | bytes 393224 | tf_op jit(solution)/shard_map/ppermute | solution.py:20
  13.3 1.6 %copy-start = (bf16[32,16,1024]{2,0,1:T(8,128)(2,1)}, bf16[32,16,1024]{2,0,1:T(8,128)(2,1)S(1)}, u32[]{:S(2)}) copy-start(bf16[32,16,1024]{2,0,1:T(8,128)(2,1)S(1)} %fusion.3) | copy-start | bytes 3145732

commit v10 on v9

--- a/solution.py
+++ b/solution.py
@@ -291,10 +291,14 @@
         a = lax.rem(t + k, n_tm)
         pl.semaphore_signal(barrier, inc=1, device_id=(s, a), device_id_type=MESH)
     basis_t = tree_levels(g_ref)
+    hi = basis_t.astype(jnp.bfloat16)
+    rest = basis_t - hi.astype(jnp.float32)
+    mid = rest.astype(jnp.bfloat16)
+    lo = (rest - mid.astype(jnp.float32)).astype(jnp.bfloat16)
+    pieces = jnp.concatenate([hi, mid, lo], axis=0)
     for x in range(w_ref.shape[0]):
-        part_ref[x] = jnp.dot(
-            basis_t, w_ref[x].astype(jnp.float32), precision=HIGH, preferred_element_type=jnp.float32
-        )
+        terms = jnp.dot(pieces, w_ref[x], preferred_element_type=jnp.float32)
+        part_ref[x] = (terms[:RANK] + terms[RANK : 2 * RANK]) + terms[2 * RANK :]
     share = part_ref.shape[1] // n_tm
     width = w_ref.shape[2]
     src_at = lambda a: part_ref.at[:, pl.ds(a * share, share), :]

time: 98.7 us -> 98.1 us (level)
  no operation moved by 1% of the time
where the time goes in v10:
time: 98.1 us; the launch traced here: 97.9 us
  Pallas kernels  81.2 us (83%)
  local copies, waits for them, and re-layouts  6.9 us (7%)
  other arithmetic  3.77 us (4%)
  starting transfers between devices  3.59 us (4%)
  waiting for transfers between devices  1.74 us (2%)
    pallas_call x1, Pallas kernels, front(): pl.pallas_call(functools.partial(front_kernel, n_space, n_tm), out_shape=...  57.4 us
    pallas_call x1, Pallas kernels, finish(): pl.pallas_call(functools.partial(finish_kernel, n_tm), out_shape=jax.Shap...  23.8 us
    unnamed x4, local copies, waits for them, and re-layouts  3.36 us
    ppermute x1, starting transfers between devices, halo_rows(): low = lax.ppermute(block[:, rows - width:], 'space', forward)  2.76 us
    convert_element_type x1, other arithmetic, local(): vorticity = (dv_dx - spanwise(stream_u)).astype(jnp.bfloat16)  2.38 us
  transfers between devices with their start and end apart: 2, of which 1 were waited for; matrix products, arithmetic and copies ran while one was open for 2% of the time, Pallas kernels for 0%

profile of v10, /device:TPU:1, one launch (start us, length us, event | category | flops | bytes accessed | tf_op | source)
XLA Modules:
  0.0 97.9 jit_solution(3157471972877325458)
XLA Ops:
  0.6 1.7 %fusion.13 = (bf16[32,1,16,1024]{3,2,1,0:T(8,128)(2,1)S(1)}, bf16[32,1,16,1024]{3,2,1,0:T(8,128)(2,1)S(1)}) fusion(bf16[32,2,16,1024]{3,2,1,0:T(8,128)(2,1)} %param.1), kind=kLoop, calls=%fused_computation.20 | loop fusion | bytes 4194304 | tf_op jit(solution)/shard_map/slice | solution.py:354
  2.4 1.2 %fusion.8 = (f32[32,16,1024]{2,0,1:T(8,128)S(1)}, bf16[32,16,1024]{2,0,1:T(8,128)(2,1)S(1)}) fusion(bf16[32,1,16,1024]{3,2,1,0:T(8,128)(2,1)S(1)} %get-tuple-element.16, bf16[32,1,16,1024]{3,2,1,0:T(8,128)(2,1)S(1)} %get-tuple-element.17), kind=kLoop, calls=%fused_computation.14 | loop fusion | flops 524288 | bytes 5242880 | tf_op jit(solution)/shard_map/convert_element_type | solution.py:354
  3.6 2.8 %collective-permute-start = (bf16[32,2,1024]{2,0,1:T(8,128)(2,1)S(1)}, bf16[32,2,1024]{2,0,1:T(8,128)(2,1)S(1)}, u32[]{:S(2)}, u32[]{:S(2)}) collective-permute-start(bf16[32,2,1024]{2,0,1:T(8,128)(2,1)S(1)} %get-tuple-element.18), channel_id=1, source_target_pairs={{0,8},{8,16},{16,24},{24,32},{32,40},{40,48},{48,56},{56,64},{64,7... | collective-permute-start | bytes 393224 | tf_op jit(solution)/shard_map/ppermute | solution.py:19
  6.3 0.8 collective-permute-start.1
  7.2 0.1 fusion.11
  7.3 0.8 fusion.12
  8.1 0.8 fusion.10
  8.8 0.1 fusion.9
  9.0 0.0 collective-permute-done
  9.0 1.7 %collective-permute-done.1 = bf16[32,2,1024]{2,0,1:T(8,128)(2,1)S(1)} collective-permute-done((bf16[32,2,1024]{2,0,1:T(8,128)(2,1)S(1)}, bf16[32,2,1024]{2,0,1:T(8,128)(2,1)S(1)}, u32[]{:S(2)}, u32[]{:S(2)}) %collective-permute-start.1) | collective-permute-done | bytes 131104 | tf_op jit(solution)/shard_map/ppermute | solution.py:20
  10.7 0.2 maximum_convert_fusion
  10.9 2.4 %fusion.3 = bf16[32,16,1024]{2,0,1:T(8,128)(2,1)S(1)} fusion(f32[32,20,1024]{2,0,1:T(8,128)S(1)} %maximum_convert_fusion, f32[32,16,1]{2,0,1:T(8,128)S(1)} %get-tuple-element.13, f32[32,16,1023]{2,0,1:T(8,128)S(1)} %get-tuple-element.15, f32[32,16,1023]{2,0,1:T(8,128)S(1)} %get-tuple-element.14, f32[32,16,1]{2,0,1:T(8,128)S(1)} %get-tuple-element.12, ...), kind=kLoop, calls=%fused_computation.4 | loop fusion | flops 8388608 | bytes 17825792 | tf_op jit(solution)/shard_map/convert_element_type | solution.py:359
  13.3 0.0 copy-start
  13.3 1.5 %copy.5 = bf16[32,16,1024]{2,1,0:T(8,128)(2,1)} copy(bf16[32,16,1024]{2,0,1:T(8,128)(2,1)S(1)} %fusion.3) | data formatting | bytes 2097152
  14.9 0.0 copy-done
  14.9 57.4 %shard_map.30 = (bf16[16,256,128]{2,1,0:T(8,128)(2,1)}, f32[32,8,256]{2,1,0:T(8,128)}) custom-call(bf16[16,32,1024]{2,1,0:T(8,128)(2,1)} %bitcast.10), custom_call_target="tpu_custom_call" | custom-call | tf_op jit(solution)/shard_map/pallas_call | solution.py:188
  72.3 23.8 %shard_map.31 = f32[16,4,1024]{2,1,0:T(4,128)} custom-call(f32[256,256]{1,0:T(8,128)} %bitcast.12, bf16[16,256,128]{2,1,0:T(8,128)(2,1)} %get-tuple-element.5.w_ref), custom_call_target="tpu_custom_call" | custom-call | tf_op jit(solution)/shard_map/pallas_call | solution.py:335
  96.1 1.8 %copy.6 = f32[4,16,1024]{2,1,0:T(8,128)} copy(f32[4,16,1024]{2,0,1:T(4,128)} %bitcast.11) | data formatting | bytes 524288
  (1 shorter events, 0.0 us)
Async XLA Ops:
  3.6 5.4 %collective-permute-start = (bf16[32,2,1024]{2,0,1:T(8,128)(2,1)S(1)}, bf16[32,2,1024]{2,0,1:T(8,128)(2,1)S(1)}, u32[]{:S(2)}, u32[]{:S(2)}) collective-permute-start(bf16[32,2,1024]{2,0,1:T(8,128)(2,1)S(1)} %get-tuple-element.18), channel_id=1, source_target_pairs={{0,8},{8,16},{16,24},{24,32},{32,40},{40,48},{48,56},{56,64},{64,7... | collective-permute-start | bytes 393224 | tf_op jit(solution)/shard_map/ppermute | solution.py:19
  6.3 4.4 %collective-permute-start.1 = (bf16[32,2,1024]{2,0,1:T(8,128)(2,1)S(1)}, bf16[32,2,1024]{2,0,1:T(8,128)(2,1)S(1)}, u32[]{:S(2)}, u32[]{:S(2)}) collective-permute-start(bf16[32,2,1024]{2,0,1:T(8,128)(2,1)S(1)} %get-tuple-element.19), channel_id=1, source_target_pairs={{8,0},{16,8},{24,16},{32,24},{40,32},{48,40},{56,48},{64,56},{72,6... | collective-permute-start | bytes 393224 | tf_op jit(solution)/shard_map/ppermute | solution.py:20
  13.3 1.6 %copy-start = (bf16[32,16,1024]{2,0,1:T(8,128)(2,1)}, bf16[32,16,1024]{2,0,1:T(8,128)(2,1)S(1)}, u32[]{:S(2)}) copy-start(bf16[32,16,1024]{2,0,1:T(8,128)(2,1)S(1)} %fusion.3) | copy-start | bytes 3145732

commit v11 on v10

--- a/solution.py
+++ b/solution.py
@@ -19,14 +19,6 @@
     low = lax.ppermute(block[:, rows - width :], "space", forward)
     high = lax.ppermute(block[:, :width], "space", backward)
     return jnp.concatenate([low, block, high], axis=1)
-
-
-def spanwise(field):
-    ahead = jnp.roll(field, -1, 2)
-    behind = jnp.roll(field, 1, 2)
-    ahead_two = jnp.roll(field, -2, 2)
-    behind_two = jnp.roll(field, 2, 2)
-    return (8.0 * (ahead - behind) - (ahead_two - behind_two)) / 12.0
 
 
 MESH = pl.DeviceIdType.MESH
@@ -350,13 +342,18 @@
 
 def local(velocity):
     rows = velocity.shape[2]
-    span_v = halo_rows(velocity[:, 1], 2).astype(jnp.float32)
-    stream_u = velocity[:, 0].astype(jnp.float32)
+    span_v = halo_rows(velocity[:, 1], 2)
+    stream_u = velocity[:, 0]
+    f32 = lambda x: x.astype(jnp.float32)
     dv_dx = (
-        8.0 * (span_v[:, 3 : rows + 3] - span_v[:, 1 : rows + 1])
-        - (span_v[:, 4:] - span_v[:, :rows])
+        8.0 * (f32(span_v[:, 3 : rows + 3]) - f32(span_v[:, 1 : rows + 1]))
+        - (f32(span_v[:, 4:]) - f32(span_v[:, :rows]))
     ) / 12.0
-    vorticity = (dv_dx - spanwise(stream_u)).astype(jnp.bfloat16)
+    du_dz = (
+        8.0 * (f32(jnp.roll(stream_u, -1, 2)) - f32(jnp.roll(stream_u, 1, 2)))
+        - (f32(jnp.roll(stream_u, -2, 2)) - f32(jnp.roll(stream_u, 2, 2)))
+    ) / 12.0
+    vorticity = (dv_dx - du_dz).astype(jnp.bfloat16)
     blocks = lax.axis_size("tm")
     cols = vorticity.shape[2]
     width = cols // blocks

time: 98.1 us -> 99.7 us (1.016)
  Pallas kernels: 81.2 us -> 82.6 us
  local copies, waits for them, and re-layouts: 6.9 us -> 8.06 us
    ppermute x1, starting transfers between devices: 2.76 us -> 0.01 us  [halo_rows(): low = lax.ppermute(block[:, rows - width:], 'space', forward)]
    ppermute x1, starting transfers between devices: 0.83 us -> 3.32 us  [halo_rows(): high = lax.ppermute(block[:, :width], 'space', backward)]
    pallas_call x1, Pallas kernels: 57.4 us -> 59.1 us  [front(): pl.pallas_call(functools.partial(front_kernel, n_space, n_tm), out_shape=...]
    ppermute x1, waiting for transfers between devices: 0.01 us -> 1.66 us  [halo_rows(): low = lax.ppermute(block[:, rows - width:], 'space', forward)]
    ppermute x1, waiting for transfers between devices: 1.73 us -> 0.28 us  [halo_rows(): high = lax.ppermute(block[:, :width], 'space', backward)]
    squeeze x0 -> x1, local copies, waits for them, and re-layouts: none -> 1.15 us  [local(): stream_u = velocity[:, 0]]
    convert_element_type x3 -> x1, other arithmetic: 3.77 us -> 2.9 us  [local(): vorticity = (dv_dx - du_dz).astype(jnp.bfloat16)]
  transfers between devices with their start and end apart: 2 -> 2, of which waited for: 1 -> 2; matrix products, arithmetic and copies ran while one was open for 2% -> 2% of each run, Pallas kernels for 0% -> 0%
where the time goes in v11:
time: 99.7 us; the launch traced here: 99.5 us
  Pallas kernels  82.6 us (83%)
  local copies, waits for them, and re-layouts  8.06 us (8%)
  starting transfers between devices  3.32 us (3%)
  other arithmetic  2.9 us (3%)
  waiting for transfers between devices  1.93 us (2%)
    pallas_call x1, Pallas kernels, front(): pl.pallas_call(functools.partial(front_kernel, n_space, n_tm), out_shape=...  59.1 us
    pallas_call x1, Pallas kernels, finish(): pl.pallas_call(functools.partial(finish_kernel, n_tm), out_shape=jax.Shap...  23.4 us
    unnamed x4, local copies, waits for them, and re-layouts  3.36 us
    ppermute x1, starting transfers between devices, halo_rows(): high = lax.ppermute(block[:, :width], 'space', backward)  3.32 us
    convert_element_type x1, other arithmetic, local(): vorticity = (dv_dx - du_dz).astype(jnp.bfloat16)  2.9 us
  transfers between devices with their start and end apart: 2, of which 2 were waited for; matrix products, arithmetic and copies ran while one was open for 2% of the time, Pallas kernels for 0%

profile of v11, /device:TPU:1, one launch (start us, length us, event | category | flops | bytes accessed | tf_op | source)
XLA Modules:
  0.0 99.5 jit_solution(15783329400341036166)
XLA Ops:
  0.6 1.7 %fusion.2 = (bf16[32,1,16,1024]{3,2,1,0:T(8,128)(2,1)S(1)}, bf16[32,1,16,1024]{3,2,1,0:T(8,128)(2,1)S(1)}) fusion(bf16[32,2,16,1024]{3,2,1,0:T(8,128)(2,1)} %param.1), kind=kLoop, calls=%fused_computation.11 | loop fusion | bytes 4194304 | tf_op jit(solution)/shard_map/slice | solution.py:346
  2.4 1.2 %copy_bitcast_fusion = (bf16[32,16,1024]{2,0,1:T(8,128)(2,1)S(1)}, bf16[32,16,1024]{2,0,1:T(8,128)(2,1)S(1)}) fusion(bf16[32,1,16,1024]{3,2,1,0:T(8,128)(2,1)S(1)} %get-tuple-element.8, bf16[32,1,16,1024]{3,2,1,0:T(8,128)(2,1)S(1)} %get-tuple-element.9), kind=kLoop, calls=%fused_computation.9 | loop fusion | bytes 4194304 | tf_op jit(solution)/shard_map/squeeze | solution.py:346
  3.5 3.3 %collective-permute-start = (bf16[32,2,1024]{2,0,1:T(8,128)(2,1)S(1)}, bf16[32,2,1024]{2,0,1:T(8,128)(2,1)S(1)}, u32[]{:S(2)}, u32[]{:S(2)}) collective-permute-start(bf16[32,2,1024]{2,0,1:T(8,128)(2,1)S(1)} %get-tuple-element.18), channel_id=1, source_target_pairs={{8,0},{16,8},{24,16},{32,24},{40,32},{48,40},{56,48},{64,56},{72,6... | collective-permute-start | bytes 393224 | tf_op jit(solution)/shard_map/ppermute | solution.py:20
  6.9 0.0 collective-permute-start.1
  6.9 0.8 fusion.4
  7.7 0.8 fusion.6
  8.5 0.1 fusion.3
  8.6 0.1 fusion.5
  8.7 0.3 collective-permute-done
  9.0 1.7 %collective-permute-done.1 = bf16[32,2,1024]{2,0,1:T(8,128)(2,1)S(1)} collective-permute-done((bf16[32,2,1024]{2,0,1:T(8,128)(2,1)S(1)}, bf16[32,2,1024]{2,0,1:T(8,128)(2,1)S(1)}, u32[]{:S(2)}, u32[]{:S(2)}) %collective-permute-start.1) | collective-permute-done | bytes 131104 | tf_op jit(solution)/shard_map/ppermute | solution.py:19
  10.6 2.9 %subtract_convert_fusion = bf16[32,16,1024]{2,0,1:T(8,128)(2,1)S(1)} fusion(bf16[32,2,1024]{2,0,1:T(8,128)(2,1)S(1)} %collective-permute-done.1, bf16[32,16,1024]{2,0,1:T(8,128)(2,1)S(1)} %get-tuple-element.21, bf16[32,2,1024]{2,0,1:T(8,128)(2,1)S(1)} %collective-permute-done, bf16[32,16,1]{2,0,1:T(8,128)(2,1)S(1)} %get-tuple-element.15, ...), kind=kLoop, calls=%fused_computation | loop fusion | flops 23068672 | bytes 6553600 | tf_op jit(solution)/shard_map/convert_element_type | solution.py:356
  13.5 0.0 copy-start
  13.5 1.5 %copy.5 = bf16[32,16,1024]{2,1,0:T(8,128)(2,1)} copy(bf16[32,16,1024]{2,0,1:T(8,128)(2,1)S(1)} %subtract_convert_fusion) | data formatting | bytes 2097152
  15.1 0.0 copy-done
  15.1 59.1 %shard_map.30 = (bf16[16,256,128]{2,1,0:T(8,128)(2,1)}, f32[32,8,256]{2,1,0:T(8,128)}) custom-call(bf16[16,32,1024]{2,1,0:T(8,128)(2,1)} %bitcast.7), custom_call_target="tpu_custom_call" | custom-call | tf_op jit(solution)/shard_map/pallas_call | solution.py:180
  74.2 23.4 %shard_map.31 = f32[16,4,1024]{2,1,0:T(4,128)} custom-call(f32[256,256]{1,0:T(8,128)} %bitcast.9, bf16[16,256,128]{2,1,0:T(8,128)(2,1)} %get-tuple-element.5.w_ref), custom_call_target="tpu_custom_call" | custom-call | tf_op jit(solution)/shard_map/pallas_call | solution.py:327
  97.7 1.8 %copy.6 = f32[4,16,1024]{2,1,0:T(8,128)} copy(f32[4,16,1024]{2,0,1:T(4,128)} %bitcast.8) | data formatting | bytes 524288
  (1 shorter events, 0.0 us)
Async XLA Ops:
  3.5 5.4 %collective-permute-start = (bf16[32,2,1024]{2,0,1:T(8,128)(2,1)S(1)}, bf16[32,2,1024]{2,0,1:T(8,128)(2,1)S(1)}, u32[]{:S(2)}, u32[]{:S(2)}) collective-permute-start(bf16[32,2,1024]{2,0,1:T(8,128)(2,1)S(1)} %get-tuple-element.18), channel_id=1, source_target_pairs={{8,0},{16,8},{24,16},{32,24},{40,32},{48,40},{56,48},{64,56},{72,6... | collective-permute-start | bytes 393224 | tf_op jit(solution)/shard_map/ppermute | solution.py:20
  6.9 3.8 %collective-permute-start.1 = (bf16[32,2,1024]{2,0,1:T(8,128)(2,1)S(1)}, bf16[32,2,1024]{2,0,1:T(8,128)(2,1)S(1)}, u32[]{:S(2)}, u32[]{:S(2)}) collective-permute-start(bf16[32,2,1024]{2,0,1:T(8,128)(2,1)S(1)} %get-tuple-element.19), channel_id=1, source_target_pairs={{0,8},{8,16},{16,24},{24,32},{32,40},{40,48},{48,56},{56,64},{64,7... | collective-permute-start | bytes 393224 | tf_op jit(solution)/shard_map/ppermute | solution.py:19
  13.5 1.6 %copy-start = (bf16[32,16,1024]{2,0,1:T(8,128)(2,1)}, bf16[32,16,1024]{2,0,1:T(8,128)(2,1)S(1)}, u32[]{:S(2)}) copy-start(bf16[32,16,1024]{2,0,1:T(8,128)(2,1)S(1)} %subtract_convert_fusion) | copy-start | bytes 3145732

commit v12 on v10

--- a/solution.py
+++ b/solution.py
@@ -155,7 +155,7 @@
         c.wait_send()
 
 
-def front_kernel(n_space, n_tm, x_ref, cells_ref, g_out_ref, cells, gpart, buf1, buf2, buf3, *sems):
+def front_kernel(n_space, n_tm, x_ref, modes_ref, cells, gpart, buf1, buf2, buf3, gfull, part, gathered, *sems):
     send, recv, own = sems[:3]
     greet_all(n_space, n_tm)
     rows, _, cols = x_ref.shape
@@ -174,8 +174,9 @@
             w, w, (((1,), (1,)), ((), ())), preferred_element_type=jnp.float32
         )
     gpart[...] = gram.reshape(gpart.shape)
-    allreduce_body(n_space, n_tm, gpart, g_out_ref, buf1, buf2, buf3, *sems[3:])
-    cells_ref[...] = cells[...]
+    allreduce_body(n_space, n_tm, gpart, buf1, buf1, buf2, buf3, *sems[3:9])
+    gfull[...] = buf3[...].reshape(gfull.shape)
+    finish_body(n_tm, gfull, cells, modes_ref, part, gathered, *sems[9:])
 
 
 def front(vort_x):
@@ -183,22 +184,24 @@
     n_tm = lax.axis_size("tm")
     rows, _, cols = vort_x.shape
     size = n_tm * RANK
-    cells_shape = (rows, size, cols // n_tm)
+    width = cols // n_tm
+    cells_shape = (rows, size, width)
     chunks = (n_space, size // n_space, size)
-    cells_x, gram = pl.pallas_call(
+    out_shape = (rows, RANK // n_tm, cols)
+    return pl.pallas_call(
         functools.partial(front_kernel, n_space, n_tm),
-        out_shape=(
-            jax.ShapeDtypeStruct(cells_shape, vort_x.dtype),
-            jax.ShapeDtypeStruct(chunks, jnp.float32),
-        ),
+        out_shape=jax.ShapeDtypeStruct(out_shape, jnp.float32),
         in_specs=[pl.BlockSpec(memory_space=pltpu.VMEM)],
-        out_specs=(pl.BlockSpec(memory_space=pltpu.VMEM), pl.BlockSpec(memory_space=pltpu.VMEM)),
+        out_specs=pl.BlockSpec(memory_space=pltpu.VMEM),
         scratch_shapes=[
             pltpu.VMEM(cells_shape, vort_x.dtype),
             pltpu.VMEM(chunks, jnp.float32),
             pltpu.VMEM(chunks, jnp.float32),
             pltpu.VMEM((n_tm,) + chunks[1:], jnp.float32),
             pltpu.VMEM(chunks, jnp.float32),
+            pltpu.VMEM((size, size), jnp.float32),
+            pltpu.VMEM((rows, RANK, width), jnp.float32),
+            pltpu.VMEM(out_shape, jnp.float32),
             pltpu.SemaphoreType.DMA((n_tm,)),
             pltpu.SemaphoreType.DMA((n_tm,)),
             pltpu.SemaphoreType.DMA((1,)),
@@ -208,10 +211,12 @@
             pltpu.SemaphoreType.DMA((n_tm,)),
             pltpu.SemaphoreType.DMA((n_space,)),
             pltpu.SemaphoreType.DMA((n_space,)),
+            pltpu.SemaphoreType.DMA((n_tm,)),
+            pltpu.SemaphoreType.DMA((n_tm,)),
+            pltpu.SemaphoreType.DMA((1,)),
         ],
         compiler_params=pltpu.CompilerParams(collective_id=0, has_side_effects=True),
     )(vort_x)
-    return cells_x, gram.reshape(size, size)
 
 
 def lanes(a, width):
@@ -283,13 +288,9 @@
     return basis[0]
 
 
-def finish_kernel(n_tm, g_ref, w_ref, out_ref, part_ref, buf, send, recv, own):
+def finish_body(n_tm, g_ref, w_ref, out_ref, part_ref, buf, send, recv, own):
     s = lax.axis_index("space")
     t = lax.axis_index("tm")
-    barrier = pltpu.get_barrier_semaphore()
-    for k in range(1, n_tm):
-        a = lax.rem(t + k, n_tm)
-        pl.semaphore_signal(barrier, inc=1, device_id=(s, a), device_id_type=MESH)
     basis_t = tree_levels(g_ref)
     hi = basis_t.astype(jnp.bfloat16)
     rest = basis_t - hi.astype(jnp.float32)
@@ -303,7 +304,6 @@
     width = w_ref.shape[2]
     src_at = lambda a: part_ref.at[:, pl.ds(a * share, share), :]
     dst_at = lambda j: buf.at[:, :, lanes(j, width)]
-    pl.semaphore_wait(barrier, n_tm - 1)
     copies = []
     for k in range(1, n_tm):
         a = lax.rem(t + k, n_tm)
@@ -325,27 +325,6 @@
     for c in copies:
         c.wait_send()
     out_ref[...] = buf[...]
-
-
-def finish(gram, cells_x):
-    n_tm = lax.axis_size("tm")
-    rows, _, width = cells_x.shape
-    share = RANK // n_tm
-    out_shape = (rows, share, width * n_tm)
-    return pl.pallas_call(
-        functools.partial(finish_kernel, n_tm),
-        out_shape=jax.ShapeDtypeStruct(out_shape, jnp.float32),
-        in_specs=[pl.BlockSpec(memory_space=pltpu.VMEM)] * 2,
-        out_specs=pl.BlockSpec(memory_space=pltpu.VMEM),
-        scratch_shapes=[
-            pltpu.VMEM((rows, RANK, width), jnp.float32),
-            pltpu.VMEM(out_shape, jnp.float32),
-            pltpu.SemaphoreType.DMA((n_tm,)),
-            pltpu.SemaphoreType.DMA((n_tm,)),
-            pltpu.SemaphoreType.DMA((1,)),
-        ],
-        compiler_params=pltpu.CompilerParams(collective_id=2, has_side_effects=True),
-    )(gram, cells_x)
 
 
 def local(velocity):
@@ -361,8 +340,7 @@
     cols = vorticity.shape[2]
     width = cols // blocks
     vort_x = jnp.swapaxes(vorticity, 0, 1)
-    cells_x, gram = front(vort_x)
-    modes = jnp.swapaxes(finish(gram, cells_x), 0, 1)
+    modes = jnp.swapaxes(front(vort_x), 0, 1)
     return (vorticity, modes)
 
 

time: 98.1 us -> 96.4 us (0.983)
  Pallas kernels: 81.2 us -> 79.5 us
    pallas_call x1 -> x0, Pallas kernels: 23.8 us -> none  [finish(): pl.pallas_call(functools.partial(finish_kernel, n_tm), out_shape=jax.Shap...]
    pallas_call x1, Pallas kernels: 57.4 us -> 79.5 us  [front(): pl.pallas_call(functools.partial(front_kernel, n_space, n_tm), out_shape=...]
where the time goes in v12:
time: 96.4 us; the launch traced here: 96.2 us
  Pallas kernels  79.5 us (82%)
  local copies, waits for them, and re-layouts  6.9 us (7%)
  other arithmetic  3.77 us (4%)
  starting transfers between devices  3.59 us (4%)
  waiting for transfers between devices  1.74 us (2%)
    pallas_call x1, Pallas kernels, front(): pl.pallas_call(functools.partial(front_kernel, n_space, n_tm), out_shape=...  79.5 us
    unnamed x4, local copies, waits for them, and re-layouts  3.36 us
    ppermute x1, starting transfers between devices, halo_rows(): low = lax.ppermute(block[:, rows - width:], 'space', forward)  2.76 us
    convert_element_type x1, other arithmetic, local(): vorticity = (dv_dx - spanwise(stream_u)).astype(jnp.bfloat16)  2.38 us
  transfers between devices with their start and end apart: 2, of which 1 were waited for; matrix products, arithmetic and copies ran while one was open for 2% of the time, Pallas kernels for 0%

profile of v12, /device:TPU:1, one launch (start us, length us, event | category | flops | bytes accessed | tf_op | source)
XLA Modules:
  0.0 96.2 jit_solution(17297484132701280275)
XLA Ops:
  0.6 1.7 %fusion.13 = (bf16[32,1,16,1024]{3,2,1,0:T(8,128)(2,1)S(1)}, bf16[32,1,16,1024]{3,2,1,0:T(8,128)(2,1)S(1)}) fusion(bf16[32,2,16,1024]{3,2,1,0:T(8,128)(2,1)} %param.1), kind=kLoop, calls=%fused_computation.20 | loop fusion | bytes 4194304 | tf_op jit(solution)/shard_map/slice | solution.py:333
  2.4 1.2 %fusion.8 = (f32[32,16,1024]{2,0,1:T(8,128)S(1)}, bf16[32,16,1024]{2,0,1:T(8,128)(2,1)S(1)}) fusion(bf16[32,1,16,1024]{3,2,1,0:T(8,128)(2,1)S(1)} %get-tuple-element.12, bf16[32,1,16,1024]{3,2,1,0:T(8,128)(2,1)S(1)} %get-tuple-element.13), kind=kLoop, calls=%fused_computation.14 | loop fusion | flops 524288 | bytes 5242880 | tf_op jit(solution)/shard_map/convert_element_type | solution.py:333
  3.6 2.8 %collective-permute-start = (bf16[32,2,1024]{2,0,1:T(8,128)(2,1)S(1)}, bf16[32,2,1024]{2,0,1:T(8,128)(2,1)S(1)}, u32[]{:S(2)}, u32[]{:S(2)}) collective-permute-start(bf16[32,2,1024]{2,0,1:T(8,128)(2,1)S(1)} %get-tuple-element.14), channel_id=1, source_target_pairs={{0,8},{8,16},{16,24},{24,32},{32,40},{40,48},{48,56},{56,64},{64,7... | collective-permute-start | bytes 393224 | tf_op jit(solution)/shard_map/ppermute | solution.py:19
  6.3 0.8 collective-permute-start.1
  7.2 0.1 fusion.11
  7.3 0.8 fusion.12
  8.1 0.8 fusion.10
  8.8 0.1 fusion.9
  9.0 0.0 collective-permute-done
  9.0 1.7 %collective-permute-done.1 = bf16[32,2,1024]{2,0,1:T(8,128)(2,1)S(1)} collective-permute-done((bf16[32,2,1024]{2,0,1:T(8,128)(2,1)S(1)}, bf16[32,2,1024]{2,0,1:T(8,128)(2,1)S(1)}, u32[]{:S(2)}, u32[]{:S(2)}) %collective-permute-start.1) | collective-permute-done | bytes 131104 | tf_op jit(solution)/shard_map/ppermute | solution.py:20
  10.7 0.2 maximum_convert_fusion
  10.9 2.4 %fusion.3 = bf16[32,16,1024]{2,0,1:T(8,128)(2,1)S(1)} fusion(f32[32,20,1024]{2,0,1:T(8,128)S(1)} %maximum_convert_fusion, f32[32,16,1]{2,0,1:T(8,128)S(1)} %get-tuple-element.9, f32[32,16,1023]{2,0,1:T(8,128)S(1)} %get-tuple-element.11, f32[32,16,1023]{2,0,1:T(8,128)S(1)} %get-tuple-element.10, f32[32,16,1]{2,0,1:T(8,128)S(1)} %get-tuple-element.8, ...), kind=kLoop, calls=%fused_computation.4 | loop fusion | flops 8388608 | bytes 17825792 | tf_op jit(solution)/shard_map/convert_element_type | solution.py:338
  13.3 0.0 copy-start
  13.3 1.5 %copy.5 = bf16[32,16,1024]{2,1,0:T(8,128)(2,1)} copy(bf16[32,16,1024]{2,0,1:T(8,128)(2,1)S(1)} %fusion.3) | data formatting | bytes 2097152
  14.9 0.0 copy-done
  14.9 79.5 %shard_map.30 = f32[16,4,1024]{2,1,0:T(4,128)} custom-call(bf16[16,32,1024]{2,1,0:T(8,128)(2,1)} %bitcast.9), custom_call_target="tpu_custom_call" | custom-call | tf_op jit(solution)/shard_map/pallas_call | solution.py:191
  94.4 1.8 %copy.6 = f32[4,16,1024]{2,1,0:T(8,128)} copy(f32[4,16,1024]{2,0,1:T(4,128)} %bitcast.10) | data formatting | bytes 524288
  (1 shorter events, 0.0 us)
Async XLA Ops:
  3.6 5.4 %collective-permute-start = (bf16[32,2,1024]{2,0,1:T(8,128)(2,1)S(1)}, bf16[32,2,1024]{2,0,1:T(8,128)(2,1)S(1)}, u32[]{:S(2)}, u32[]{:S(2)}) collective-permute-start(bf16[32,2,1024]{2,0,1:T(8,128)(2,1)S(1)} %get-tuple-element.14), channel_id=1, source_target_pairs={{0,8},{8,16},{16,24},{24,32},{32,40},{40,48},{48,56},{56,64},{64,7... | collective-permute-start | bytes 393224 | tf_op jit(solution)/shard_map/ppermute | solution.py:19
  6.3 4.4 %collective-permute-start.1 = (bf16[32,2,1024]{2,0,1:T(8,128)(2,1)S(1)}, bf16[32,2,1024]{2,0,1:T(8,128)(2,1)S(1)}, u32[]{:S(2)}, u32[]{:S(2)}) collective-permute-start(bf16[32,2,1024]{2,0,1:T(8,128)(2,1)S(1)} %get-tuple-element.15), channel_id=1, source_target_pairs={{8,0},{16,8},{24,16},{32,24},{40,32},{48,40},{56,48},{64,56},{72,6... | collective-permute-start | bytes 393224 | tf_op jit(solution)/shard_map/ppermute | solution.py:20
  13.3 1.6 %copy-start = (bf16[32,16,1024]{2,0,1:T(8,128)(2,1)}, bf16[32,16,1024]{2,0,1:T(8,128)(2,1)S(1)}, u32[]{:S(2)}) copy-start(bf16[32,16,1024]{2,0,1:T(8,128)(2,1)S(1)} %fusion.3) | copy-start | bytes 3145732

commit v13 on v12

--- a/solution.py
+++ b/solution.py
@@ -127,7 +127,8 @@
         return carry
 
     lax.fori_loop(1, n_space, drain, 0)
-    out_ref[...] = buf3[...]
+    if out_ref is not None:
+        out_ref[...] = buf3[...]
 
 
 def a2a_body(n_tm, src_at, dst_at, x_ref, buf, send, recv, own):
@@ -155,7 +156,7 @@
         c.wait_send()
 
 
-def front_kernel(n_space, n_tm, x_ref, modes_ref, cells, gpart, buf1, buf2, buf3, gfull, part, gathered, *sems):
+def front_kernel(n_space, n_tm, x_ref, modes_ref, cells, gpart, buf1, buf2, buf3, part, gathered, *sems):
     send, recv, own = sems[:3]
     greet_all(n_space, n_tm)
     rows, _, cols = x_ref.shape
@@ -174,9 +175,8 @@
             w, w, (((1,), (1,)), ((), ())), preferred_element_type=jnp.float32
         )
     gpart[...] = gram.reshape(gpart.shape)
-    allreduce_body(n_space, n_tm, gpart, buf1, buf1, buf2, buf3, *sems[3:9])
-    gfull[...] = buf3[...].reshape(gfull.shape)
-    finish_body(n_tm, gfull, cells, modes_ref, part, gathered, *sems[9:])
+    allreduce_body(n_space, n_tm, gpart, None, buf1, buf2, buf3, *sems[3:9])
+    finish_body(n_tm, buf3, cells, modes_ref, part, gathered, *sems[9:])
 
 
 def front(vort_x):
@@ -199,7 +199,6 @@
             pltpu.VMEM(chunks, jnp.float32),
             pltpu.VMEM((n_tm,) + chunks[1:], jnp.float32),
             pltpu.VMEM(chunks, jnp.float32),
-            pltpu.VMEM((size, size), jnp.float32),
             pltpu.VMEM((rows, RANK, width), jnp.float32),
             pltpu.VMEM(out_shape, jnp.float32),
             pltpu.SemaphoreType.DMA((n_tm,)),
@@ -214,6 +213,7 @@
             pltpu.SemaphoreType.DMA((n_tm,)),
             pltpu.SemaphoreType.DMA((n_tm,)),
             pltpu.SemaphoreType.DMA((1,)),
+            pltpu.SemaphoreType.DMA((n_tm,)),
         ],
         compiler_params=pltpu.CompilerParams(collective_id=0, has_side_effects=True),
     )(vort_x)
@@ -263,13 +263,19 @@
     return bdot(x, jnp.where(col == row + offset, 1.0, 0.0))
 
 
+def g_rows(g_ref, r0, r1):
+    c = g_ref.shape[1]
+    lo, hi = r0 // c, -(-r1 // c)
+    return g_ref[lo:hi].reshape((hi - lo) * c, g_ref.shape[2])[r0 - lo * c : r1 - lo * c]
+
+
 def tree_levels(g_ref):
     size = 2 * RANK
-    leaves = g_ref.shape[0] // RANK
+    leaves = g_ref.shape[2] // RANK
     picks = []
     for k in range(leaves // 2):
         lane0 = (k * size) // 128 * 128
-        block = g_ref[k * size : (k + 1) * size, lane0 : lane0 + 128][None]
+        block = g_rows(g_ref, k * size, (k + 1) * size)[:, lane0 : lane0 + 128][None]
         picks.append(place(block, -(k * size - lane0), size))
     basis = merge_coeffs(jnp.concatenate(picks, axis=0))
     while basis.shape[0] > 1:
@@ -280,7 +286,7 @@
             [place(pairs[:, 0], 0, 2 * w), place(pairs[:, 1], w, 2 * w)], axis=1
         )
         gs = jnp.concatenate(
-            [g_ref[k * 2 * w : (k + 1) * 2 * w, k * 2 * w : (k + 1) * 2 * w][None] for k in range(n)],
+            [g_rows(g_ref, k * 2 * w, (k + 1) * 2 * w)[:, k * 2 * w : (k + 1) * 2 * w][None] for k in range(n)],
             axis=0,
         )
         h = bdot_t(bdot(bt, gs), bt)
@@ -288,7 +294,7 @@
     return basis[0]
 
 
-def finish_body(n_tm, g_ref, w_ref, out_ref, part_ref, buf, send, recv, own):
+def finish_body(n_tm, g_ref, w_ref, out_ref, part_ref, buf, send, recv, own, send_late):
     s = lax.axis_index("space")
     t = lax.axis_index("tm")
     basis_t = tree_levels(g_ref)
@@ -297,29 +303,32 @@
     mid = rest.astype(jnp.bfloat16)
     lo = (rest - mid.astype(jnp.float32)).astype(jnp.bfloat16)
     pieces = jnp.concatenate([hi, mid, lo], axis=0)
-    for x in range(w_ref.shape[0]):
-        terms = jnp.dot(pieces, w_ref[x], preferred_element_type=jnp.float32)
-        part_ref[x] = (terms[:RANK] + terms[RANK : 2 * RANK]) + terms[2 * RANK :]
+    rows = w_ref.shape[0]
     share = part_ref.shape[1] // n_tm
     width = w_ref.shape[2]
-    src_at = lambda a: part_ref.at[:, pl.ds(a * share, share), :]
-    dst_at = lambda j: buf.at[:, :, lanes(j, width)]
+    src_at = lambda a, r0, nr: part_ref.at[pl.ds(r0, nr), pl.ds(a * share, share), :]
+    dst_at = lambda j, r0, nr: buf.at[pl.ds(r0, nr), :, lanes(j, width)]
+    halves = ((0, rows // 2, send), (rows // 2, rows - rows // 2, send_late))
     copies = []
-    for k in range(1, n_tm):
-        a = lax.rem(t + k, n_tm)
-        c = pltpu.make_async_remote_copy(
-            src_ref=src_at(a), dst_ref=dst_at(t), send_sem=send.at[k], recv_sem=recv.at[t],
-            device_id=(s, a), device_id_type=MESH,
-        )
-        c.start()
-        copies.append(c)
-    mine = pltpu.make_async_copy(src_at(t), dst_at(t), own.at[0])
+    for r0, nr, sems in halves:
+        for x in range(r0, r0 + nr):
+            terms = jnp.dot(pieces, w_ref[x], preferred_element_type=jnp.float32)
+            part_ref[x] = (terms[:RANK] + terms[RANK : 2 * RANK]) + terms[2 * RANK :]
+        for k in range(1, n_tm):
+            a = lax.rem(t + k, n_tm)
+            c = pltpu.make_async_remote_copy(
+                src_ref=src_at(a, r0, nr), dst_ref=dst_at(t, r0, nr), send_sem=sems.at[k], recv_sem=recv.at[t],
+                device_id=(s, a), device_id_type=MESH,
+            )
+            c.start()
+            copies.append(c)
+    mine = pltpu.make_async_copy(src_at(t, 0, rows), dst_at(t, 0, rows), own.at[0])
     mine.start()
     mine.wait()
     for k in range(1, n_tm):
         j = lax.rem(t + k, n_tm)
         pltpu.make_async_remote_copy(
-            src_ref=src_at(j), dst_ref=dst_at(j), send_sem=send.at[k], recv_sem=recv.at[j],
+            src_ref=src_at(j, 0, rows), dst_ref=dst_at(j, 0, rows), send_sem=send.at[k], recv_sem=recv.at[j],
             device_id=(s, j), device_id_type=MESH,
         ).wait_recv()
     for c in copies:

time: 96.4 us -> 96.4 us (level)
  no operation moved by 1% of the time
where the time goes in v13:
time: 96.4 us; the launch traced here: 96.2 us
  Pallas kernels  79.5 us (82%)
  local copies, waits for them, and re-layouts  6.9 us (7%)
  other arithmetic  3.77 us (4%)
  starting transfers between devices  3.59 us (4%)
  waiting for transfers between devices  1.74 us (2%)
    pallas_call x1, Pallas kernels, front(): pl.pallas_call(functools.partial(front_kernel, n_space, n_tm), out_shape=...  79.5 us
    unnamed x4, local copies, waits for them, and re-layouts  3.36 us
    ppermute x1, starting transfers between devices, halo_rows(): low = lax.ppermute(block[:, rows - width:], 'space', forward)  2.76 us
    convert_element_type x1, other arithmetic, local(): vorticity = (dv_dx - spanwise(stream_u)).astype(jnp.bfloat16)  2.38 us
  transfers between devices with their start and end apart: 2, of which 1 were waited for; matrix products, arithmetic and copies ran while one was open for 2% of the time, Pallas kernels for 0%

profile of v13, /device:TPU:1, one launch (start us, length us, event | category | flops | bytes accessed | tf_op | source)
XLA Modules:
  0.0 96.2 jit_solution(15887565442855825075)
XLA Ops:
  0.6 1.7 %fusion.13 = (bf16[32,1,16,1024]{3,2,1,0:T(8,128)(2,1)S(1)}, bf16[32,1,16,1024]{3,2,1,0:T(8,128)(2,1)S(1)}) fusion(bf16[32,2,16,1024]{3,2,1,0:T(8,128)(2,1)} %param.1), kind=kLoop, calls=%fused_computation.20 | loop fusion | bytes 4194304 | tf_op jit(solution)/shard_map/slice | solution.py:342
  2.4 1.2 %fusion.8 = (f32[32,16,1024]{2,0,1:T(8,128)S(1)}, bf16[32,16,1024]{2,0,1:T(8,128)(2,1)S(1)}) fusion(bf16[32,1,16,1024]{3,2,1,0:T(8,128)(2,1)S(1)} %get-tuple-element.12, bf16[32,1,16,1024]{3,2,1,0:T(8,128)(2,1)S(1)} %get-tuple-element.13), kind=kLoop, calls=%fused_computation.14 | loop fusion | flops 524288 | bytes 5242880 | tf_op jit(solution)/shard_map/convert_element_type | solution.py:342
  3.6 2.8 %collective-permute-start = (bf16[32,2,1024]{2,0,1:T(8,128)(2,1)S(1)}, bf16[32,2,1024]{2,0,1:T(8,128)(2,1)S(1)}, u32[]{:S(2)}, u32[]{:S(2)}) collective-permute-start(bf16[32,2,1024]{2,0,1:T(8,128)(2,1)S(1)} %get-tuple-element.14), channel_id=1, source_target_pairs={{0,8},{8,16},{16,24},{24,32},{32,40},{40,48},{48,56},{56,64},{64,7... | collective-permute-start | bytes 393224 | tf_op jit(solution)/shard_map/ppermute | solution.py:19
  6.3 0.8 collective-permute-start.1
  7.2 0.1 fusion.11
  7.3 0.8 fusion.12
  8.1 0.8 fusion.10
  8.8 0.1 fusion.9
  9.0 0.0 collective-permute-done
  9.0 1.7 %collective-permute-done.1 = bf16[32,2,1024]{2,0,1:T(8,128)(2,1)S(1)} collective-permute-done((bf16[32,2,1024]{2,0,1:T(8,128)(2,1)S(1)}, bf16[32,2,1024]{2,0,1:T(8,128)(2,1)S(1)}, u32[]{:S(2)}, u32[]{:S(2)}) %collective-permute-start.1) | collective-permute-done | bytes 131104 | tf_op jit(solution)/shard_map/ppermute | solution.py:20
  10.7 0.2 maximum_convert_fusion
  10.9 2.4 %fusion.3 = bf16[32,16,1024]{2,0,1:T(8,128)(2,1)S(1)} fusion(f32[32,20,1024]{2,0,1:T(8,128)S(1)} %maximum_convert_fusion, f32[32,16,1]{2,0,1:T(8,128)S(1)} %get-tuple-element.9, f32[32,16,1023]{2,0,1:T(8,128)S(1)} %get-tuple-element.11, f32[32,16,1023]{2,0,1:T(8,128)S(1)} %get-tuple-element.10, f32[32,16,1]{2,0,1:T(8,128)S(1)} %get-tuple-element.8, ...), kind=kLoop, calls=%fused_computation.4 | loop fusion | flops 8388608 | bytes 17825792 | tf_op jit(solution)/shard_map/convert_element_type | solution.py:347
  13.3 0.0 copy-start
  13.3 1.5 %copy.5 = bf16[32,16,1024]{2,1,0:T(8,128)(2,1)} copy(bf16[32,16,1024]{2,0,1:T(8,128)(2,1)S(1)} %fusion.3) | data formatting | bytes 2097152
  14.9 0.0 copy-done
  14.9 79.5 %shard_map.30 = f32[16,4,1024]{2,1,0:T(4,128)} custom-call(bf16[16,32,1024]{2,1,0:T(8,128)(2,1)} %bitcast.9), custom_call_target="tpu_custom_call" | custom-call | tf_op jit(solution)/shard_map/pallas_call | solution.py:191
  94.4 1.8 %copy.6 = f32[4,16,1024]{2,1,0:T(8,128)} copy(f32[4,16,1024]{2,0,1:T(4,128)} %bitcast.10) | data formatting | bytes 524288
  (1 shorter events, 0.0 us)
Async XLA Ops:
  3.6 5.4 %collective-permute-start = (bf16[32,2,1024]{2,0,1:T(8,128)(2,1)S(1)}, bf16[32,2,1024]{2,0,1:T(8,128)(2,1)S(1)}, u32[]{:S(2)}, u32[]{:S(2)}) collective-permute-start(bf16[32,2,1024]{2,0,1:T(8,128)(2,1)S(1)} %get-tuple-element.14), channel_id=1, source_target_pairs={{0,8},{8,16},{16,24},{24,32},{32,40},{40,48},{48,56},{56,64},{64,7... | collective-permute-start | bytes 393224 | tf_op jit(solution)/shard_map/ppermute | solution.py:19
  6.3 4.4 %collective-permute-start.1 = (bf16[32,2,1024]{2,0,1:T(8,128)(2,1)S(1)}, bf16[32,2,1024]{2,0,1:T(8,128)(2,1)S(1)}, u32[]{:S(2)}, u32[]{:S(2)}) collective-permute-start(bf16[32,2,1024]{2,0,1:T(8,128)(2,1)S(1)} %get-tuple-element.15), channel_id=1, source_target_pairs={{8,0},{16,8},{24,16},{32,24},{40,32},{48,40},{56,48},{64,56},{72,6... | collective-permute-start | bytes 393224 | tf_op jit(solution)/shard_map/ppermute | solution.py:20
  13.3 1.6 %copy-start = (bf16[32,16,1024]{2,0,1:T(8,128)(2,1)}, bf16[32,16,1024]{2,0,1:T(8,128)(2,1)S(1)}, u32[]{:S(2)}) copy-start(bf16[32,16,1024]{2,0,1:T(8,128)(2,1)S(1)} %fusion.3) | copy-start | bytes 3145732

commit v14 on v12

--- a/solution.py
+++ b/solution.py
@@ -257,10 +257,22 @@
     return r * (scales / jnp.sqrt(diag_u))
 
 
+def split3(x):
+    hi = x.astype(jnp.bfloat16)
+    rest = x - hi.astype(jnp.float32)
+    mid = rest.astype(jnp.bfloat16)
+    lo = (rest - mid.astype(jnp.float32)).astype(jnp.bfloat16)
+    return hi, mid, lo
+
+
 def place(x, offset, width):
-    n, _, w = x.shape
+    n, r, w = x.shape
     row, col = iotas((n, w, width))
-    return bdot(x, jnp.where(col == row + offset, 1.0, 0.0))
+    pick = jnp.where(col == row + offset, 1.0, 0.0).astype(jnp.bfloat16)
+    terms = jnp.einsum(
+        "nab,nbc->nac", jnp.concatenate(split3(x), axis=1), pick, preferred_element_type=jnp.float32
+    )
+    return (terms[:, :r] + terms[:, r : 2 * r]) + terms[:, 2 * r :]
 
 
 def tree_levels(g_ref):

time: 96.4 us -> 96 us (level)
  no operation moved by 1% of the time
where the time goes in v14:
time: 96 us; the launch traced here: 95.8 us
  Pallas kernels  79.1 us (82%)
  local copies, waits for them, and re-layouts  6.9 us (7%)
  other arithmetic  3.77 us (4%)
  starting transfers between devices  3.59 us (4%)
  waiting for transfers between devices  1.74 us (2%)
    pallas_call x1, Pallas kernels, front(): pl.pallas_call(functools.partial(front_kernel, n_space, n_tm), out_shape=...  79.1 us
    unnamed x4, local copies, waits for them, and re-layouts  3.36 us
    ppermute x1, starting transfers between devices, halo_rows(): low = lax.ppermute(block[:, rows - width:], 'space', forward)  2.76 us
    convert_element_type x1, other arithmetic, local(): vorticity = (dv_dx - spanwise(stream_u)).astype(jnp.bfloat16)  2.38 us
  transfers between devices with their start and end apart: 2, of which 1 were waited for; matrix products, arithmetic and copies ran while one was open for 2% of the time, Pallas kernels for 0%

profile of v14, /device:TPU:1, one launch (start us, length us, event | category | flops | bytes accessed | tf_op | source)
XLA Modules:
  0.0 95.8 jit_solution(9986688614368218940)
XLA Ops:
  0.6 1.7 %fusion.13 = (bf16[32,1,16,1024]{3,2,1,0:T(8,128)(2,1)S(1)}, bf16[32,1,16,1024]{3,2,1,0:T(8,128)(2,1)S(1)}) fusion(bf16[32,2,16,1024]{3,2,1,0:T(8,128)(2,1)} %param.1), kind=kLoop, calls=%fused_computation.20 | loop fusion | bytes 4194304 | tf_op jit(solution)/shard_map/slice | solution.py:345
  2.4 1.2 %fusion.8 = (f32[32,16,1024]{2,0,1:T(8,128)S(1)}, bf16[32,16,1024]{2,0,1:T(8,128)(2,1)S(1)}) fusion(bf16[32,1,16,1024]{3,2,1,0:T(8,128)(2,1)S(1)} %get-tuple-element.12, bf16[32,1,16,1024]{3,2,1,0:T(8,128)(2,1)S(1)} %get-tuple-element.13), kind=kLoop, calls=%fused_computation.14 | loop fusion | flops 524288 | bytes 5242880 | tf_op jit(solution)/shard_map/convert_element_type | solution.py:345
  3.6 2.8 %collective-permute-start = (bf16[32,2,1024]{2,0,1:T(8,128)(2,1)S(1)}, bf16[32,2,1024]{2,0,1:T(8,128)(2,1)S(1)}, u32[]{:S(2)}, u32[]{:S(2)}) collective-permute-start(bf16[32,2,1024]{2,0,1:T(8,128)(2,1)S(1)} %get-tuple-element.14), channel_id=1, source_target_pairs={{0,8},{8,16},{16,24},{24,32},{32,40},{40,48},{48,56},{56,64},{64,7... | collective-permute-start | bytes 393224 | tf_op jit(solution)/shard_map/ppermute | solution.py:19
  6.3 0.8 collective-permute-start.1
  7.2 0.1 fusion.11
  7.3 0.8 fusion.12
  8.1 0.8 fusion.10
  8.8 0.1 fusion.9
  9.0 0.0 collective-permute-done
  9.0 1.7 %collective-permute-done.1 = bf16[32,2,1024]{2,0,1:T(8,128)(2,1)S(1)} collective-permute-done((bf16[32,2,1024]{2,0,1:T(8,128)(2,1)S(1)}, bf16[32,2,1024]{2,0,1:T(8,128)(2,1)S(1)}, u32[]{:S(2)}, u32[]{:S(2)}) %collective-permute-start.1) | collective-permute-done | bytes 131104 | tf_op jit(solution)/shard_map/ppermute | solution.py:20
  10.7 0.2 maximum_convert_fusion
  10.9 2.4 %fusion.3 = bf16[32,16,1024]{2,0,1:T(8,128)(2,1)S(1)} fusion(f32[32,20,1024]{2,0,1:T(8,128)S(1)} %maximum_convert_fusion, f32[32,16,1]{2,0,1:T(8,128)S(1)} %get-tuple-element.9, f32[32,16,1023]{2,0,1:T(8,128)S(1)} %get-tuple-element.11, f32[32,16,1023]{2,0,1:T(8,128)S(1)} %get-tuple-element.10, f32[32,16,1]{2,0,1:T(8,128)S(1)} %get-tuple-element.8, ...), kind=kLoop, calls=%fused_computation.4 | loop fusion | flops 8388608 | bytes 17825792 | tf_op jit(solution)/shard_map/convert_element_type | solution.py:350
  13.3 0.0 copy-start
  13.3 1.5 %copy.5 = bf16[32,16,1024]{2,1,0:T(8,128)(2,1)} copy(bf16[32,16,1024]{2,0,1:T(8,128)(2,1)S(1)} %fusion.3) | data formatting | bytes 2097152
  14.9 0.0 copy-done
  14.9 79.1 %shard_map.30 = f32[16,4,1024]{2,1,0:T(4,128)} custom-call(bf16[16,32,1024]{2,1,0:T(8,128)(2,1)} %bitcast.9), custom_call_target="tpu_custom_call" | custom-call | tf_op jit(solution)/shard_map/pallas_call | solution.py:191
  94.0 1.8 %copy.6 = f32[4,16,1024]{2,1,0:T(8,128)} copy(f32[4,16,1024]{2,0,1:T(4,128)} %bitcast.10) | data formatting | bytes 524288
  (1 shorter events, 0.0 us)
Async XLA Ops:
  3.6 5.4 %collective-permute-start = (bf16[32,2,1024]{2,0,1:T(8,128)(2,1)S(1)}, bf16[32,2,1024]{2,0,1:T(8,128)(2,1)S(1)}, u32[]{:S(2)}, u32[]{:S(2)}) collective-permute-start(bf16[32,2,1024]{2,0,1:T(8,128)(2,1)S(1)} %get-tuple-element.14), channel_id=1, source_target_pairs={{0,8},{8,16},{16,24},{24,32},{32,40},{40,48},{48,56},{56,64},{64,7... | collective-permute-start | bytes 393224 | tf_op jit(solution)/shard_map/ppermute | solution.py:19
  6.3 4.4 %collective-permute-start.1 = (bf16[32,2,1024]{2,0,1:T(8,128)(2,1)S(1)}, bf16[32,2,1024]{2,0,1:T(8,128)(2,1)S(1)}, u32[]{:S(2)}, u32[]{:S(2)}) collective-permute-start(bf16[32,2,1024]{2,0,1:T(8,128)(2,1)S(1)} %get-tuple-element.15), channel_id=1, source_target_pairs={{8,0},{16,8},{24,16},{32,24},{40,32},{48,40},{56,48},{64,56},{72,6... | collective-permute-start | bytes 393224 | tf_op jit(solution)/shard_map/ppermute | solution.py:20
  13.3 1.6 %copy-start = (bf16[32,16,1024]{2,0,1:T(8,128)(2,1)}, bf16[32,16,1024]{2,0,1:T(8,128)(2,1)S(1)}, u32[]{:S(2)}) copy-start(bf16[32,16,1024]{2,0,1:T(8,128)(2,1)S(1)} %fusion.3) | copy-start | bytes 3145732

commit v15 on v14

--- a/solution.py
+++ b/solution.py
@@ -187,7 +187,7 @@
     width = cols // n_tm
     cells_shape = (rows, size, width)
     chunks = (n_space, size // n_space, size)
-    out_shape = (rows, RANK // n_tm, cols)
+    out_shape = (RANK // n_tm, rows, cols)
     return pl.pallas_call(
         functools.partial(front_kernel, n_space, n_tm),
         out_shape=jax.ShapeDtypeStruct(out_shape, jnp.float32),
@@ -200,7 +200,7 @@
             pltpu.VMEM((n_tm,) + chunks[1:], jnp.float32),
             pltpu.VMEM(chunks, jnp.float32),
             pltpu.VMEM((size, size), jnp.float32),
-            pltpu.VMEM((rows, RANK, width), jnp.float32),
+            pltpu.VMEM((RANK, rows, width), jnp.float32),
             pltpu.VMEM(out_shape, jnp.float32),
             pltpu.SemaphoreType.DMA((n_tm,)),
             pltpu.SemaphoreType.DMA((n_tm,)),
@@ -311,10 +311,10 @@
     pieces = jnp.concatenate([hi, mid, lo], axis=0)
     for x in range(w_ref.shape[0]):
         terms = jnp.dot(pieces, w_ref[x], preferred_element_type=jnp.float32)
-        part_ref[x] = (terms[:RANK] + terms[RANK : 2 * RANK]) + terms[2 * RANK :]
-    share = part_ref.shape[1] // n_tm
+        part_ref[:, x, :] = (terms[:RANK] + terms[RANK : 2 * RANK]) + terms[2 * RANK :]
+    share = part_ref.shape[0] // n_tm
     width = w_ref.shape[2]
-    src_at = lambda a: part_ref.at[:, pl.ds(a * share, share), :]
+    src_at = lambda a: part_ref.at[pl.ds(a * share, share)]
     dst_at = lambda j: buf.at[:, :, lanes(j, width)]
     copies = []
     for k in range(1, n_tm):
@@ -352,7 +352,7 @@
     cols = vorticity.shape[2]
     width = cols // blocks
     vort_x = jnp.swapaxes(vorticity, 0, 1)
-    modes = jnp.swapaxes(front(vort_x), 0, 1)
+    modes = front(vort_x)
     return (vorticity, modes)
 
 

time: 96 us -> 95.8 us (level)
  no operation moved by 1% of the time
where the time goes in v15:
time: 95.8 us; the launch traced here: 95.6 us
  Pallas kernels  79.1 us (83%)
  local copies, waits for them, and re-layouts  6.76 us (7%)
  other arithmetic  3.77 us (4%)
  starting transfers between devices  3.59 us (4%)
  waiting for transfers between devices  1.74 us (2%)
    pallas_call x1, Pallas kernels, front(): pl.pallas_call(functools.partial(front_kernel, n_space, n_tm), out_shape=...  79.1 us
    unnamed x4, local copies, waits for them, and re-layouts  3.22 us
    ppermute x1, starting transfers between devices, halo_rows(): low = lax.ppermute(block[:, rows - width:], 'space', forward)  2.76 us
    convert_element_type x1, other arithmetic, local(): vorticity = (dv_dx - spanwise(stream_u)).astype(jnp.bfloat16)  2.38 us
  transfers between devices with their start and end apart: 2, of which 1 were waited for; matrix products, arithmetic and copies ran while one was open for 2% of the time, Pallas kernels for 0%

profile of v15, /device:TPU:1, one launch (start us, length us, event | category | flops | bytes accessed | tf_op | source)
XLA Modules:
  0.0 95.6 jit_solution(6042077292904723896)
XLA Ops:
  0.6 1.7 %fusion.13 = (bf16[32,1,16,1024]{3,2,1,0:T(8,128)(2,1)S(1)}, bf16[32,1,16,1024]{3,2,1,0:T(8,128)(2,1)S(1)}) fusion(bf16[32,2,16,1024]{3,2,1,0:T(8,128)(2,1)} %param.1), kind=kLoop, calls=%fused_computation.20 | loop fusion | bytes 4194304 | tf_op jit(solution)/shard_map/slice | solution.py:345
  2.4 1.2 %fusion.8 = (f32[32,16,1024]{2,0,1:T(8,128)S(1)}, bf16[32,16,1024]{2,0,1:T(8,128)(2,1)S(1)}) fusion(bf16[32,1,16,1024]{3,2,1,0:T(8,128)(2,1)S(1)} %get-tuple-element.12, bf16[32,1,16,1024]{3,2,1,0:T(8,128)(2,1)S(1)} %get-tuple-element.13), kind=kLoop, calls=%fused_computation.14 | loop fusion | flops 524288 | bytes 5242880 | tf_op jit(solution)/shard_map/convert_element_type | solution.py:345
  3.6 2.8 %collective-permute-start = (bf16[32,2,1024]{2,0,1:T(8,128)(2,1)S(1)}, bf16[32,2,1024]{2,0,1:T(8,128)(2,1)S(1)}, u32[]{:S(2)}, u32[]{:S(2)}) collective-permute-start(bf16[32,2,1024]{2,0,1:T(8,128)(2,1)S(1)} %get-tuple-element.14), channel_id=1, source_target_pairs={{0,8},{8,16},{16,24},{24,32},{32,40},{40,48},{48,56},{56,64},{64,7... | collective-permute-start | bytes 393224 | tf_op jit(solution)/shard_map/ppermute | solution.py:19
  6.3 0.8 collective-permute-start.1
  7.2 0.1 fusion.11
  7.3 0.8 fusion.12
  8.1 0.8 fusion.10
  8.8 0.1 fusion.9
  9.0 0.0 collective-permute-done
  9.0 1.7 %collective-permute-done.1 = bf16[32,2,1024]{2,0,1:T(8,128)(2,1)S(1)} collective-permute-done((bf16[32,2,1024]{2,0,1:T(8,128)(2,1)S(1)}, bf16[32,2,1024]{2,0,1:T(8,128)(2,1)S(1)}, u32[]{:S(2)}, u32[]{:S(2)}) %collective-permute-start.1) | collective-permute-done | bytes 131104 | tf_op jit(solution)/shard_map/ppermute | solution.py:20
  10.7 0.2 maximum_convert_fusion
  10.9 2.4 %fusion.3 = bf16[32,16,1024]{2,0,1:T(8,128)(2,1)S(1)} fusion(f32[32,20,1024]{2,0,1:T(8,128)S(1)} %maximum_convert_fusion, f32[32,16,1]{2,0,1:T(8,128)S(1)} %get-tuple-element.9, f32[32,16,1023]{2,0,1:T(8,128)S(1)} %get-tuple-element.11, f32[32,16,1023]{2,0,1:T(8,128)S(1)} %get-tuple-element.10, f32[32,16,1]{2,0,1:T(8,128)S(1)} %get-tuple-element.8, ...), kind=kLoop, calls=%fused_computation.4 | loop fusion | flops 8388608 | bytes 17825792 | tf_op jit(solution)/shard_map/convert_element_type | solution.py:350
  13.3 0.0 copy-start
  13.3 1.5 %copy.5 = bf16[32,16,1024]{2,1,0:T(8,128)(2,1)} copy(bf16[32,16,1024]{2,0,1:T(8,128)(2,1)S(1)} %fusion.3) | data formatting | bytes 2097152
  14.9 0.0 copy-done
  14.9 79.1 %shard_map.30 = f32[4,16,1024]{2,1,0:T(8,128)} custom-call(bf16[16,32,1024]{2,1,0:T(8,128)(2,1)} %bitcast.8), custom_call_target="tpu_custom_call" | custom-call | tf_op jit(solution)/shard_map/pallas_call | solution.py:191
  94.0 1.7 %copy.13 = f32[4,16,1024]{2,1,0:T(8,128)} copy(f32[4,16,1024]{2,1,0:T(8,128)} %shard_map.30) | data formatting | bytes 524288
  (1 shorter events, 0.0 us)
Async XLA Ops:
  3.6 5.4 %collective-permute-start = (bf16[32,2,1024]{2,0,1:T(8,128)(2,1)S(1)}, bf16[32,2,1024]{2,0,1:T(8,128)(2,1)S(1)}, u32[]{:S(2)}, u32[]{:S(2)}) collective-permute-start(bf16[32,2,1024]{2,0,1:T(8,128)(2,1)S(1)} %get-tuple-element.14), channel_id=1, source_target_pairs={{0,8},{8,16},{16,24},{24,32},{32,40},{40,48},{48,56},{56,64},{64,7... | collective-permute-start | bytes 393224 | tf_op jit(solution)/shard_map/ppermute | solution.py:19
  6.3 4.4 %collective-permute-start.1 = (bf16[32,2,1024]{2,0,1:T(8,128)(2,1)S(1)}, bf16[32,2,1024]{2,0,1:T(8,128)(2,1)S(1)}, u32[]{:S(2)}, u32[]{:S(2)}) collective-permute-start(bf16[32,2,1024]{2,0,1:T(8,128)(2,1)S(1)} %get-tuple-element.15), channel_id=1, source_target_pairs={{8,0},{16,8},{24,16},{32,24},{40,32},{48,40},{56,48},{64,56},{72,6... | collective-permute-start | bytes 393224 | tf_op jit(solution)/shard_map/ppermute | solution.py:20
  13.3 1.6 %copy-start = (bf16[32,16,1024]{2,0,1:T(8,128)(2,1)}, bf16[32,16,1024]{2,0,1:T(8,128)(2,1)S(1)}, u32[]{:S(2)}) copy-start(bf16[32,16,1024]{2,0,1:T(8,128)(2,1)S(1)} %fusion.3) | copy-start | bytes 3145732

commit v16 on v14

--- a/solution.py
+++ b/solution.py
@@ -155,17 +155,77 @@
         c.wait_send()
 
 
-def front_kernel(n_space, n_tm, x_ref, modes_ref, cells, gpart, buf1, buf2, buf3, gfull, part, gathered, *sems):
-    send, recv, own = sems[:3]
+def fix_edges(vloc_ref, dudz_ref, halo, fix):
+    f = lambda ref, i: ref[i].astype(jnp.float32)
+    d = lambda ahead, behind, ahead_two, behind_two: (8.0 * (ahead - behind) - (ahead_two - behind_two)) / 12.0
+    v = [f(vloc_ref, i) for i in range(8)]
+    lo = [f(halo, 0), f(halo, 1)]
+    hi = [f(halo, 2), f(halo, 3)]
+    rows_dv = [
+        d(v[1], lo[1], v[2], lo[0]),
+        d(v[2], v[0], v[3], lo[1]),
+        d(v[7], v[5], hi[0], v[4]),
+        d(hi[0], v[6], hi[1], v[5]),
+    ]
+    for i in range(4):
+        fix[i] = (rows_dv[i] - dudz_ref[i]).astype(fix.dtype)
+
+
+def front_kernel(
+    n_space, n_tm, x_ref, vloc_ref, dudz_ref, modes_ref, fixed_ref,
+    cells, gpart, buf1, buf2, buf3, gfull, part, gathered, halo, fix, *sems,
+):
+    send, recv, own, esend, hsend, hrecv = sems[:6]
+    s = lax.axis_index("space")
+    t = lax.axis_index("tm")
     greet_all(n_space, n_tm)
     rows, _, cols = x_ref.shape
     width = cols // n_tm
-    a2a_body(
-        n_tm,
-        lambda ref, a: ref.at[:, :, lanes(a, width)],
-        lambda ref, j: ref.at[:, pl.ds(j * RANK, RANK), :],
-        x_ref, cells, send, recv, own,
-    )
+    left = lax.rem(s + n_space - 1, n_space)
+    right = lax.rem(s + 1, n_space)
+
+    def remote(src_ref, dst_ref, ss, rs, dev):
+        return pltpu.make_async_remote_copy(
+            src_ref=src_ref, dst_ref=dst_ref, send_sem=ss, recv_sem=rs, device_id=dev, device_id_type=MESH
+        )
+
+    halo_out = [
+        remote(vloc_ref.at[pl.ds(6, 2)], halo.at[pl.ds(0, 2)], hsend.at[0], hrecv.at[0], (right, t)),
+        remote(vloc_ref.at[pl.ds(0, 2)], halo.at[pl.ds(2, 2)], hsend.at[1], hrecv.at[1], (left, t)),
+    ]
+    for c in halo_out:
+        c.start()
+    src = lambda ref, a, r0, nr: ref.at[pl.ds(r0, nr), :, lanes(a, width)]
+    dst = lambda j, r0, nr: cells.at[pl.ds(r0, nr), pl.ds(j * RANK, RANK), :]
+    inner = rows - 4
+    copies = []
+    for k in range(1, n_tm):
+        a = lax.rem(t + k, n_tm)
+        c = remote(src(x_ref, a, 2, inner), dst(t, 2, inner), send.at[k], recv.at[t], (s, a))
+        c.start()
+        copies.append(c)
+    mine = pltpu.make_async_copy(src(x_ref, t, 2, inner), dst(t, 2, inner), own.at[0])
+    mine.start()
+    mine.wait()
+    remote(vloc_ref.at[pl.ds(6, 2)], halo.at[pl.ds(0, 2)], hsend.at[0], hrecv.at[0], (left, t)).wait_recv()
+    remote(vloc_ref.at[pl.ds(0, 2)], halo.at[pl.ds(2, 2)], hsend.at[1], hrecv.at[1], (right, t)).wait_recv()
+    fix_edges(vloc_ref, dudz_ref, halo, fix)
+    fixed_ref[...] = fix[...]
+    for k in range(1, n_tm):
+        a = lax.rem(t + k, n_tm)
+        for e, (r0, d0) in enumerate(((0, 0), (2, rows - 2))):
+            c = remote(src(fix, a, r0, 2), dst(t, d0, 2), esend.at[k, e], recv.at[t], (s, a))
+            c.start()
+            copies.append(c)
+    for r0, d0 in ((0, 0), (2, rows - 2)):
+        mine = pltpu.make_async_copy(src(fix, t, r0, 2), dst(t, d0, 2), own.at[0])
+        mine.start()
+        mine.wait()
+    for k in range(1, n_tm):
+        j = lax.rem(t + k, n_tm)
+        remote(src(x_ref, j, 0, rows), dst(j, 0, rows), send.at[k], recv.at[j], (s, j)).wait_recv()
+    for c in copies + halo_out:
+        c.wait_send()
     size = cells.shape[1]
     gram = jnp.zeros((size, size), jnp.float32)
     for x in range(rows):
@@ -174,12 +234,12 @@
             w, w, (((1,), (1,)), ((), ())), preferred_element_type=jnp.float32
         )
     gpart[...] = gram.reshape(gpart.shape)
-    allreduce_body(n_space, n_tm, gpart, buf1, buf1, buf2, buf3, *sems[3:9])
+    allreduce_body(n_space, n_tm, gpart, buf1, buf1, buf2, buf3, *sems[6:12])
     gfull[...] = buf3[...].reshape(gfull.shape)
-    finish_body(n_tm, gfull, cells, modes_ref, part, gathered, *sems[9:])
-
-
-def front(vort_x):
+    finish_body(n_tm, gfull, cells, modes_ref, part, gathered, *sems[12:])
+
+
+def front(vort_x, vloc, dudz):
     n_space = lax.axis_size("space")
     n_tm = lax.axis_size("tm")
     rows, _, cols = vort_x.shape
@@ -188,11 +248,15 @@
     cells_shape = (rows, size, width)
     chunks = (n_space, size // n_space, size)
     out_shape = (rows, RANK // n_tm, cols)
+    edge_shape = (4, RANK, cols)
     return pl.pallas_call(
         functools.partial(front_kernel, n_space, n_tm),
-        out_shape=jax.ShapeDtypeStruct(out_shape, jnp.float32),
-        in_specs=[pl.BlockSpec(memory_space=pltpu.VMEM)],
-        out_specs=pl.BlockSpec(memory_space=pltpu.VMEM),
+        out_shape=(
+            jax.ShapeDtypeStruct(out_shape, jnp.float32),
+            jax.ShapeDtypeStruct(edge_shape, vort_x.dtype),
+        ),
+        in_specs=[pl.BlockSpec(memory_space=pltpu.VMEM)] * 3,
+        out_specs=(pl.BlockSpec(memory_space=pltpu.VMEM), pl.BlockSpec(memory_space=pltpu.VMEM)),
         scratch_shapes=[
             pltpu.VMEM(cells_shape, vort_x.dtype),
             pltpu.VMEM(chunks, jnp.float32),
@@ -202,9 +266,14 @@
             pltpu.VMEM((size, size), jnp.float32),
             pltpu.VMEM((rows, RANK, width), jnp.float32),
             pltpu.VMEM(out_shape, jnp.float32),
+            pltpu.VMEM(edge_shape, vort_x.dtype),
+            pltpu.VMEM(edge_shape, vort_x.dtype),
             pltpu.SemaphoreType.DMA((n_tm,)),
             pltpu.SemaphoreType.DMA((n_tm,)),
             pltpu.SemaphoreType.DMA((1,)),
+            pltpu.SemaphoreType.DMA((n_tm, 2)),
+            pltpu.SemaphoreType.DMA((2,)),
+            pltpu.SemaphoreType.DMA((2,)),
             pltpu.SemaphoreType.DMA((n_space,)),
             pltpu.SemaphoreType.DMA((n_space,)),
             pltpu.SemaphoreType.DMA((n_tm,)),
@@ -216,7 +285,7 @@
             pltpu.SemaphoreType.DMA((1,)),
         ],
         compiler_params=pltpu.CompilerParams(collective_id=0, has_side_effects=True),
-    )(vort_x)
+    )(vort_x, vloc, dudz)
 
 
 def lanes(a, width):
@@ -341,19 +410,20 @@
 
 def local(velocity):
     rows = velocity.shape[2]
-    span_v = halo_rows(velocity[:, 1], 2).astype(jnp.float32)
+    span_v = velocity[:, 1].astype(jnp.float32)
     stream_u = velocity[:, 0].astype(jnp.float32)
+    du_dz = spanwise(stream_u)
     dv_dx = (
-        8.0 * (span_v[:, 3 : rows + 3] - span_v[:, 1 : rows + 1])
-        - (span_v[:, 4:] - span_v[:, :rows])
+        8.0 * (jnp.roll(span_v, -1, 1) - jnp.roll(span_v, 1, 1))
+        - (jnp.roll(span_v, -2, 1) - jnp.roll(span_v, 2, 1))
     ) / 12.0
-    vorticity = (dv_dx - spanwise(stream_u)).astype(jnp.bfloat16)
-    blocks = lax.axis_size("tm")
-    cols = vorticity.shape[2]
-    width = cols // blocks
-    vort_x = jnp.swapaxes(vorticity, 0, 1)
-    modes = jnp.swapaxes(front(vort_x), 0, 1)
-    return (vorticity, modes)
+    local_vort = (dv_dx - du_dz).astype(jnp.bfloat16)
+    edge = [0, 1, rows - 2, rows - 1]
+    vloc = jnp.swapaxes(velocity[:, 1][:, [0, 1, 2, 3, rows - 4, rows - 3, rows - 2, rows - 1]], 0, 1)
+    dudz = jnp.swapaxes(du_dz[:, edge], 0, 1)
+    modes, fixed = front(jnp.swapaxes(local_vort, 0, 1), vloc, dudz)
+    vorticity = local_vort.at[:, edge].set(jnp.swapaxes(fixed, 0, 1))
+    return (vorticity, jnp.swapaxes(modes, 0, 1))
 
 
 def solution(mesh):

time: 96 us -> 102 us (1.062)
  local copies, waits for them, and re-layouts: 6.9 us -> 15.5 us
  other arithmetic: 3.77 us -> 7.49 us
  starting transfers between devices: 3.59 us -> 0 us
  waiting for transfers between devices: 1.74 us -> 0 us
    gather x0 -> x2, local copies, waits for them, and re-layouts: none -> 4.43 us  [the longest x1 3.06 us: local(): dudz = jnp.swapaxes(du_dz[:, edge], 0, 1)]
    ppermute x2 -> x0, starting transfers between devices: 3.59 us -> none  [the longest x1 2.76 us: halo_rows(): low = lax.ppermute(block[:, rows - width:], 'space', forward)]
    slice x5 -> x8, local copies, waits for them, and re-layouts: 1.81 us -> 5.32 us  [the longest x2 1.83 us: local(): jnp.roll(span_v, 1, 1)]
    squeeze x0 -> x1, other arithmetic: none -> 2.65 us  [local(): span_v = velocity[:, 1].astype(jnp.float32)]
    ppermute x2 -> x0, waiting for transfers between devices: 1.74 us -> none  [the longest x1 1.73 us: halo_rows(): high = lax.ppermute(block[:, :width], 'space', backward)]
    scatter x0 -> x1, local copies, waits for them, and re-layouts: none -> 1.58 us  [local(): vorticity = local_vort.at[:, edge].set(jnp.swapaxes(fixed, 0, 1))]
    gather x0 -> x2, other arithmetic: none -> 1.32 us  [the longest x1 0.66 us: local(): velocity[:, 1][:, [0, 1, 2, 3, rows - 4, rows - 3, rows - 2, rows - 1]]]
    unnamed x4 -> x10, local copies, waits for them, and re-layouts: 3.36 us -> 2.42 us
  transfers between devices with their start and end apart: 2 -> 0, of which waited for: 1 -> 0; matrix products, arithmetic and copies ran while one was open for 2% -> 0% of each run, Pallas kernels for 0% -> 0%
where the time goes in v16:
time: 102 us
  Pallas kernels  78.4 us (77%)
  local copies, waits for them, and re-layouts  15.5 us (15%)
  other arithmetic  7.49 us (7%)
    pallas_call x1, Pallas kernels, front(): pl.pallas_call(functools.partial(front_kernel, n_space, n_tm), out_shape=...  78.4 us
    convert_element_type x1, other arithmetic, local(): local_vort = (dv_dx - du_dz).astype(jnp.bfloat16)  3.51 us
    gather x1, local copies, waits for them, and re-layouts, local(): dudz = jnp.swapaxes(du_dz[:, edge], 0, 1)  3.06 us
    squeeze x1, other arithmetic, local(): span_v = velocity[:, 1].astype(jnp.float32)  2.65 us
    unnamed x10, local copies, waits for them, and re-layouts  2.42 us

profile of v16, /device:TPU:1, one launch (start us, length us, event | category | flops | bytes accessed | tf_op | source)
XLA Modules:
  0.0 102.1 jit_solution(12831326593483071763)
XLA Ops:
  0.6 0.7 pad_clamp_fusion.1
  1.3 0.7 pad_clamp_fusion
  2.0 1.7 %fusion.15 = (bf16[32,1,16,1024]{3,2,1,0:T(8,128)(2,1)S(1)}, bf16[32,1,16,1024]{3,2,1,0:T(8,128)(2,1)S(1)}) fusion(bf16[32,2,16,1024]{3,2,1,0:T(8,128)(2,1)} %param.4), kind=kLoop, calls=%fused_computation.25 | loop fusion | bytes 4194304 | tf_op jit(solution)/shard_map/slice | solution.py:414
  3.7 2.7 %copy_bitcast_fusion.1 = (bf16[32,16,1024]{2,0,1:T(8,128)(2,1)S(1)}, f32[32,16,1024]{2,0,1:T(8,128)}, f32[32,16,1024]{2,0,1:T(8,128)S(1)}) fusion(bf16[32,1,16,1024]{3,2,1,0:T(8,128)(2,1)S(1)} %get-tuple-element.19, bf16[32,1,16,1024]{3,2,1,0:T(8,128)(2,1)S(1)} %get-tuple-element.18), kind=kLoop, calls=%fused_computation.17 | loop fusion | flops 1048576 | bytes 7340032 | tf_op jit(solution)/shard_map/squeeze | solution.py:413
  6.3 1.4 %gather_fusion = bf16[8,32,1024]{2,1,0:T(8,128)(2,1)} fusion(bf16[32,16,1024]{2,0,1:T(8,128)(2,1)S(1)} %get-tuple-element.28, s32[1024]{0:T(1024)S(1)} %pad_clamp_fusion.1), kind=kCustom, calls=%fused_computation | custom fusion | bytes 1048608 | tf_op jit(solution)/shard_map/gather | solution.py:422
  7.7 0.0 copy-start
  7.7 1.1 %fusion.18 = (f32[32,1,1024]{2,0,1:T(8,128)S(1)}, f32[32,1,1024]{2,0,1:T(8,128)S(1)}) fusion(f32[32,16,1024]{2,0,1:T(8,128)} %get-tuple-element.29), kind=kLoop, calls=%fused_computation.28 | loop fusion | bytes 524288 | tf_op jit(solution)/shard_map/jit(_roll_static)/slice | solution.py:417
  8.9 1.1 %fusion.16 = (f32[32,2,1024]{2,0,1:T(8,128)S(1)}, f32[32,2,1024]{2,0,1:T(8,128)S(1)}) fusion(f32[32,16,1024]{2,0,1:T(8,128)} %get-tuple-element.29), kind=kLoop, calls=%fused_computation.26 | loop fusion | bytes 1048576 | tf_op jit(solution)/shard_map/jit(_roll_static)/slice | solution.py:418
  9.9 0.1 fusion.14
  10.1 0.1 fusion.12
  10.2 0.0 copy-done
  10.2 0.6 fusion.17
  10.9 0.7 fusion.19
  11.6 0.8 fusion.13
  12.3 0.8 fusion.11
  13.1 3.5 %fusion.4 = (bf16[32,16,1024]{2,0,1:T(8,128)(2,1)}, f32[32,16,1024]{2,0,1:T(8,128)}) fusion(f32[32,1,1024]{2,0,1:T(8,128)S(1)} %get-tuple-element.25, f32[32,15,1024]{2,0,1:T(8,128)S(1)} %get-tuple-element.27, f32[32,15,1024]{2,0,1:T(8,128)S(1)} %get-tuple-element.26, f32[32,1,1024]{2,0,1:T(8,128)S(1)} %get-tuple-element.24, ...), kind=kLoop, calls=%fused_computation.8 | loop fusion | flops 10485760 | bytes 19922944 | tf_op jit(solution)/shard_map/convert_element_type | solution.py:420
  16.6 0.0 copy-start.1
  16.6 0.0 copy-start.3
  16.6 3.1 %gather_fusion.1 = f32[4,32,1024]{2,1,0:T(8,128)} fusion(f32[32,16,1024]{2,0,1:T(8,128)} %get-tuple-element.9, s32[1024]{0:T(1024)S(1)} %pad_clamp_fusion), kind=kCustom, calls=%fused_computation.1 | custom fusion | bytes 1048592 | tf_op jit(solution)/shard_map/gather | solution.py:423
  19.7 78.4 %shard_map.59 = (f32[16,4,1024]{2,1,0:T(4,128)}, bf16[4,32,1024]{2,1,0:T(8,128)(2,1)}) custom-call(bf16[16,32,1024]{2,1,0:T(8,128)(2,1)} %bitcast.12, bf16[8,32,1024]{2,1,0:T(8,128)(2,1)} %gather_fusion, f32[4,32,1024]{2,1,0:T(8,128)} %gather_fusion.1), custom_call_target="tpu_custom_call" | custom-call | tf_op jit(solution)/shard_map/pallas_call | solution.py:252
  98.1 0.0 copy-start.2
  98.1 0.0 copy-done.1
  98.1 0.0 copy-done.3
  98.1 1.6 %scatter_fusion = bf16[32,16,1024]{2,0,1:T(8,128)(2,1)S(1)} fusion(bf16[32,16,1024]{2,0,1:T(8,128)(2,1)S(1)} %copy-done.1, s32[4]{0:T(128)S(1)} %copy-done.3, bf16[4,32,1024]{2,1,0:T(8,128)(2,1)} %get-tuple-element.4), kind=kCustom, calls=%fused_computation.2 | custom fusion | bytes 786448 | tf_op jit(solution)/shard_map/scatter | solution.py:425
  99.7 1.5 %copy.8 = bf16[32,16,1024]{2,1,0:T(8,128)(2,1)} copy(bf16[32,16,1024]{2,0,1:T(8,128)(2,1)S(1)} %scatter_fusion) | data formatting | bytes 2097152
  101.2 0.0 copy-done.2
  101.3 0.9 copy.9
Async XLA Ops:
  7.7 2.5 %copy-start = (f32[32,16,1024]{2,0,1:T(8,128)S(1)}, f32[32,16,1024]{2,0,1:T(8,128)}, u32[]{:S(2)}) copy-start(f32[32,16,1024]{2,0,1:T(8,128)} %get-tuple-element.29) | copy-start | bytes 6291460
  16.6 81.5 %copy-start.1 = (bf16[32,16,1024]{2,0,1:T(8,128)(2,1)S(1)}, bf16[32,16,1024]{2,0,1:T(8,128)(2,1)}, u32[]{:S(2)}) copy-start(bf16[32,16,1024]{2,0,1:T(8,128)(2,1)} %get-tuple-element.8) | copy-start | bytes 3145732
  16.6 81.5 %copy-start.3 = (s32[4]{0:T(128)S(1)}, s32[4]{0:T(128)}, u32[]{:S(2)}) copy-start(s32[4]{0:T(128)} %constant.27) | copy-start | bytes 52
  98.1 3.2 %copy-start.2 = (f32[16,4,1024]{2,1,0:T(4,128)S(1)}, f32[16,4,1024]{2,1,0:T(4,128)}, u32[]{:S(2)}) copy-start(f32[16,4,1024]{2,1,0:T(4,128)} %get-tuple-element.5) | copy-start | bytes 786436

commit v17 on v16

--- a/solution.py
+++ b/solution.py
@@ -418,11 +418,12 @@
         - (jnp.roll(span_v, -2, 1) - jnp.roll(span_v, 2, 1))
     ) / 12.0
     local_vort = (dv_dx - du_dz).astype(jnp.bfloat16)
-    edge = [0, 1, rows - 2, rows - 1]
-    vloc = jnp.swapaxes(velocity[:, 1][:, [0, 1, 2, 3, rows - 4, rows - 3, rows - 2, rows - 1]], 0, 1)
-    dudz = jnp.swapaxes(du_dz[:, edge], 0, 1)
+    v = velocity[:, 1]
+    vloc = jnp.swapaxes(jnp.concatenate([v[:, :4], v[:, rows - 4 :]], axis=1), 0, 1)
+    dudz = jnp.swapaxes(jnp.concatenate([du_dz[:, :2], du_dz[:, rows - 2 :]], axis=1), 0, 1)
     modes, fixed = front(jnp.swapaxes(local_vort, 0, 1), vloc, dudz)
-    vorticity = local_vort.at[:, edge].set(jnp.swapaxes(fixed, 0, 1))
+    fixed = jnp.swapaxes(fixed, 0, 1)
+    vorticity = jnp.concatenate([fixed[:, :2], local_vort[:, 2 : rows - 2], fixed[:, 2:]], axis=1)
     return (vorticity, jnp.swapaxes(modes, 0, 1))
 
 

time: 102 us -> 94.8 us (0.929)
  local copies, waits for them, and re-layouts: 15.5 us -> 8.97 us
  other arithmetic: 7.49 us -> 6.46 us
    gather x2 -> x0, local copies, waits for them, and re-layouts: 4.43 us -> none  [the longest x1 3.06 us: local(): dudz = jnp.swapaxes(du_dz[:, edge], 0, 1)]
    transpose x0 -> x2, other arithmetic: none -> 1.67 us  [the longest x1 0.84 us: local(): jnp.swapaxes(jnp.concatenate([v[:, :4], v[:, rows - 4:]], axis=1), 0, 1)]
    scatter x1 -> x0, local copies, waits for them, and re-layouts: 1.58 us -> none  [local(): vorticity = local_vort.at[:, edge].set(jnp.swapaxes(fixed, 0, 1))]
    squeeze x1, other arithmetic: 2.65 us -> 1.29 us  [local(): span_v = velocity[:, 1].astype(jnp.float32)]
    gather x2 -> x0, other arithmetic: 1.32 us -> none  [the longest x1 0.66 us: local(): velocity[:, 1][:, [0, 1, 2, 3, rows - 4, rows - 3, rows - 2, rows - 1]]]
    slice x2, local copies, waits for them, and re-layouts: 1.83 us -> 0.5 us  [local(): jnp.roll(span_v, 1, 1)]
    slice x2, local copies, waits for them, and re-layouts: 1.7 us -> 0.48 us  [local(): jnp.roll(span_v, 2, 1)]
    slice x0 -> x4, local copies, waits for them, and re-layouts: none -> 1.11 us  [the longest x1 0.98 us: local(): fixed[:, :2]]
where the time goes in v17:
time: 94.8 us; the launch traced here: 94.7 us
  Pallas kernels  78.5 us (83%)
  local copies, waits for them, and re-layouts  8.97 us (9%)
  other arithmetic  6.46 us (7%)
    pallas_call x1, Pallas kernels, front(): pl.pallas_call(functools.partial(front_kernel, n_space, n_tm), out_shape=...  78.5 us
    convert_element_type x1, other arithmetic, local(): local_vort = (dv_dx - du_dz).astype(jnp.bfloat16)  3.37 us
    unnamed x4, local copies, waits for them, and re-layouts  3.36 us

profile of v17, /device:TPU:1, one launch (start us, length us, event | category | flops | bytes accessed | tf_op | source)
XLA Modules:
  0.0 94.7 jit_solution(2571589061731610523)
XLA Ops:
  0.6 1.7 %fusion.16 = (bf16[32,1,16,1024]{3,2,1,0:T(8,128)(2,1)S(1)}, bf16[32,1,16,1024]{3,2,1,0:T(8,128)(2,1)S(1)}) fusion(bf16[32,2,16,1024]{3,2,1,0:T(8,128)(2,1)} %param.1), kind=kLoop, calls=%fused_computation.24 | loop fusion | bytes 4194304 | tf_op jit(solution)/shard_map/slice | solution.py:414
  2.4 1.3 %copy_bitcast_fusion.1 = (bf16[32,16,1024]{2,0,1:T(8,128)(2,1)S(1)}, f32[32,16,1024]{2,0,1:T(8,128)S(1)}, f32[32,16,1024]{2,0,1:T(8,128)S(1)}) fusion(bf16[32,1,16,1024]{3,2,1,0:T(8,128)(2,1)S(1)} %get-tuple-element.21, bf16[32,1,16,1024]{3,2,1,0:T(8,128)(2,1)S(1)} %get-tuple-element.20), kind=kLoop, calls=%fused_computation.15 | loop fusion | flops 1048576 | bytes 7340032 | tf_op jit(solution)/shard_map/squeeze | solution.py:413
  3.7 0.8 maximum_bitcast_fusion.vloc_ref
  4.6 0.1 fusion.15
  4.8 0.1 fusion.13
  4.9 0.4 fusion.18
  5.4 0.5 fusion.20
  5.9 0.7 fusion.14
  6.6 0.7 fusion.12
  7.4 3.4 %fusion.4 = (bf16[32,16,1024]{2,0,1:T(8,128)(2,1)}, f32[32,16,1024]{2,0,1:T(8,128)S(1)}) fusion(f32[32,1,1024]{2,0,1:T(8,128)S(1)} %get-tuple-element.27, f32[32,15,1024]{2,0,1:T(8,128)S(1)} %get-tuple-element.29, f32[32,15,1024]{2,0,1:T(8,128)S(1)} %get-tuple-element.28, f32[32,1,1024]{2,0,1:T(8,128)S(1)} %get-tuple-element.26, ...), kind=kLoop, calls=%fused_computation.5 | loop fusion | flops 10485760 | bytes 19922944 | tf_op jit(solution)/shard_map/convert_element_type | solution.py:420
  10.8 0.0 copy-start
  10.8 0.8 maximum_bitcast_fusion.1.dudz_ref
  11.6 78.5 %shard_map.30 = (f32[16,4,1024]{2,1,0:T(4,128)}, bf16[4,32,1024]{2,1,0:T(8,128)(2,1)}) custom-call(bf16[16,32,1024]{2,1,0:T(8,128)(2,1)} %bitcast.16, bf16[8,32,1024]{2,1,0:T(8,128)(2,1)} %maximum_bitcast_fusion.vloc_ref, f32[4,32,1024]{2,1,0:T(8,128)} %maximum_bitcast_fusion.1.dudz_ref), custom_call_target="tpu_custom_call" | custom-call | tf_op jit(solution)/shard_map/pallas_call | solution.py:252
  90.1 1.8 %copy.6 = f32[4,16,1024]{2,1,0:T(8,128)} copy(f32[4,16,1024]{2,0,1:T(4,128)} %bitcast.18) | data formatting | bytes 524288
  91.9 1.0 %fusion.22 = (bf16[32,2,1024]{2,0,1:T(8,128)(2,1)S(1)}, bf16[32,2,1024]{2,0,1:T(8,128)(2,1)S(1)}) fusion(bf16[32,4,1024]{2,0,1:T(8,128)(2,1)} %bitcast.17), kind=kLoop, calls=%fused_computation.30 | loop fusion | bytes 524288 | tf_op jit(solution)/shard_map/slice | solution.py:426
  92.9 0.0 copy-done
  92.9 0.1 slice.138
  93.0 0.1 pad_maximum_fusion
  93.1 1.5 %copy.5 = bf16[32,16,1024]{2,1,0:T(8,128)(2,1)} copy(bf16[32,16,1024]{2,0,1:T(8,128)(2,1)S(1)} %pad_maximum_fusion) | data formatting | bytes 2097152
  (4 shorter events, 0.1 us)
Async XLA Ops:
  10.8 82.1 %copy-start = (bf16[32,16,1024]{2,0,1:T(8,128)(2,1)S(1)}, bf16[32,16,1024]{2,0,1:T(8,128)(2,1)}, u32[]{:S(2)}) copy-start(bf16[32,16,1024]{2,0,1:T(8,128)(2,1)} %get-tuple-element.8) | copy-start | bytes 3145732

commit v18 on v17

--- a/solution.py
+++ b/solution.py
@@ -423,7 +423,8 @@
     dudz = jnp.swapaxes(jnp.concatenate([du_dz[:, :2], du_dz[:, rows - 2 :]], axis=1), 0, 1)
     modes, fixed = front(jnp.swapaxes(local_vort, 0, 1), vloc, dudz)
     fixed = jnp.swapaxes(fixed, 0, 1)
-    vorticity = jnp.concatenate([fixed[:, :2], local_vort[:, 2 : rows - 2], fixed[:, 2:]], axis=1)
+    vorticity = lax.dynamic_update_slice(local_vort, fixed[:, :2], (0, 0, 0))
+    vorticity = lax.dynamic_update_slice(vorticity, fixed[:, 2:], (0, rows - 2, 0))
     return (vorticity, jnp.swapaxes(modes, 0, 1))
 
 

time: 94.8 us -> 94.8 us (level)
    dynamic_update_slice x0 -> x2, local copies, waits for them, and re-layouts: none -> 1.87 us  [the longest x1 0.95 us: local(): vorticity = lax.dynamic_update_slice(local_vort, fixed[:, :2], (0, 0, 0))]
    slice x2 -> x0, local copies, waits for them, and re-layouts: 1.04 us -> none  [the longest x1 0.98 us: local(): fixed[:, :2]]
    unnamed x4 -> x6, local copies, waits for them, and re-layouts: 3.36 us -> 2.42 us
where the time goes in v18:
time: 94.8 us; the launch traced here: 94.6 us
  Pallas kernels  78.5 us (83%)
  local copies, waits for them, and re-layouts  9.26 us (10%)
  other arithmetic  6.16 us (6%)
    pallas_call x1, Pallas kernels, front(): pl.pallas_call(functools.partial(front_kernel, n_space, n_tm), out_shape=...  78.5 us
    convert_element_type x1, other arithmetic, local(): local_vort = (dv_dx - du_dz).astype(jnp.bfloat16)  3.19 us
    unnamed x6, local copies, waits for them, and re-layouts  2.42 us

profile of v18, /device:TPU:1, one launch (start us, length us, event | category | flops | bytes accessed | tf_op | source)
XLA Modules:
  0.0 94.6 jit_solution(2470933401672669313)
XLA Ops:
  0.6 1.7 %fusion.16 = (bf16[32,1,16,1024]{3,2,1,0:T(8,128)(2,1)S(1)}, bf16[32,1,16,1024]{3,2,1,0:T(8,128)(2,1)S(1)}) fusion(bf16[32,2,16,1024]{3,2,1,0:T(8,128)(2,1)} %param.1), kind=kLoop, calls=%fused_computation.25 | loop fusion | bytes 4194304 | tf_op jit(solution)/shard_map/slice | solution.py:414
  2.4 1.3 %copy_bitcast_fusion.1 = (bf16[32,16,1024]{2,0,1:T(8,128)(2,1)S(1)}, f32[32,16,1024]{2,0,1:T(8,128)S(1)}, f32[32,16,1024]{2,0,1:T(8,128)S(1)}) fusion(bf16[32,1,16,1024]{3,2,1,0:T(8,128)(2,1)S(1)} %get-tuple-element.21, bf16[32,1,16,1024]{3,2,1,0:T(8,128)(2,1)S(1)} %get-tuple-element.20), kind=kLoop, calls=%fused_computation.14 | loop fusion | flops 1048576 | bytes 7340032 | tf_op jit(solution)/shard_map/squeeze | solution.py:413
  3.7 0.8 maximum_bitcast_fusion.vloc_ref
  4.6 0.1 fusion.15
  4.8 0.1 fusion.13
  4.9 0.6 fusion.18
  5.5 0.7 fusion.20
  6.2 0.8 fusion.14
  7.0 0.8 fusion.12
  7.8 3.2 %fusion.4 = (bf16[32,16,1024]{2,0,1:T(8,128)(2,1)}, f32[32,16,1024]{2,0,1:T(8,128)S(1)}) fusion(f32[32,1,1024]{2,0,1:T(8,128)S(1)} %get-tuple-element.27, f32[32,15,1024]{2,0,1:T(8,128)S(1)} %get-tuple-element.29, f32[32,15,1024]{2,0,1:T(8,128)S(1)} %get-tuple-element.28, f32[32,1,1024]{2,0,1:T(8,128)S(1)} %get-tuple-element.26, ...), kind=kLoop, calls=%fused_computation.5 | loop fusion | flops 10485760 | bytes 19922944 | tf_op jit(solution)/shard_map/convert_element_type | solution.py:420
  11.0 0.0 copy-start
  11.0 0.8 maximum_bitcast_fusion.1.dudz_ref
  11.9 78.5 %shard_map.30 = (f32[16,4,1024]{2,1,0:T(4,128)}, bf16[4,32,1024]{2,1,0:T(8,128)(2,1)}) custom-call(bf16[16,32,1024]{2,1,0:T(8,128)(2,1)} %bitcast.16, bf16[8,32,1024]{2,1,0:T(8,128)(2,1)} %maximum_bitcast_fusion.vloc_ref, f32[4,32,1024]{2,1,0:T(8,128)} %maximum_bitcast_fusion.1.dudz_ref), custom_call_target="tpu_custom_call" | custom-call | tf_op jit(solution)/shard_map/pallas_call | solution.py:252
  90.3 0.0 copy-start.1
  90.3 0.0 copy-done
  90.3 1.0 %slice_dynamic-update-slice_fusion.1 = bf16[32,16,1024]{2,0,1:T(8,128)(2,1)S(1)} fusion(bf16[32,16,1024]{2,0,1:T(8,128)(2,1)S(1)} %copy-done, bf16[32,4,1024]{2,0,1:T(8,128)(2,1)} %bitcast.18), kind=kLoop, calls=%fused_computation.18 | loop fusion | bytes 262144 | tf_op jit(solution)/shard_map/dynamic_update_slice | solution.py:426
  91.3 0.9 slice_dynamic-update-slice_fusion
  92.2 1.5 %copy.5 = bf16[32,16,1024]{2,1,0:T(8,128)(2,1)} copy(bf16[32,16,1024]{2,0,1:T(8,128)(2,1)S(1)} %slice_dynamic-update-slice_fusion) | data formatting | bytes 2097152
  93.8 0.0 copy-done.1
  93.8 0.9 copy.6
  (4 shorter events, 0.1 us)
Async XLA Ops:
  11.0 79.4 %copy-start = (bf16[32,16,1024]{2,0,1:T(8,128)(2,1)S(1)}, bf16[32,16,1024]{2,0,1:T(8,128)(2,1)}, u32[]{:S(2)}) copy-start(bf16[32,16,1024]{2,0,1:T(8,128)(2,1)} %get-tuple-element.8) | copy-start | bytes 3145732
  90.3 3.4 %copy-start.1 = (f32[16,4,1024]{2,1,0:T(4,128)S(1)}, f32[16,4,1024]{2,1,0:T(4,128)}, u32[]{:S(2)}) copy-start(f32[16,4,1024]{2,1,0:T(4,128)} %get-tuple-element.5) | copy-start | bytes 786436

commit v19 on v17

--- a/solution.py
+++ b/solution.py
@@ -179,7 +179,8 @@
     s = lax.axis_index("space")
     t = lax.axis_index("tm")
     greet_all(n_space, n_tm)
-    rows, _, cols = x_ref.shape
+    inner, _, cols = x_ref.shape
+    rows = inner + 4
     width = cols // n_tm
     left = lax.rem(s + n_space - 1, n_space)
     right = lax.rem(s + 1, n_space)
@@ -197,14 +198,13 @@
         c.start()
     src = lambda ref, a, r0, nr: ref.at[pl.ds(r0, nr), :, lanes(a, width)]
     dst = lambda j, r0, nr: cells.at[pl.ds(r0, nr), pl.ds(j * RANK, RANK), :]
-    inner = rows - 4
     copies = []
     for k in range(1, n_tm):
         a = lax.rem(t + k, n_tm)
-        c = remote(src(x_ref, a, 2, inner), dst(t, 2, inner), send.at[k], recv.at[t], (s, a))
+        c = remote(src(x_ref, a, 0, inner), dst(t, 2, inner), send.at[k], recv.at[t], (s, a))
         c.start()
         copies.append(c)
-    mine = pltpu.make_async_copy(src(x_ref, t, 2, inner), dst(t, 2, inner), own.at[0])
+    mine = pltpu.make_async_copy(src(x_ref, t, 0, inner), dst(t, 2, inner), own.at[0])
     mine.start()
     mine.wait()
     remote(vloc_ref.at[pl.ds(6, 2)], halo.at[pl.ds(0, 2)], hsend.at[0], hrecv.at[0], (left, t)).wait_recv()
@@ -223,7 +223,7 @@
         mine.wait()
     for k in range(1, n_tm):
         j = lax.rem(t + k, n_tm)
-        remote(src(x_ref, j, 0, rows), dst(j, 0, rows), send.at[k], recv.at[j], (s, j)).wait_recv()
+        remote(dst(j, 0, rows), dst(j, 0, rows), send.at[k], recv.at[j], (s, j)).wait_recv()
     for c in copies + halo_out:
         c.wait_send()
     size = cells.shape[1]
@@ -242,7 +242,8 @@
 def front(vort_x, vloc, dudz):
     n_space = lax.axis_size("space")
     n_tm = lax.axis_size("tm")
-    rows, _, cols = vort_x.shape
+    inner, _, cols = vort_x.shape
+    rows = inner + 4
     size = n_tm * RANK
     width = cols // n_tm
     cells_shape = (rows, size, width)
@@ -414,16 +415,16 @@
     stream_u = velocity[:, 0].astype(jnp.float32)
     du_dz = spanwise(stream_u)
     dv_dx = (
-        8.0 * (jnp.roll(span_v, -1, 1) - jnp.roll(span_v, 1, 1))
-        - (jnp.roll(span_v, -2, 1) - jnp.roll(span_v, 2, 1))
+        8.0 * (span_v[:, 3 : rows - 1] - span_v[:, 1 : rows - 3])
+        - (span_v[:, 4:rows] - span_v[:, : rows - 4])
     ) / 12.0
-    local_vort = (dv_dx - du_dz).astype(jnp.bfloat16)
+    interior = (dv_dx - du_dz[:, 2 : rows - 2]).astype(jnp.bfloat16)
     v = velocity[:, 1]
     vloc = jnp.swapaxes(jnp.concatenate([v[:, :4], v[:, rows - 4 :]], axis=1), 0, 1)
     dudz = jnp.swapaxes(jnp.concatenate([du_dz[:, :2], du_dz[:, rows - 2 :]], axis=1), 0, 1)
-    modes, fixed = front(jnp.swapaxes(local_vort, 0, 1), vloc, dudz)
+    modes, fixed = front(jnp.swapaxes(interior, 0, 1), vloc, dudz)
     fixed = jnp.swapaxes(fixed, 0, 1)
-    vorticity = jnp.concatenate([fixed[:, :2], local_vort[:, 2 : rows - 2], fixed[:, 2:]], axis=1)
+    vorticity = jnp.concatenate([fixed[:, :2], interior, fixed[:, 2:]], axis=1)
     return (vorticity, jnp.swapaxes(modes, 0, 1))
 
 

time: 94.8 us -> 93.1 us (0.982)
  local copies, waits for them, and re-layouts: 8.97 us -> 7.94 us
    convert_element_type x1, other arithmetic: 3.37 us -> 1.31 us  [local(): interior = (dv_dx - du_dz[:, 2:rows - 2]).astype(jnp.bfloat16)]
    div x0 -> x1, other arithmetic: none -> 1.46 us  [spanwise(): return (8.0 * (ahead - behind) - (ahead_two - behind_two)) / 12.0]
    slice x11 -> x6, local copies, waits for them, and re-layouts: 5.53 us -> 4.5 us  [the longest x1 1.74 us: local(): span_v = velocity[:, 1].astype(jnp.float32)]
where the time goes in v19:
time: 93.1 us; the launch traced here: 92.9 us
  Pallas kernels  78.3 us (84%)
  local copies, waits for them, and re-layouts  7.94 us (9%)
  other arithmetic  5.86 us (6%)
    pallas_call x1, Pallas kernels, front(): pl.pallas_call(functools.partial(front_kernel, n_space, n_tm), out_shape=...  78.3 us
    unnamed x4, local copies, waits for them, and re-layouts  3.36 us

profile of v19, /device:TPU:1, one launch (start us, length us, event | category | flops | bytes accessed | tf_op | source)
XLA Modules:
  0.0 92.9 jit_solution(11190651021374142910)
XLA Ops:
  0.6 1.7 %fusion.10 = (bf16[32,1,16,1024]{3,2,1,0:T(8,128)(2,1)S(1)}, bf16[32,1,16,1024]{3,2,1,0:T(8,128)(2,1)S(1)}) fusion(bf16[32,2,16,1024]{3,2,1,0:T(8,128)(2,1)} %param.1), kind=kLoop, calls=%fused_computation.20 | loop fusion | bytes 4194304 | tf_op jit(solution)/shard_map/slice | solution.py:414
  2.4 1.3 %copy_bitcast_fusion.1 = (bf16[32,16,1024]{2,0,1:T(8,128)(2,1)S(1)}, f32[32,16,1024]{2,0,1:T(8,128)S(1)}, f32[32,16,1024]{2,0,1:T(8,128)S(1)}) fusion(bf16[32,1,16,1024]{3,2,1,0:T(8,128)(2,1)S(1)} %get-tuple-element.10, bf16[32,1,16,1024]{3,2,1,0:T(8,128)(2,1)S(1)} %get-tuple-element.11), kind=kLoop, calls=%fused_computation.15 | loop fusion | flops 1048576 | bytes 7340032 | tf_op jit(solution)/shard_map/squeeze | solution.py:414
  3.7 0.8 maximum_bitcast_fusion.vloc_ref
  4.5 0.1 fusion.13
  4.7 0.1 fusion.11
  4.8 0.7 fusion.14
  5.6 0.8 fusion.12
  6.4 1.5 %fusion.2 = f32[32,16,1024]{2,0,1:T(8,128)S(1)} fusion(f32[32,16,1]{2,0,1:T(8,128)S(1)} %get-tuple-element.17, f32[32,16,1023]{2,0,1:T(8,128)S(1)} %get-tuple-element.19, f32[32,16,1023]{2,0,1:T(8,128)S(1)} %get-tuple-element.18, f32[32,16,1]{2,0,1:T(8,128)S(1)} %get-tuple-element.16, f32[32,16,2]{2,0,1:T(8,128)S(1)} %get-tuple-element.13, ...), kind=kLoop, calls=%fused_computation.3 | loop fusion | flops 4718592 | bytes 10485760 | tf_op jit(solution)/shard_map/div | solution.py:29
  7.8 1.3 %fusion.3 = bf16[32,12,1024]{2,0,1:T(8,128)(2,1)} fusion(f32[32,16,1024]{2,0,1:T(8,128)S(1)} %fusion.2, f32[32,16,1024]{2,0,1:T(8,128)S(1)} %get-tuple-element.23), kind=kLoop, calls=%fused_computation.6 | loop fusion | flops 2752512 | bytes 8650752 | tf_op jit(solution)/shard_map/convert_element_type | solution.py:421
  9.2 0.0 copy-start
  9.2 0.8 maximum_bitcast_fusion.1.dudz_ref
  10.0 78.3 %shard_map.30 = (f32[16,4,1024]{2,1,0:T(4,128)}, bf16[4,32,1024]{2,1,0:T(8,128)(2,1)}) custom-call(bf16[12,32,1024]{2,1,0:T(8,128)(2,1)} %bitcast.16, bf16[8,32,1024]{2,1,0:T(8,128)(2,1)} %maximum_bitcast_fusion.vloc_ref, f32[4,32,1024]{2,1,0:T(8,128)} %maximum_bitcast_fusion.1.dudz_ref), custom_call_target="tpu_custom_call" | custom-call | tf_op jit(solution)/shard_map/pallas_call | solution.py:253
  88.4 1.8 %copy.6 = f32[4,16,1024]{2,1,0:T(8,128)} copy(f32[4,16,1024]{2,0,1:T(4,128)} %bitcast.18) | data formatting | bytes 524288
  90.2 1.0 %fusion.16 = (bf16[32,2,1024]{2,0,1:T(8,128)(2,1)S(1)}, bf16[32,2,1024]{2,0,1:T(8,128)(2,1)S(1)}) fusion(bf16[32,4,1024]{2,0,1:T(8,128)(2,1)} %bitcast.17), kind=kLoop, calls=%fused_computation.26 | loop fusion | bytes 524288 | tf_op jit(solution)/shard_map/slice | solution.py:427
  91.2 0.0 copy-done
  91.2 0.1 pad_maximum_fusion
  91.3 1.5 %copy.5 = bf16[32,16,1024]{2,1,0:T(8,128)(2,1)} copy(bf16[32,16,1024]{2,0,1:T(8,128)(2,1)S(1)} %pad_maximum_fusion) | data formatting | bytes 2097152
  (2 shorter events, 0.1 us)
Async XLA Ops:
  9.2 82.0 %copy-start = (bf16[32,12,1024]{2,0,1:T(8,128)(2,1)S(1)}, bf16[32,12,1024]{2,0,1:T(8,128)(2,1)}, u32[]{:S(2)}) copy-start(bf16[32,12,1024]{2,0,1:T(8,128)(2,1)} %fusion.3) | copy-start | bytes 2359300

commit v20 on v19

--- a/solution.py
+++ b/solution.py
@@ -412,8 +412,11 @@
 def local(velocity):
     rows = velocity.shape[2]
     span_v = velocity[:, 1].astype(jnp.float32)
-    stream_u = velocity[:, 0].astype(jnp.float32)
-    du_dz = spanwise(stream_u)
+    u = velocity[:, 0]
+    cols = u.shape[2]
+    wrapped = jnp.concatenate([u[:, :, cols - 2 :], u, u[:, :, :2]], axis=2)
+    f32 = lambda lo: wrapped[:, :, lo : lo + cols].astype(jnp.float32)
+    du_dz = (8.0 * (f32(3) - f32(1)) - (f32(4) - f32(0))) / 12.0
     dv_dx = (
         8.0 * (span_v[:, 3 : rows - 1] - span_v[:, 1 : rows - 3])
         - (span_v[:, 4:rows] - span_v[:, : rows - 4])

time: 93.1 us -> 91.8 us (0.986)
  local copies, waits for them, and re-layouts: 7.94 us -> 6.25 us
    slice x4 -> x1, local copies, waits for them, and re-layouts: 1.78 us -> 0.11 us  [local(): wrapped = jnp.concatenate([u[:, :, cols - 2:], u, u[:, :, :2]], axis=2)]
where the time goes in v20:
time: 91.8 us; the launch traced here: 91.6 us
  Pallas kernels  78.3 us (85%)
  other arithmetic  6.27 us (7%)
  local copies, waits for them, and re-layouts  6.25 us (7%)
    pallas_call x1, Pallas kernels, front(): pl.pallas_call(functools.partial(front_kernel, n_space, n_tm), out_shape=...  78.3 us
    unnamed x4, local copies, waits for them, and re-layouts  3.36 us
    div x1, other arithmetic, local(): du_dz = (8.0 * (f32(3) - f32(1)) - (f32(4) - f32(0))) / 12.0  1.88 us

profile of v20, /device:TPU:1, one launch (start us, length us, event | category | flops | bytes accessed | tf_op | source)
XLA Modules:
  0.0 91.6 jit_solution(6817794276640744445)
XLA Ops:
  0.6 1.7 %fusion.8 = (bf16[32,1,16,1024]{3,2,1,0:T(8,128)(2,1)S(1)}, bf16[32,1,16,1024]{3,2,1,0:T(8,128)(2,1)S(1)}) fusion(bf16[32,2,16,1024]{3,2,1,0:T(8,128)(2,1)} %param.1), kind=kLoop, calls=%fused_computation.23 | loop fusion | bytes 4194304 | tf_op jit(solution)/shard_map/slice | solution.py:414
  2.4 1.3 %copy_bitcast_fusion.1 = (bf16[32,16,1024]{2,0,1:T(8,128)(2,1)S(1)}, f32[32,16,1024]{2,0,1:T(8,128)S(1)}, bf16[32,16,1024]{2,0,1:T(8,128)(2,1)S(1)}) fusion(bf16[32,1,16,1024]{3,2,1,0:T(8,128)(2,1)S(1)} %get-tuple-element.10, bf16[32,1,16,1024]{3,2,1,0:T(8,128)(2,1)S(1)} %get-tuple-element.11), kind=kLoop, calls=%fused_computation.18 | loop fusion | flops 524288 | bytes 6291456 | tf_op jit(solution)/shard_map/squeeze | solution.py:414
  3.7 0.8 maximum_bitcast_fusion.vloc_ref
  4.5 0.1 fusion.10
  4.6 1.9 %subtract_multiply_fusion = f32[32,16,1024]{2,0,1:T(8,128)S(1)} fusion(bf16[32,16,2]{2,0,1:T(8,128)(2,1)S(1)} %get-tuple-element.17, bf16[32,16,1024]{2,0,1:T(8,128)(2,1)S(1)} %get-tuple-element.20, bf16[32,16,2]{2,0,1:T(8,128)(2,1)S(1)} %get-tuple-element.16), kind=kLoop, calls=%fused_computation | loop fusion | flops 11010048 | bytes 3149824 | tf_op jit(solution)/shard_map/div | solution.py:419
  6.5 1.3 %fusion = bf16[32,12,1024]{2,0,1:T(8,128)(2,1)} fusion(f32[32,16,1024]{2,0,1:T(8,128)S(1)} %subtract_multiply_fusion, f32[32,16,1024]{2,0,1:T(8,128)S(1)} %get-tuple-element.15), kind=kLoop, calls=%fused_computation.2 | loop fusion | flops 2752512 | bytes 8650752 | tf_op jit(solution)/shard_map/convert_element_type | solution.py:424
  7.9 0.0 copy-start
  7.9 0.8 maximum_bitcast_fusion.1.dudz_ref
  8.7 78.3 %shard_map.30 = (f32[16,4,1024]{2,1,0:T(4,128)}, bf16[4,32,1024]{2,1,0:T(8,128)(2,1)}) custom-call(bf16[12,32,1024]{2,1,0:T(8,128)(2,1)} %bitcast.13, bf16[8,32,1024]{2,1,0:T(8,128)(2,1)} %maximum_bitcast_fusion.vloc_ref, f32[4,32,1024]{2,1,0:T(8,128)} %maximum_bitcast_fusion.1.dudz_ref), custom_call_target="tpu_custom_call" | custom-call | tf_op jit(solution)/shard_map/pallas_call | solution.py:253
  87.1 1.8 %copy.6 = f32[4,16,1024]{2,1,0:T(8,128)} copy(f32[4,16,1024]{2,0,1:T(4,128)} %bitcast.15) | data formatting | bytes 524288
  88.9 1.0 %fusion.11 = (bf16[32,2,1024]{2,0,1:T(8,128)(2,1)S(1)}, bf16[32,2,1024]{2,0,1:T(8,128)(2,1)S(1)}) fusion(bf16[32,4,1024]{2,0,1:T(8,128)(2,1)} %bitcast.14), kind=kLoop, calls=%fused_computation.26 | loop fusion | bytes 524288 | tf_op jit(solution)/shard_map/slice | solution.py:430
  89.9 0.0 copy-done
  89.9 0.1 pad_maximum_fusion.2
  90.0 1.5 %copy.5 = bf16[32,16,1024]{2,1,0:T(8,128)(2,1)} copy(bf16[32,16,1024]{2,0,1:T(8,128)(2,1)S(1)} %pad_maximum_fusion.2) | data formatting | bytes 2097152
  (2 shorter events, 0.1 us)
Async XLA Ops:
  7.9 82.0 %copy-start = (bf16[32,12,1024]{2,0,1:T(8,128)(2,1)S(1)}, bf16[32,12,1024]{2,0,1:T(8,128)(2,1)}, u32[]{:S(2)}) copy-start(bf16[32,12,1024]{2,0,1:T(8,128)(2,1)} %fusion) | copy-start | bytes 2359300

commit v21 on v20

--- a/solution.py
+++ b/solution.py
@@ -320,7 +320,8 @@
     for j in range(RANK):
         a_row = a[:, j : j + 1, :]
         r_row = r[:, j : j + 1, :]
-        factor = jnp.where(below > j, a[:, :, j : j + 1] / a_row[:, :, j : j + 1], 0.0)
+        inv = 1.0 / a_row[:, :, j : j + 1]
+        factor = jnp.where(below > j, a[:, :, j : j + 1] * inv, 0.0)
         a = a - factor * a_row
         r = r - factor * r_row
     diag_u = jnp.sum(jnp.where(row == col, a, 0.0), axis=2, keepdims=True)

time: 91.8 us -> 91.8 us (level)
  no operation moved by 1% of the time
where the time goes in v21:
time: 91.8 us; the launch traced here: 91.6 us
  Pallas kernels  78.3 us (85%)
  other arithmetic  6.27 us (7%)
  local copies, waits for them, and re-layouts  6.25 us (7%)
    pallas_call x1, Pallas kernels, front(): pl.pallas_call(functools.partial(front_kernel, n_space, n_tm), out_shape=...  78.3 us
    unnamed x4, local copies, waits for them, and re-layouts  3.36 us
    div x1, other arithmetic, local(): du_dz = (8.0 * (f32(3) - f32(1)) - (f32(4) - f32(0))) / 12.0  1.88 us

profile of v21, /device:TPU:1, one launch (start us, length us, event | category | flops | bytes accessed | tf_op | source)
XLA Modules:
  0.0 91.6 jit_solution(15571650598810703500)
XLA Ops:
  0.6 1.7 %fusion.8 = (bf16[32,1,16,1024]{3,2,1,0:T(8,128)(2,1)S(1)}, bf16[32,1,16,1024]{3,2,1,0:T(8,128)(2,1)S(1)}) fusion(bf16[32,2,16,1024]{3,2,1,0:T(8,128)(2,1)} %param.1), kind=kLoop, calls=%fused_computation.23 | loop fusion | bytes 4194304 | tf_op jit(solution)/shard_map/slice | solution.py:415
  2.4 1.3 %copy_bitcast_fusion.1 = (bf16[32,16,1024]{2,0,1:T(8,128)(2,1)S(1)}, f32[32,16,1024]{2,0,1:T(8,128)S(1)}, bf16[32,16,1024]{2,0,1:T(8,128)(2,1)S(1)}) fusion(bf16[32,1,16,1024]{3,2,1,0:T(8,128)(2,1)S(1)} %get-tuple-element.10, bf16[32,1,16,1024]{3,2,1,0:T(8,128)(2,1)S(1)} %get-tuple-element.11), kind=kLoop, calls=%fused_computation.18 | loop fusion | flops 524288 | bytes 6291456 | tf_op jit(solution)/shard_map/squeeze | solution.py:415
  3.7 0.8 maximum_bitcast_fusion.vloc_ref
  4.5 0.1 fusion.10
  4.6 1.9 %subtract_multiply_fusion = f32[32,16,1024]{2,0,1:T(8,128)S(1)} fusion(bf16[32,16,2]{2,0,1:T(8,128)(2,1)S(1)} %get-tuple-element.17, bf16[32,16,1024]{2,0,1:T(8,128)(2,1)S(1)} %get-tuple-element.20, bf16[32,16,2]{2,0,1:T(8,128)(2,1)S(1)} %get-tuple-element.16), kind=kLoop, calls=%fused_computation | loop fusion | flops 11010048 | bytes 3149824 | tf_op jit(solution)/shard_map/div | solution.py:420
  6.5 1.3 %fusion = bf16[32,12,1024]{2,0,1:T(8,128)(2,1)} fusion(f32[32,16,1024]{2,0,1:T(8,128)S(1)} %subtract_multiply_fusion, f32[32,16,1024]{2,0,1:T(8,128)S(1)} %get-tuple-element.15), kind=kLoop, calls=%fused_computation.2 | loop fusion | flops 2752512 | bytes 8650752 | tf_op jit(solution)/shard_map/convert_element_type | solution.py:425
  7.9 0.0 copy-start
  7.9 0.8 maximum_bitcast_fusion.1.dudz_ref
  8.7 78.3 %shard_map.30 = (f32[16,4,1024]{2,1,0:T(4,128)}, bf16[4,32,1024]{2,1,0:T(8,128)(2,1)}) custom-call(bf16[12,32,1024]{2,1,0:T(8,128)(2,1)} %bitcast.13, bf16[8,32,1024]{2,1,0:T(8,128)(2,1)} %maximum_bitcast_fusion.vloc_ref, f32[4,32,1024]{2,1,0:T(8,128)} %maximum_bitcast_fusion.1.dudz_ref), custom_call_target="tpu_custom_call" | custom-call | tf_op jit(solution)/shard_map/pallas_call | solution.py:253
  87.1 1.8 %copy.6 = f32[4,16,1024]{2,1,0:T(8,128)} copy(f32[4,16,1024]{2,0,1:T(4,128)} %bitcast.15) | data formatting | bytes 524288
  88.9 1.0 %fusion.11 = (bf16[32,2,1024]{2,0,1:T(8,128)(2,1)S(1)}, bf16[32,2,1024]{2,0,1:T(8,128)(2,1)S(1)}) fusion(bf16[32,4,1024]{2,0,1:T(8,128)(2,1)} %bitcast.14), kind=kLoop, calls=%fused_computation.26 | loop fusion | bytes 524288 | tf_op jit(solution)/shard_map/slice | solution.py:431
  89.9 0.0 copy-done
  89.9 0.1 pad_maximum_fusion.2
  90.0 1.5 %copy.5 = bf16[32,16,1024]{2,1,0:T(8,128)(2,1)} copy(bf16[32,16,1024]{2,0,1:T(8,128)(2,1)S(1)} %pad_maximum_fusion.2) | data formatting | bytes 2097152
  (2 shorter events, 0.1 us)
Async XLA Ops:
  7.9 82.0 %copy-start = (bf16[32,12,1024]{2,0,1:T(8,128)(2,1)S(1)}, bf16[32,12,1024]{2,0,1:T(8,128)(2,1)}, u32[]{:S(2)}) copy-start(bf16[32,12,1024]{2,0,1:T(8,128)(2,1)} %fusion) | copy-start | bytes 2359300

commit v22 on v20

--- a/solution.py
+++ b/solution.py
@@ -248,7 +248,7 @@
     width = cols // n_tm
     cells_shape = (rows, size, width)
     chunks = (n_space, size // n_space, size)
-    out_shape = (rows, RANK // n_tm, cols)
+    out_shape = (RANK // n_tm, rows, cols)
     edge_shape = (4, RANK, cols)
     return pl.pallas_call(
         functools.partial(front_kernel, n_space, n_tm),
@@ -265,7 +265,7 @@
             pltpu.VMEM((n_tm,) + chunks[1:], jnp.float32),
             pltpu.VMEM(chunks, jnp.float32),
             pltpu.VMEM((size, size), jnp.float32),
-            pltpu.VMEM((rows, RANK, width), jnp.float32),
+            pltpu.VMEM((RANK, rows, width), jnp.float32),
             pltpu.VMEM(out_shape, jnp.float32),
             pltpu.VMEM(edge_shape, vort_x.dtype),
             pltpu.VMEM(edge_shape, vort_x.dtype),
@@ -381,10 +381,10 @@
     pieces = jnp.concatenate([hi, mid, lo], axis=0)
     for x in range(w_ref.shape[0]):
         terms = jnp.dot(pieces, w_ref[x], preferred_element_type=jnp.float32)
-        part_ref[x] = (terms[:RANK] + terms[RANK : 2 * RANK]) + terms[2 * RANK :]
-    share = part_ref.shape[1] // n_tm
+        part_ref[:, x, :] = (terms[:RANK] + terms[RANK : 2 * RANK]) + terms[2 * RANK :]
+    share = part_ref.shape[0] // n_tm
     width = w_ref.shape[2]
-    src_at = lambda a: part_ref.at[:, pl.ds(a * share, share), :]
+    src_at = lambda a: part_ref.at[pl.ds(a * share, share)]
     dst_at = lambda j: buf.at[:, :, lanes(j, width)]
     copies = []
     for k in range(1, n_tm):
@@ -428,7 +428,7 @@
     modes, fixed = front(jnp.swapaxes(interior, 0, 1), vloc, dudz)
     fixed = jnp.swapaxes(fixed, 0, 1)
     vorticity = jnp.concatenate([fixed[:, :2], interior, fixed[:, 2:]], axis=1)
-    return (vorticity, jnp.swapaxes(modes, 0, 1))
+    return (vorticity, modes)
 
 
 def solution(mesh):

time: 91.8 us -> 90.7 us (0.988)
  local copies, waits for them, and re-layouts: 6.25 us -> 5.15 us
    unnamed x4 -> x6, local copies, waits for them, and re-layouts: 3.36 us -> 2.26 us
where the time goes in v22:
time: 90.7 us; the launch traced here: 90.5 us
  Pallas kernels  78.4 us (86%)
  other arithmetic  6.3 us (7%)
  local copies, waits for them, and re-layouts  5.15 us (6%)
    pallas_call x1, Pallas kernels, front(): pl.pallas_call(functools.partial(front_kernel, n_space, n_tm), out_shape=...  78.4 us
    unnamed x6, local copies, waits for them, and re-layouts  2.26 us
    div x1, other arithmetic, local(): du_dz = (8.0 * (f32(3) - f32(1)) - (f32(4) - f32(0))) / 12.0  1.88 us

profile of v22, /device:TPU:1, one launch (start us, length us, event | category | flops | bytes accessed | tf_op | source)
XLA Modules:
  0.0 90.5 jit_solution(12714600177584462826)
XLA Ops:
  0.6 1.7 %fusion.8 = (bf16[32,1,16,1024]{3,2,1,0:T(8,128)(2,1)S(1)}, bf16[32,1,16,1024]{3,2,1,0:T(8,128)(2,1)S(1)}) fusion(bf16[32,2,16,1024]{3,2,1,0:T(8,128)(2,1)} %param.1), kind=kLoop, calls=%fused_computation.23 | loop fusion | bytes 4194304 | tf_op jit(solution)/shard_map/slice | solution.py:414
  2.4 1.3 %copy_bitcast_fusion.1 = (bf16[32,16,1024]{2,0,1:T(8,128)(2,1)S(1)}, f32[32,16,1024]{2,0,1:T(8,128)S(1)}, bf16[32,16,1024]{2,0,1:T(8,128)(2,1)S(1)}) fusion(bf16[32,1,16,1024]{3,2,1,0:T(8,128)(2,1)S(1)} %get-tuple-element.10, bf16[32,1,16,1024]{3,2,1,0:T(8,128)(2,1)S(1)} %get-tuple-element.11), kind=kLoop, calls=%fused_computation.18 | loop fusion | flops 524288 | bytes 6291456 | tf_op jit(solution)/shard_map/squeeze | solution.py:414
  3.7 0.9 maximum_bitcast_fusion.vloc_ref
  4.5 0.1 fusion.10
  4.6 1.9 %subtract_multiply_fusion = f32[32,16,1024]{2,0,1:T(8,128)S(1)} fusion(bf16[32,16,2]{2,0,1:T(8,128)(2,1)S(1)} %get-tuple-element.17, bf16[32,16,1024]{2,0,1:T(8,128)(2,1)S(1)} %get-tuple-element.20, bf16[32,16,2]{2,0,1:T(8,128)(2,1)S(1)} %get-tuple-element.16), kind=kLoop, calls=%fused_computation | loop fusion | flops 11010048 | bytes 3149824 | tf_op jit(solution)/shard_map/div | solution.py:419
  6.5 1.3 %fusion = bf16[32,12,1024]{2,0,1:T(8,128)(2,1)} fusion(f32[32,16,1024]{2,0,1:T(8,128)S(1)} %subtract_multiply_fusion, f32[32,16,1024]{2,0,1:T(8,128)S(1)} %get-tuple-element.15), kind=kLoop, calls=%fused_computation.2 | loop fusion | flops 2752512 | bytes 8650752 | tf_op jit(solution)/shard_map/convert_element_type | solution.py:424
  7.8 0.0 copy-start
  7.9 0.8 maximum_bitcast_fusion.1.dudz_ref
  8.7 78.4 %shard_map.30 = (f32[4,16,1024]{2,1,0:T(8,128)}, bf16[4,32,1024]{2,1,0:T(8,128)(2,1)}) custom-call(bf16[12,32,1024]{2,1,0:T(8,128)(2,1)} %bitcast.12, bf16[8,32,1024]{2,1,0:T(8,128)(2,1)} %maximum_bitcast_fusion.vloc_ref, f32[4,32,1024]{2,1,0:T(8,128)} %maximum_bitcast_fusion.1.dudz_ref), custom_call_target="tpu_custom_call" | custom-call | tf_op jit(solution)/shard_map/pallas_call | solution.py:253
  87.1 1.0 %fusion.11 = (bf16[32,2,1024]{2,0,1:T(8,128)(2,1)S(1)}, bf16[32,2,1024]{2,0,1:T(8,128)(2,1)S(1)}) fusion(bf16[32,4,1024]{2,0,1:T(8,128)(2,1)} %bitcast.13), kind=kLoop, calls=%fused_computation.26 | loop fusion | bytes 524288 | tf_op jit(solution)/shard_map/slice | solution.py:430
  88.1 0.0 copy-done
  88.1 0.0 copy-start.1
  88.1 0.1 pad_maximum_fusion.2
  88.2 1.5 %copy.5 = bf16[32,16,1024]{2,1,0:T(8,128)(2,1)} copy(bf16[32,16,1024]{2,0,1:T(8,128)(2,1)S(1)} %pad_maximum_fusion.2) | data formatting | bytes 2097152
  89.8 0.0 copy-done.1
  89.8 0.7 copy.13
  (2 shorter events, 0.1 us)
Async XLA Ops:
  7.8 80.2 %copy-start = (bf16[32,12,1024]{2,0,1:T(8,128)(2,1)S(1)}, bf16[32,12,1024]{2,0,1:T(8,128)(2,1)}, u32[]{:S(2)}) copy-start(bf16[32,12,1024]{2,0,1:T(8,128)(2,1)} %fusion) | copy-start | bytes 2359300
  88.1 1.7 %copy-start.1 = (f32[4,16,1024]{2,1,0:T(8,128)S(1)}, f32[4,16,1024]{2,1,0:T(8,128)}, u32[]{:S(2)}) copy-start(f32[4,16,1024]{2,1,0:T(8,128)} %get-tuple-element.24) | copy-start | bytes 786436

commit v23 on v22

--- a/solution.py
+++ b/solution.py
@@ -206,7 +206,6 @@
         copies.append(c)
     mine = pltpu.make_async_copy(src(x_ref, t, 0, inner), dst(t, 2, inner), own.at[0])
     mine.start()
-    mine.wait()
     remote(vloc_ref.at[pl.ds(6, 2)], halo.at[pl.ds(0, 2)], hsend.at[0], hrecv.at[0], (left, t)).wait_recv()
     remote(vloc_ref.at[pl.ds(0, 2)], halo.at[pl.ds(2, 2)], hsend.at[1], hrecv.at[1], (right, t)).wait_recv()
     fix_edges(vloc_ref, dudz_ref, halo, fix)
@@ -217,6 +216,7 @@
             c = remote(src(fix, a, r0, 2), dst(t, d0, 2), esend.at[k, e], recv.at[t], (s, a))
             c.start()
             copies.append(c)
+    mine.wait()
     for r0, d0 in ((0, 0), (2, rows - 2)):
         mine = pltpu.make_async_copy(src(fix, t, r0, 2), dst(t, d0, 2), own.at[0])
         mine.start()

time: 90.7 us -> 90.7 us (level)
  no operation moved by 1% of the time
where the time goes in v23:
time: 90.7 us; the launch traced here: 90.5 us
  Pallas kernels  78.4 us (86%)
  other arithmetic  6.3 us (7%)
  local copies, waits for them, and re-layouts  5.15 us (6%)
    pallas_call x1, Pallas kernels, front(): pl.pallas_call(functools.partial(front_kernel, n_space, n_tm), out_shape=...  78.4 us
    unnamed x6, local copies, waits for them, and re-layouts  2.26 us
    div x1, other arithmetic, local(): du_dz = (8.0 * (f32(3) - f32(1)) - (f32(4) - f32(0))) / 12.0  1.88 us

profile of v23, /device:TPU:1, one launch (start us, length us, event | category | flops | bytes accessed | tf_op | source)
XLA Modules:
  0.0 90.5 jit_solution(15104645286748665954)
XLA Ops:
  0.6 1.7 %fusion.8 = (bf16[32,1,16,1024]{3,2,1,0:T(8,128)(2,1)S(1)}, bf16[32,1,16,1024]{3,2,1,0:T(8,128)(2,1)S(1)}) fusion(bf16[32,2,16,1024]{3,2,1,0:T(8,128)(2,1)} %param.1), kind=kLoop, calls=%fused_computation.23 | loop fusion | bytes 4194304 | tf_op jit(solution)/shard_map/slice | solution.py:414
  2.4 1.3 %copy_bitcast_fusion.1 = (bf16[32,16,1024]{2,0,1:T(8,128)(2,1)S(1)}, f32[32,16,1024]{2,0,1:T(8,128)S(1)}, bf16[32,16,1024]{2,0,1:T(8,128)(2,1)S(1)}) fusion(bf16[32,1,16,1024]{3,2,1,0:T(8,128)(2,1)S(1)} %get-tuple-element.10, bf16[32,1,16,1024]{3,2,1,0:T(8,128)(2,1)S(1)} %get-tuple-element.11), kind=kLoop, calls=%fused_computation.18 | loop fusion | flops 524288 | bytes 6291456 | tf_op jit(solution)/shard_map/squeeze | solution.py:414
  3.7 0.9 maximum_bitcast_fusion.vloc_ref
  4.5 0.1 fusion.10
  4.6 1.9 %subtract_multiply_fusion = f32[32,16,1024]{2,0,1:T(8,128)S(1)} fusion(bf16[32,16,2]{2,0,1:T(8,128)(2,1)S(1)} %get-tuple-element.17, bf16[32,16,1024]{2,0,1:T(8,128)(2,1)S(1)} %get-tuple-element.20, bf16[32,16,2]{2,0,1:T(8,128)(2,1)S(1)} %get-tuple-element.16), kind=kLoop, calls=%fused_computation | loop fusion | flops 11010048 | bytes 3149824 | tf_op jit(solution)/shard_map/div | solution.py:419
  6.5 1.3 %fusion = bf16[32,12,1024]{2,0,1:T(8,128)(2,1)} fusion(f32[32,16,1024]{2,0,1:T(8,128)S(1)} %subtract_multiply_fusion, f32[32,16,1024]{2,0,1:T(8,128)S(1)} %get-tuple-element.15), kind=kLoop, calls=%fused_computation.2 | loop fusion | flops 2752512 | bytes 8650752 | tf_op jit(solution)/shard_map/convert_element_type | solution.py:424
  7.8 0.0 copy-start
  7.9 0.8 maximum_bitcast_fusion.1.dudz_ref
  8.7 78.4 %shard_map.30 = (f32[4,16,1024]{2,1,0:T(8,128)}, bf16[4,32,1024]{2,1,0:T(8,128)(2,1)}) custom-call(bf16[12,32,1024]{2,1,0:T(8,128)(2,1)} %bitcast.12, bf16[8,32,1024]{2,1,0:T(8,128)(2,1)} %maximum_bitcast_fusion.vloc_ref, f32[4,32,1024]{2,1,0:T(8,128)} %maximum_bitcast_fusion.1.dudz_ref), custom_call_target="tpu_custom_call" | custom-call | tf_op jit(solution)/shard_map/pallas_call | solution.py:253
  87.1 1.0 %fusion.11 = (bf16[32,2,1024]{2,0,1:T(8,128)(2,1)S(1)}, bf16[32,2,1024]{2,0,1:T(8,128)(2,1)S(1)}) fusion(bf16[32,4,1024]{2,0,1:T(8,128)(2,1)} %bitcast.13), kind=kLoop, calls=%fused_computation.26 | loop fusion | bytes 524288 | tf_op jit(solution)/shard_map/slice | solution.py:430
  88.1 0.0 copy-done
  88.1 0.0 copy-start.1
  88.1 0.1 pad_maximum_fusion.2
  88.2 1.5 %copy.5 = bf16[32,16,1024]{2,1,0:T(8,128)(2,1)} copy(bf16[32,16,1024]{2,0,1:T(8,128)(2,1)S(1)} %pad_maximum_fusion.2) | data formatting | bytes 2097152
  89.8 0.0 copy-done.1
  89.8 0.7 copy.13
  (2 shorter events, 0.1 us)
Async XLA Ops:
  7.8 80.2 %copy-start = (bf16[32,12,1024]{2,0,1:T(8,128)(2,1)S(1)}, bf16[32,12,1024]{2,0,1:T(8,128)(2,1)}, u32[]{:S(2)}) copy-start(bf16[32,12,1024]{2,0,1:T(8,128)(2,1)} %fusion) | copy-start | bytes 2359300
  88.1 1.7 %copy-start.1 = (f32[4,16,1024]{2,1,0:T(8,128)S(1)}, f32[4,16,1024]{2,1,0:T(8,128)}, u32[]{:S(2)}) copy-start(f32[4,16,1024]{2,1,0:T(8,128)} %get-tuple-element.24) | copy-start | bytes 786436

commit v24 on v23

--- a/solution.py
+++ b/solution.py
@@ -397,13 +397,13 @@
         copies.append(c)
     mine = pltpu.make_async_copy(src_at(t), dst_at(t), own.at[0])
     mine.start()
-    mine.wait()
     for k in range(1, n_tm):
         j = lax.rem(t + k, n_tm)
         pltpu.make_async_remote_copy(
             src_ref=src_at(j), dst_ref=dst_at(j), send_sem=send.at[k], recv_sem=recv.at[j],
             device_id=(s, j), device_id_type=MESH,
         ).wait_recv()
+    mine.wait()
     for c in copies:
         c.wait_send()
     out_ref[...] = buf[...]

time: 90.7 us -> 90.7 us (level)
  no operation moved by 1% of the time
where the time goes in v24:
time: 90.7 us; the launch traced here: 90.5 us
  Pallas kernels  78.4 us (86%)
  other arithmetic  6.3 us (7%)
  local copies, waits for them, and re-layouts  5.15 us (6%)
    pallas_call x1, Pallas kernels, front(): pl.pallas_call(functools.partial(front_kernel, n_space, n_tm), out_shape=...  78.4 us
    unnamed x6, local copies, waits for them, and re-layouts  2.26 us
    div x1, other arithmetic, local(): du_dz = (8.0 * (f32(3) - f32(1)) - (f32(4) - f32(0))) / 12.0  1.88 us

profile of v24, /device:TPU:1, one launch (start us, length us, event | category | flops | bytes accessed | tf_op | source)
XLA Modules:
  0.0 90.5 jit_solution(9286093211355667603)
XLA Ops:
  0.6 1.7 %fusion.8 = (bf16[32,1,16,1024]{3,2,1,0:T(8,128)(2,1)S(1)}, bf16[32,1,16,1024]{3,2,1,0:T(8,128)(2,1)S(1)}) fusion(bf16[32,2,16,1024]{3,2,1,0:T(8,128)(2,1)} %param.1), kind=kLoop, calls=%fused_computation.23 | loop fusion | bytes 4194304 | tf_op jit(solution)/shard_map/slice | solution.py:414
  2.4 1.3 %copy_bitcast_fusion.1 = (bf16[32,16,1024]{2,0,1:T(8,128)(2,1)S(1)}, f32[32,16,1024]{2,0,1:T(8,128)S(1)}, bf16[32,16,1024]{2,0,1:T(8,128)(2,1)S(1)}) fusion(bf16[32,1,16,1024]{3,2,1,0:T(8,128)(2,1)S(1)} %get-tuple-element.10, bf16[32,1,16,1024]{3,2,1,0:T(8,128)(2,1)S(1)} %get-tuple-element.11), kind=kLoop, calls=%fused_computation.18 | loop fusion | flops 524288 | bytes 6291456 | tf_op jit(solution)/shard_map/squeeze | solution.py:414
  3.7 0.9 maximum_bitcast_fusion.vloc_ref
  4.5 0.1 fusion.10
  4.6 1.9 %subtract_multiply_fusion = f32[32,16,1024]{2,0,1:T(8,128)S(1)} fusion(bf16[32,16,2]{2,0,1:T(8,128)(2,1)S(1)} %get-tuple-element.17, bf16[32,16,1024]{2,0,1:T(8,128)(2,1)S(1)} %get-tuple-element.20, bf16[32,16,2]{2,0,1:T(8,128)(2,1)S(1)} %get-tuple-element.16), kind=kLoop, calls=%fused_computation | loop fusion | flops 11010048 | bytes 3149824 | tf_op jit(solution)/shard_map/div | solution.py:419
  6.5 1.3 %fusion = bf16[32,12,1024]{2,0,1:T(8,128)(2,1)} fusion(f32[32,16,1024]{2,0,1:T(8,128)S(1)} %subtract_multiply_fusion, f32[32,16,1024]{2,0,1:T(8,128)S(1)} %get-tuple-element.15), kind=kLoop, calls=%fused_computation.2 | loop fusion | flops 2752512 | bytes 8650752 | tf_op jit(solution)/shard_map/convert_element_type | solution.py:424
  7.8 0.0 copy-start
  7.9 0.8 maximum_bitcast_fusion.1.dudz_ref
  8.7 78.4 %shard_map.30 = (f32[4,16,1024]{2,1,0:T(8,128)}, bf16[4,32,1024]{2,1,0:T(8,128)(2,1)}) custom-call(bf16[12,32,1024]{2,1,0:T(8,128)(2,1)} %bitcast.12, bf16[8,32,1024]{2,1,0:T(8,128)(2,1)} %maximum_bitcast_fusion.vloc_ref, f32[4,32,1024]{2,1,0:T(8,128)} %maximum_bitcast_fusion.1.dudz_ref), custom_call_target="tpu_custom_call" | custom-call | tf_op jit(solution)/shard_map/pallas_call | solution.py:253
  87.1 1.0 %fusion.11 = (bf16[32,2,1024]{2,0,1:T(8,128)(2,1)S(1)}, bf16[32,2,1024]{2,0,1:T(8,128)(2,1)S(1)}) fusion(bf16[32,4,1024]{2,0,1:T(8,128)(2,1)} %bitcast.13), kind=kLoop, calls=%fused_computation.26 | loop fusion | bytes 524288 | tf_op jit(solution)/shard_map/slice | solution.py:430
  88.1 0.0 copy-done
  88.1 0.0 copy-start.1
  88.1 0.1 pad_maximum_fusion.2
  88.2 1.5 %copy.5 = bf16[32,16,1024]{2,1,0:T(8,128)(2,1)} copy(bf16[32,16,1024]{2,0,1:T(8,128)(2,1)S(1)} %pad_maximum_fusion.2) | data formatting | bytes 2097152
  89.8 0.0 copy-done.1
  89.8 0.7 copy.13
  (2 shorter events, 0.1 us)
Async XLA Ops:
  7.8 80.2 %copy-start = (bf16[32,12,1024]{2,0,1:T(8,128)(2,1)S(1)}, bf16[32,12,1024]{2,0,1:T(8,128)(2,1)}, u32[]{:S(2)}) copy-start(bf16[32,12,1024]{2,0,1:T(8,128)(2,1)} %fusion) | copy-start | bytes 2359300
  88.1 1.7 %copy-start.1 = (f32[4,16,1024]{2,1,0:T(8,128)S(1)}, f32[4,16,1024]{2,1,0:T(8,128)}, u32[]{:S(2)}) copy-start(f32[4,16,1024]{2,1,0:T(8,128)} %get-tuple-element.24) | copy-start | bytes 786436
